TPU v7x, 32 devices: a whole 2x2x4 slice. The times are simulated.
32 devices in a mesh: gx: 4 (over y, core), gy: 8 (over z, x).
Axes of the slice: x: 2, y: 2, z: 4, core: 2. Of those that a mesh axis runs over, the one named last changes fastest.
Arguments:
- velocity: float32 [3, 32, 64, 128], P(None, 'gx', 'gy'), may hold values from -6 to 6
- viscosity: float32 [32, 64, 128], P('gx', 'gy'), may hold values from 0.02 to 0.16
- forcing: float32 [4, 3, 32, 64, 128], P(None, None, 'gx', 'gy'), may hold values from -6 to 6
- earlier: float32 [60, 3, 32, 64, 128], P(None, None, 'gx', 'gy'), may hold values from -12 to 12
Outputs:
- velocity_out: float32 [3, 32, 64, 128], P(None, 'gx', 'gy')
- basis: float32 [64, 3, 32, 64, 128], P(None, None, 'gx', 'gy')
- factor: float32 [64, 64], replicated
All inputs are finite; a program needn't handle non-finite values.
Results may differ from a plain program's by a relative error of at most 0.000068.
Values sent between devices are 32-bit elements; how exact they have to be, the bound alone decides.
No kernel may reach another device: no remote copies, remote signals or barrier semaphores. Data moves between devices by JAX's collectives and lax.ppermute only.
A program may use at most 64 MiB of HBM per device.

v0:
```python
import jax
import jax.numpy as jnp
from jax import lax
from jax.sharding import PartitionSpec as P


def padded_2(array, sides, width):
    for axis, dim in sides:
        count, length = (lax.axis_size(axis), array.shape[dim])
        up = [(i, (i + 1) % count) for i in range(count - 1)]
        down = [(j, i) for i, j in up]
        last = lax.slice_in_dim(array, length - width, length, axis=dim)
        initial = lax.slice_in_dim(array, 0, width, axis=dim)
        before = lax.ppermute(last, axis, up)
        after = lax.ppermute(initial, axis, down)
        array = jnp.concatenate([before, array, after], axis=dim)
    return array


def laplace(padded, visc_pad):
    size_x = padded.shape[1] - 2
    size_y = padded.shape[2] - 2
    size_z = padded.shape[3] - 2
    centre = padded[:, 1 : 1 + size_x, 1 : 1 + size_y, 1 : 1 + size_z]
    visc_mid = visc_pad[1 : 1 + size_x, 1 : 1 + size_y, 1 : 1 + size_z]
    result = jnp.zeros_like(centre)
    for offset in ((2, 1, 1), (0, 1, 1), (1, 2, 1), (1, 0, 1), (1, 1, 2), (1, 1, 0)):
        first, second, third = offset
        beside = padded[:, first : first + size_x, second : second + size_y, third : third + size_z]
        visc_beside = visc_pad[
            first : first + size_x, second : second + size_y, third : third + size_z
        ]
        result = result + 0.5 * (visc_mid + visc_beside) * (beside - centre)
    return result


def factorize(panel, total_rows):
    local_gram = (
        lax.dot_general(
            panel,
            panel,
            (((1,), (1,)), ((), ())),
            precision=lax.Precision.HIGHEST,
            preferred_element_type=jnp.float32,
        )
        / total_rows
    )
    lower_factor = jnp.linalg.cholesky(lax.psum(local_gram, ("gx", "gy")))
    basis = jax.scipy.linalg.solve_triangular(lower_factor, panel, lower=True)
    return (lower_factor, basis)


def fields_rim_each(velocity, viscosity, forcing):
    visc_halo = padded_2(viscosity, (("gx", 0), ("gy", 1)), 1)
    visc_pad = jnp.pad(visc_halo, ((0, 0), (0, 0), (1, 1)))
    field = velocity
    fields = []
    for index in range(forcing.shape[0]):
        field_halo = padded_2(field, (("gx", 1), ("gy", 2)), 1)
        padded = jnp.pad(field_halo, ((0, 0), (0, 0), (0, 0), (1, 1)))
        field = field + laplace(padded, visc_pad) + forcing[index]
        fields.append(field)
    return fields


def local(velocity, viscosity, forcing, earlier):
    cell_rows = velocity.shape[0] * velocity.shape[1] * velocity.shape[2] * velocity.shape[3]
    total_rows = cell_rows * lax.axis_size("gx") * lax.axis_size("gy")
    fields = fields_rim_each(velocity, viscosity, forcing)
    panel_old = earlier.reshape(earlier.shape[0], cell_rows)
    snapshots = [field.reshape(1, cell_rows) for field in fields]
    lower_factor, basis = factorize(jnp.concatenate([panel_old] + snapshots, 0), total_rows)
    return (fields[-1], basis.reshape((basis.shape[0],) + velocity.shape), lower_factor.T)


def solution(mesh):
    return jax.shard_map(
        local,
        mesh=mesh,
        in_specs=(
            P(None, "gx", "gy", None),
            P("gx", "gy", None),
            P(None, None, "gx", "gy", None),
            P(None, None, "gx", "gy", None),
        ),
        out_specs=(P(None, "gx", "gy", None), P(None, None, "gx", "gy", None), P()),
        check_vma=False,
    )
```

profile of v0, /device:TPU:0, one launch (start us, length us, event | category | flops | bytes accessed | tf_op | source)
XLA Modules:
  0.0 195.6 jit_solution(2520877468651563737)
XLA Ops:
  1.5 2.6 %collective-permute-start.2 = (f32[1,8,128]{2,1,0:T(8,128)S(1)}, f32[1,8,128]{2,1,0:T(8,128)S(1)}, u32[]{:S(2)}, u32[]{:S(2)}) collective-permute-start(f32[1,8,128]{2,1,0:T(8,128)S(1)} %get-tuple-element.39), channel_id=1, source_target_pairs={{0,8},{8,16},{16,24},{1,9},{9,17},{17,25},{2,10},{10,18},{18,26},{... | collective-permute-start | bytes 12296 | tf_op jit(solution)/shard_map/ppermute | solution.py:14
  5.4 3.9 %collective-permute-done = f32[1,8,128]{2,1,0:T(8,128)S(1)} collective-permute-done((f32[1,8,128]{2,1,0:T(8,128)S(1)}, f32[1,8,128]{2,1,0:T(8,128)S(1)}, u32[]{:S(2)}, u32[]{:S(2)}) %collective-permute-start) | collective-permute-done | bytes 4128 | tf_op jit(solution)/shard_map/ppermute | solution.py:15
  10.2 3.4 %collective-permute-start.6 = (f32[10,1,128]{2,1,0:T(1,128)S(1)}, f32[10,1,128]{2,1,0:T(1,128)S(1)}, u32[]{:S(2)}, u32[]{:S(2)}) collective-permute-start(f32[10,1,128]{2,1,0:T(1,128)S(1)} %get-tuple-element.29), channel_id=1, source_target_pairs={{0,1},{1,2},{2,3},{3,4},{4,5},{5,6},{6,7},{8,9},{9,10},{10,11},{11... | collective-permute-start | bytes 15368 | tf_op jit(solution)/shard_map/ppermute | solution.py:14
  16.9 4.6 %collective-permute-start.3 = (f32[3,1,8,128]{3,2,1,0:T(8,128)S(1)}, f32[3,1,8,128]{3,2,1,0:T(8,128)S(1)}, u32[]{:S(2)}, u32[]{:S(2)}) collective-permute-start(f32[3,1,8,128]{3,2,1,0:T(8,128)S(1)} %get-tuple-element.26), channel_id=1, source_target_pairs={{0,8},{8,16},{16,24},{1,9},{9,17},{17,25},{2,10},{10,18},{18,26},{... | collective-permute-start | bytes 36872 | tf_op jit(solution)/shard_map/ppermute | solution.py:14
  23.3 4.3 %collective-permute-start.7 = (f32[3,10,1,128]{3,2,1,0:T(1,128)S(1)}, f32[3,10,1,128]{3,2,1,0:T(1,128)S(1)}, u32[]{:S(2)}, u32[]{:S(2)}) collective-permute-start(f32[3,10,1,128]{3,2,1,0:T(1,128)S(1)} %get-tuple-element.17), channel_id=1, source_target_pairs={{0,1},{1,2},{2,3},{3,4},{4,5},{5,6},{6,7},{8,9},{9,10},{10,11},{11... | collective-permute-start | bytes 46088 | tf_op jit(solution)/shard_map/ppermute | solution.py:14
  29.8 3.9 %collective-permute-done.5 = f32[3,10,1,128]{3,2,1,0:T(1,128)S(1)} collective-permute-done((f32[3,10,1,128]{3,2,1,0:T(1,128)S(1)}, f32[3,10,1,128]{3,2,1,0:T(1,128)S(1)}, u32[]{:S(2)}, u32[]{:S(2)}) %collective-permute-start.5) | collective-permute-done | bytes 15392 | tf_op jit(solution)/shard_map/ppermute | solution.py:15
  39.0 4.7 %collective-permute-done.8 = f32[3,1,8,128]{3,2,1,0:T(8,128)S(1)} collective-permute-done((f32[3,1,8,128]{3,2,1,0:T(8,128)S(1)}, f32[3,1,8,128]{3,2,1,0:T(8,128)S(1)}, u32[]{:S(2)}, u32[]{:S(2)}) %collective-permute-start.8) | collective-permute-done | bytes 12320 | tf_op jit(solution)/shard_map/ppermute | solution.py:15
  43.7 4.8 %collective-permute-start.11 = (f32[3,10,1,128]{3,2,1,0:T(1,128)S(1)}, f32[3,10,1,128]{3,2,1,0:T(1,128)S(1)}, u32[]{:S(2)}, u32[]{:S(2)}) collective-permute-start(f32[3,10,1,128]{3,2,1,0:T(1,128)S(1)} %get-tuple-element.15), channel_id=1, source_target_pairs={{0,1},{1,2},{2,3},{3,4},{4,5},{5,6},{6,7},{8,9},{9,10},{10,11},{11... | collective-permute-start | bytes 46088 | tf_op jit(solution)/shard_map/ppermute | solution.py:14
  50.0 4.2 %collective-permute-done.10 = f32[3,10,1,128]{3,2,1,0:T(1,128)S(1)} collective-permute-done((f32[3,10,1,128]{3,2,1,0:T(1,128)S(1)}, f32[3,10,1,128]{3,2,1,0:T(1,128)S(1)}, u32[]{:S(2)}, u32[]{:S(2)}) %collective-permute-start.10) | collective-permute-done | bytes 15392 | tf_op jit(solution)/shard_map/ppermute | solution.py:15
  55.6 2.9 %collective-permute-start.13 = (f32[3,1,8,128]{3,2,1,0:T(8,128)S(1)}, f32[3,1,8,128]{3,2,1,0:T(8,128)S(1)}, u32[]{:S(2)}, u32[]{:S(2)}) collective-permute-start(f32[3,1,8,128]{3,2,1,0:T(8,128)S(1)} %get-tuple-element.21), channel_id=1, source_target_pairs={{0,8},{8,16},{16,24},{1,9},{9,17},{17,25},{2,10},{10,18},{18,26},{... | collective-permute-start | bytes 36872 | tf_op jit(solution)/shard_map/ppermute | solution.py:14
  59.8 2.7 %collective-permute-done.12 = f32[3,1,8,128]{3,2,1,0:T(8,128)S(1)} collective-permute-done((f32[3,1,8,128]{3,2,1,0:T(8,128)S(1)}, f32[3,1,8,128]{3,2,1,0:T(8,128)S(1)}, u32[]{:S(2)}, u32[]{:S(2)}) %collective-permute-start.12) | collective-permute-done | bytes 12320 | tf_op jit(solution)/shard_map/ppermute | solution.py:15
  62.5 2.9 %collective-permute-start.15 = (f32[3,10,1,128]{3,2,1,0:T(1,128)S(1)}, f32[3,10,1,128]{3,2,1,0:T(1,128)S(1)}, u32[]{:S(2)}, u32[]{:S(2)}) collective-permute-start(f32[3,10,1,128]{3,2,1,0:T(1,128)S(1)} %get-tuple-element.13), channel_id=1, source_target_pairs={{0,1},{1,2},{2,3},{3,4},{4,5},{5,6},{6,7},{8,9},{9,10},{10,11},{11... | collective-permute-start | bytes 46088 | tf_op jit(solution)/shard_map/ppermute | solution.py:14
  66.9 4.2 %collective-permute-done.14 = f32[3,10,1,128]{3,2,1,0:T(1,128)S(1)} collective-permute-done((f32[3,10,1,128]{3,2,1,0:T(1,128)S(1)}, f32[3,10,1,128]{3,2,1,0:T(1,128)S(1)}, u32[]{:S(2)}, u32[]{:S(2)}) %collective-permute-start.14) | collective-permute-done | bytes 15392 | tf_op jit(solution)/shard_map/ppermute | solution.py:15
  72.5 3.2 %collective-permute-start.17 = (f32[3,1,8,128]{3,2,1,0:T(8,128)S(1)}, f32[3,1,8,128]{3,2,1,0:T(8,128)S(1)}, u32[]{:S(2)}, u32[]{:S(2)}) collective-permute-start(f32[3,1,8,128]{3,2,1,0:T(8,128)S(1)} %get-tuple-element.19), channel_id=1, source_target_pairs={{0,8},{8,16},{16,24},{1,9},{9,17},{17,25},{2,10},{10,18},{18,26},{... | collective-permute-start | bytes 36872 | tf_op jit(solution)/shard_map/ppermute | solution.py:14
  79.5 4.8 %collective-permute-start.19 = (f32[3,10,1,128]{3,2,1,0:T(1,128)S(1)}, f32[3,10,1,128]{3,2,1,0:T(1,128)S(1)}, u32[]{:S(2)}, u32[]{:S(2)}) collective-permute-start(f32[3,10,1,128]{3,2,1,0:T(1,128)S(1)} %get-tuple-element.11), channel_id=1, source_target_pairs={{0,1},{1,2},{2,3},{3,4},{4,5},{5,6},{6,7},{8,9},{9,10},{10,11},{11... | collective-permute-start | bytes 46088 | tf_op jit(solution)/shard_map/ppermute | solution.py:14
  86.6 6.3 %copy.21 = f32[8,8,192,128]{3,1,2,0:T(8,128)} copy(f32[8,8,192,128]{3,2,1,0:T(8,128)S(1)} %bitcast.40) | data formatting | bytes 12582912
  94.3 17.8 %concatenate.123 = f32[64,24576]{1,0:T(8,128)} concatenate(f32[60,24576]{1,0:T(8,128)} %bitcast.38, f32[1,24576]{1,0:T(1,128)S(1)} %bitcast.42, f32[1,24576]{1,0:T(1,128)S(1)} %bitcast.43, f32[1,24576]{1,0:T(1,128)S(1)} %bitcast.44, f32[1,24576]{1,0:T(1,128)S(1)} %bitcast.45), dimensions={0} | concatenate | bytes 12582912 | tf_op jit(solution)/shard_map/concatenate | solution.py:72
  112.1 8.2 %convolution_multiply_fusion = f32[64,64]{0,1:T(8,128)S(1)} fusion(f32[64,24576]{1,0:T(8,128)} %concatenate.123), kind=kOutput, calls=%fused_computation.2 | convolution fusion | flops 1207963648 | bytes 6307840 | tf_op jit(solution)/shard_map/dot_general | solution.py:39
  120.2 42.6 %psum.7 = f32[64,64]{0,1:T(8,128)S(1)} all-reduce(f32[64,64]{0,1:T(8,128)S(1)} %convolution_multiply_fusion), channel_id=1, replica_groups=mesh['gx'=4,'gy'=8] {'gx','gy'}, use_global_device_ids=true, to_apply=%region_0.1 | all-reduce | flops 4096 | bytes 32768 | tf_op jit(solution)/shard_map/psum | solution.py:48
  163.0 5.8 %cholesky.16 = f32[64,64]{1,0:T(8,128)S(1)} custom-call(f32[64,64]{1,0:T(8,128)S(1)} %fusion.83), custom_call_target="Cholesky" | custom-call | tf_op jit(solution)/shard_map/jit(cholesky)/cholesky | solution.py:48
  170.8 4.9 %custom-call.7 = f32[1,64,64]{1,2,0:T(8,128)S(1)} custom-call(f32[1,64,64]{2,1,0:T(8,128)S(1)} %get-tuple-element.32), custom_call_target="InvertDiagBlocksLowerTriangular" | custom-call | tf_op jit(solution)/shard_map/jit(_solve_triangular)/triangular_solve | solution.py:49
  175.7 3.9 %copy.22 = f32[8,8,192,128]{3,2,1,0:T(8,128)S(1)} copy(f32[8,8,192,128]{3,1,2,0:T(8,128)} %bitcast.37) | data formatting | bytes 12582912
  179.7 9.3 %fusion = f32[64,3,8,8,128]{4,0,3,2,1:T(8,128)S(1)} fusion(f32[3,8,8,128,64]{3,2,1,0,4:T(8,128)S(1)} %bitcast.39, f32[1,64,64]{1,2,0:T(8,128)S(1)} %custom-call.7), kind=kOutput, calls=%fused_computation | convolution fusion | flops 1207959552 | bytes 12599296 | tf_op jit(solution)/shard_map/jit(_solve_triangular)/triangular_solve | solution.py:49
  189.0 6.6 %copy.16 = f32[64,3,8,8,128]{4,3,2,1,0:T(8,128)} copy(f32[64,3,8,8,128]{4,0,3,2,1:T(8,128)S(1)} %fusion) | data formatting | bytes 12582912
  (62 shorter events, 31.9 us)
Async XLA Ops:
  0.6 85.0 %copy-start = (f32[60,3,8,8,128]{4,3,2,1,0:T(8,128)S(1)}, f32[60,3,8,8,128]{4,3,2,1,0:T(8,128)}, u32[]{:S(2)}) copy-start(f32[60,3,8,8,128]{4,3,2,1,0:T(8,128)} %param.7) | copy-start | bytes 17694724
  1.5 3.9 %collective-permute-start.2 = (f32[1,8,128]{2,1,0:T(8,128)S(1)}, f32[1,8,128]{2,1,0:T(8,128)S(1)}, u32[]{:S(2)}, u32[]{:S(2)}) collective-permute-start(f32[1,8,128]{2,1,0:T(8,128)S(1)} %get-tuple-element.39), channel_id=1, source_target_pairs={{0,8},{8,16},{16,24},{1,9},{9,17},{17,25},{2,10},{10,18},{18,26},{... | collective-permute-start | bytes 12296 | tf_op jit(solution)/shard_map/ppermute | solution.py:14
  4.1 5.2 %collective-permute-start = (f32[1,8,128]{2,1,0:T(8,128)S(1)}, f32[1,8,128]{2,1,0:T(8,128)S(1)}, u32[]{:S(2)}, u32[]{:S(2)}) collective-permute-start(f32[1,8,128]{2,1,0:T(8,128)S(1)} %get-tuple-element.38), channel_id=1, source_target_pairs={{8,0},{16,8},{24,16},{9,1},{17,9},{25,17},{10,2},{18,10},{26,18},{... | collective-permute-start | bytes 12296 | tf_op jit(solution)/shard_map/ppermute | solution.py:15
  10.2 11.3 %collective-permute-start.6 = (f32[10,1,128]{2,1,0:T(1,128)S(1)}, f32[10,1,128]{2,1,0:T(1,128)S(1)}, u32[]{:S(2)}, u32[]{:S(2)}) collective-permute-start(f32[10,1,128]{2,1,0:T(1,128)S(1)} %get-tuple-element.29), channel_id=1, source_target_pairs={{0,1},{1,2},{2,3},{3,4},{4,5},{5,6},{6,7},{8,9},{9,10},{10,11},{11... | collective-permute-start | bytes 15368 | tf_op jit(solution)/shard_map/ppermute | solution.py:14
  13.6 8.0 %collective-permute-start.4 = (f32[10,1,128]{2,1,0:T(1,128)S(1)}, f32[10,1,128]{2,1,0:T(1,128)S(1)}, u32[]{:S(2)}, u32[]{:S(2)}) collective-permute-start(f32[10,1,128]{2,1,0:T(1,128)S(1)} %get-tuple-element.30), channel_id=1, source_target_pairs={{1,0},{2,1},{3,2},{4,3},{5,4},{6,5},{7,6},{9,8},{10,9},{11,10},{12... | collective-permute-start | bytes 15368 | tf_op jit(solution)/shard_map/ppermute | solution.py:15
  15.6 7.6 %collective-permute-start.1 = (f32[3,1,8,128]{3,2,1,0:T(8,128)S(1)}, f32[3,1,8,128]{3,2,1,0:T(8,128)S(1)}, u32[]{:S(2)}, u32[]{:S(2)}) collective-permute-start(f32[3,1,8,128]{3,2,1,0:T(8,128)S(1)} %get-tuple-element.25), channel_id=1, source_target_pairs={{8,0},{16,8},{24,16},{9,1},{17,9},{25,17},{10,2},{18,10},{26,18},{... | collective-permute-start | bytes 36872 | tf_op jit(solution)/shard_map/ppermute | solution.py:15
  16.9 5.4 %collective-permute-start.3 = (f32[3,1,8,128]{3,2,1,0:T(8,128)S(1)}, f32[3,1,8,128]{3,2,1,0:T(8,128)S(1)}, u32[]{:S(2)}, u32[]{:S(2)}) collective-permute-start(f32[3,1,8,128]{3,2,1,0:T(8,128)S(1)} %get-tuple-element.26), channel_id=1, source_target_pairs={{0,8},{8,16},{16,24},{1,9},{9,17},{17,25},{2,10},{10,18},{18,26},{... | collective-permute-start | bytes 36872 | tf_op jit(solution)/shard_map/ppermute | solution.py:14
  23.3 6.4 %collective-permute-start.7 = (f32[3,10,1,128]{3,2,1,0:T(1,128)S(1)}, f32[3,10,1,128]{3,2,1,0:T(1,128)S(1)}, u32[]{:S(2)}, u32[]{:S(2)}) collective-permute-start(f32[3,10,1,128]{3,2,1,0:T(1,128)S(1)} %get-tuple-element.17), channel_id=1, source_target_pairs={{0,1},{1,2},{2,3},{3,4},{4,5},{5,6},{6,7},{8,9},{9,10},{10,11},{11... | collective-permute-start | bytes 46088 | tf_op jit(solution)/shard_map/ppermute | solution.py:14
  27.6 6.1 %collective-permute-start.5 = (f32[3,10,1,128]{3,2,1,0:T(1,128)S(1)}, f32[3,10,1,128]{3,2,1,0:T(1,128)S(1)}, u32[]{:S(2)}, u32[]{:S(2)}) collective-permute-start(f32[3,10,1,128]{3,2,1,0:T(1,128)S(1)} %get-tuple-element.18), channel_id=1, source_target_pairs={{1,0},{2,1},{3,2},{4,3},{5,4},{6,5},{7,6},{9,8},{10,9},{11,10},{12... | collective-permute-start | bytes 46088 | tf_op jit(solution)/shard_map/ppermute | solution.py:15
  35.2 3.8 %collective-permute-start.9 = (f32[3,1,8,128]{3,2,1,0:T(8,128)S(1)}, f32[3,1,8,128]{3,2,1,0:T(8,128)S(1)}, u32[]{:S(2)}, u32[]{:S(2)}) collective-permute-start(f32[3,1,8,128]{3,2,1,0:T(8,128)S(1)} %get-tuple-element.23), channel_id=1, source_target_pairs={{0,8},{8,16},{16,24},{1,9},{9,17},{17,25},{2,10},{10,18},{18,26},{... | collective-permute-start | bytes 36872 | tf_op jit(solution)/shard_map/ppermute | solution.py:14
  37.7 6.0 %collective-permute-start.8 = (f32[3,1,8,128]{3,2,1,0:T(8,128)S(1)}, f32[3,1,8,128]{3,2,1,0:T(8,128)S(1)}, u32[]{:S(2)}, u32[]{:S(2)}) collective-permute-start(f32[3,1,8,128]{3,2,1,0:T(8,128)S(1)} %get-tuple-element.24), channel_id=1, source_target_pairs={{8,0},{16,8},{24,16},{9,1},{17,9},{25,17},{10,2},{18,10},{26,18},{... | collective-permute-start | bytes 36872 | tf_op jit(solution)/shard_map/ppermute | solution.py:15
  43.7 6.2 %collective-permute-start.11 = (f32[3,10,1,128]{3,2,1,0:T(1,128)S(1)}, f32[3,10,1,128]{3,2,1,0:T(1,128)S(1)}, u32[]{:S(2)}, u32[]{:S(2)}) collective-permute-start(f32[3,10,1,128]{3,2,1,0:T(1,128)S(1)} %get-tuple-element.15), channel_id=1, source_target_pairs={{0,1},{1,2},{2,3},{3,4},{4,5},{5,6},{6,7},{8,9},{9,10},{10,11},{11... | collective-permute-start | bytes 46088 | tf_op jit(solution)/shard_map/ppermute | solution.py:14
  48.6 5.6 %collective-permute-start.10 = (f32[3,10,1,128]{3,2,1,0:T(1,128)S(1)}, f32[3,10,1,128]{3,2,1,0:T(1,128)S(1)}, u32[]{:S(2)}, u32[]{:S(2)}) collective-permute-start(f32[3,10,1,128]{3,2,1,0:T(1,128)S(1)} %get-tuple-element.16), channel_id=1, source_target_pairs={{1,0},{2,1},{3,2},{4,3},{5,4},{6,5},{7,6},{9,8},{10,9},{11,10},{12... | collective-permute-start | bytes 46088 | tf_op jit(solution)/shard_map/ppermute | solution.py:15
  55.6 4.2 %collective-permute-start.13 = (f32[3,1,8,128]{3,2,1,0:T(8,128)S(1)}, f32[3,1,8,128]{3,2,1,0:T(8,128)S(1)}, u32[]{:S(2)}, u32[]{:S(2)}) collective-permute-start(f32[3,1,8,128]{3,2,1,0:T(8,128)S(1)} %get-tuple-element.21), channel_id=1, source_target_pairs={{0,8},{8,16},{16,24},{1,9},{9,17},{17,25},{2,10},{10,18},{18,26},{... | collective-permute-start | bytes 36872 | tf_op jit(solution)/shard_map/ppermute | solution.py:14
  58.5 4.0 %collective-permute-start.12 = (f32[3,1,8,128]{3,2,1,0:T(8,128)S(1)}, f32[3,1,8,128]{3,2,1,0:T(8,128)S(1)}, u32[]{:S(2)}, u32[]{:S(2)}) collective-permute-start(f32[3,1,8,128]{3,2,1,0:T(8,128)S(1)} %get-tuple-element.22), channel_id=1, source_target_pairs={{8,0},{16,8},{24,16},{9,1},{17,9},{25,17},{10,2},{18,10},{26,18},{... | collective-permute-start | bytes 36872 | tf_op jit(solution)/shard_map/ppermute | solution.py:15
  62.5 4.4 %collective-permute-start.15 = (f32[3,10,1,128]{3,2,1,0:T(1,128)S(1)}, f32[3,10,1,128]{3,2,1,0:T(1,128)S(1)}, u32[]{:S(2)}, u32[]{:S(2)}) collective-permute-start(f32[3,10,1,128]{3,2,1,0:T(1,128)S(1)} %get-tuple-element.13), channel_id=1, source_target_pairs={{0,1},{1,2},{2,3},{3,4},{4,5},{5,6},{6,7},{8,9},{9,10},{10,11},{11... | collective-permute-start | bytes 46088 | tf_op jit(solution)/shard_map/ppermute | solution.py:14
  65.5 5.6 %collective-permute-start.14 = (f32[3,10,1,128]{3,2,1,0:T(1,128)S(1)}, f32[3,10,1,128]{3,2,1,0:T(1,128)S(1)}, u32[]{:S(2)}, u32[]{:S(2)}) collective-permute-start(f32[3,10,1,128]{3,2,1,0:T(1,128)S(1)} %get-tuple-element.14), channel_id=1, source_target_pairs={{1,0},{2,1},{3,2},{4,3},{5,4},{6,5},{7,6},{9,8},{10,9},{11,10},{12... | collective-permute-start | bytes 46088 | tf_op jit(solution)/shard_map/ppermute | solution.py:15
  72.5 4.5 %collective-permute-start.17 = (f32[3,1,8,128]{3,2,1,0:T(8,128)S(1)}, f32[3,1,8,128]{3,2,1,0:T(8,128)S(1)}, u32[]{:S(2)}, u32[]{:S(2)}) collective-permute-start(f32[3,1,8,128]{3,2,1,0:T(8,128)S(1)} %get-tuple-element.19), channel_id=1, source_target_pairs={{0,8},{8,16},{16,24},{1,9},{9,17},{17,25},{2,10},{10,18},{18,26},{... | collective-permute-start | bytes 36872 | tf_op jit(solution)/shard_map/ppermute | solution.py:14
  75.7 3.8 %collective-permute-start.16 = (f32[3,1,8,128]{3,2,1,0:T(8,128)S(1)}, f32[3,1,8,128]{3,2,1,0:T(8,128)S(1)}, u32[]{:S(2)}, u32[]{:S(2)}) collective-permute-start(f32[3,1,8,128]{3,2,1,0:T(8,128)S(1)} %get-tuple-element.20), channel_id=1, source_target_pairs={{8,0},{16,8},{24,16},{9,1},{17,9},{25,17},{10,2},{18,10},{26,18},{... | collective-permute-start | bytes 36872 | tf_op jit(solution)/shard_map/ppermute | solution.py:15
  79.5 13.4 %collective-permute-start.19 = (f32[3,10,1,128]{3,2,1,0:T(1,128)S(1)}, f32[3,10,1,128]{3,2,1,0:T(1,128)S(1)}, u32[]{:S(2)}, u32[]{:S(2)}) collective-permute-start(f32[3,10,1,128]{3,2,1,0:T(1,128)S(1)} %get-tuple-element.11), channel_id=1, source_target_pairs={{0,1},{1,2},{2,3},{3,4},{4,5},{5,6},{6,7},{8,9},{9,10},{10,11},{11... | collective-permute-start | bytes 46088 | tf_op jit(solution)/shard_map/ppermute | solution.py:14
  84.3 8.6 %collective-permute-start.18 = (f32[3,10,1,128]{3,2,1,0:T(1,128)S(1)}, f32[3,10,1,128]{3,2,1,0:T(1,128)S(1)}, u32[]{:S(2)}, u32[]{:S(2)}) collective-permute-start(f32[3,10,1,128]{3,2,1,0:T(1,128)S(1)} %get-tuple-element.12), channel_id=1, source_target_pairs={{1,0},{2,1},{3,2},{4,3},{5,4},{6,5},{7,6},{9,8},{10,9},{11,10},{12... | collective-permute-start | bytes 46088 | tf_op jit(solution)/shard_map/ppermute | solution.py:15
  94.3 17.8 %copy-start.1 = (f32[3,8,8,128]{3,2,1,0:T(8,128)}, f32[3,8,8,128]{3,2,1,0:T(8,128)S(1)}, u32[]{:S(2)}) copy-start(f32[3,8,8,128]{3,2,1,0:T(8,128)S(1)} %fusion.7) | copy-start | bytes 294916
where the time goes:
time: 197 us; the launch traced here: 196 us
  starting transfers between devices  49 us (25%)
  blocking collectives  42.6 us (22%)
  local copies, waits for them, and re-layouts  38.9 us (20%)
  waiting for transfers between devices  27 us (14%)
  other arithmetic  19.6 us (10%)
  matrix products  17.5 us (9%)
    psum x1, blocking collectives, factorize(): lower_factor = jnp.linalg.cholesky(lax.psum(local_gram, ('gx', 'gy')))  42.6 us
    ppermute x10, starting transfers between devices, padded_2(): before = lax.ppermute(last, axis, up)  36.1 us
    ppermute x10, waiting for transfers between devices, padded_2(): after = lax.ppermute(initial, axis, down)  26.1 us
    unnamed x12, local copies, waits for them, and re-layouts  19.4 us
    concatenate x1, local copies, waits for them, and re-layouts, local(): jnp.concatenate([panel_old] + snapshots, 0)  17.8 us
    ppermute x10, starting transfers between devices, padded_2(): after = lax.ppermute(initial, axis, down)  12.9 us
    another operation x1, matrix products, factorize(): basis = jax.scipy.linalg.solve_triangular(lower_factor, panel, lower=True)  9.33 us
    dot_general x1, matrix products, factorize(): lax.dot_general(panel, panel, (((1,), (1,)), ((), ())), precision=lax.Pre...  8.18 us
  transfers between devices with their start and end apart: 20, of which 10 were waited for; matrix products, arithmetic and copies ran while one was open for 5% of the time, Pallas kernels for 0%

commit v1 on v0

v1 whole, which is shorter than its diff:
```python
import functools
import jax
import jax.numpy as jnp
from jax import lax
from jax.experimental import pallas as pl
from jax.experimental.pallas import tpu as pltpu
from jax.sharding import PartitionSpec as P

F32 = jnp.float32
BF16 = jnp.bfloat16
DEPTH = 4
VMEM = pl.BlockSpec(memory_space=pltpu.VMEM)
PARAMS = pltpu.CompilerParams(vmem_limit_bytes=48 << 20)


def struct(*shape):
    return jax.ShapeDtypeStruct(shape, F32)


def sub_index():
    return lax.broadcasted_iota(jnp.int32, (8, 128), 0)


def turn(tile, shift):
    return pltpu.roll(tile, shift, 0)


def y_items(v, nu, f, up):
    sub = sub_index()
    comps, size_x = v.shape[0], v.shape[1]
    cells = [(c, x) for c in range(comps) for x in range(size_x)]
    items = [v[c, x] for c, x in cells] + [nu[x] for x in range(size_x)]
    for c, x in cells:
        if up:
            items.append(jnp.where(sub == 4, turn(f[2, c, x], 5), f[0, c, x]))
        else:
            items.append(jnp.where(sub == 3, turn(f[2, c, x], 3), f[0, c, x]))
    for (c, x), (d, w) in zip(cells[0::2], cells[1::2]):
        if up:
            items.append(jnp.where(sub >= 6, f[1, c, x], turn(f[1, d, w], 6)))
        else:
            items.append(jnp.where(sub < 2, f[1, c, x], turn(f[1, d, w], 2)))
    return items


def pack_y_kernel(v, nu, f, send_a, send_b):
    sub = sub_index()
    even = lax.rem(lax.axis_index("gy"), 2) == 0
    upper, lower = (y_items(v, nu, f, True), y_items(v, nu, f, False))
    half = send_a.shape[0]
    for j in range(half):
        to_up = jnp.where(sub >= 4, upper[j], turn(upper[half + j], 4))
        to_down = jnp.where(sub < 4, lower[j], turn(lower[half + j], 4))
        send_a[j] = jnp.where(even, to_up, to_down)
        send_b[j] = jnp.where(even, to_down, to_up)


def unpack_y(recv_a, recv_b, even, j):
    sub = sub_index()
    half = recv_a.shape[0]
    k = j % half
    a, b = recv_a[k], recv_b[k]
    above, below = jnp.where(even, a, b), jnp.where(even, b, a)
    if j < half:
        return jnp.where(sub < 4, above, below)
    return turn(jnp.where(sub < 4, below, above), 4)


def x_items(comps):
    own = [("v", c, d) for c in range(comps) for d in range(1, 5)]
    own += [("nu", 0, d) for d in range(1, 5)]
    for t in range(3):
        own += [(t, c, d) for c in range(comps) for d in range(1, 4 - t)]
    rim = [("v", c, d) for c in range(comps) for d in range(1, 4)]
    rim += [("nu", 0, d) for d in range(1, 4)]
    for t in range(2):
        rim += [(t, c, d) for c in range(comps) for d in range(1, 3 - t)]
    return own, rim


def pack_x_kernel(v, nu, f, recv_a, recv_b, rv, rnu, rf, send_a, send_b):
    sub = sub_index()
    even_y = lax.rem(lax.axis_index("gy"), 2) == 0
    even_x = lax.rem(lax.axis_index("gx"), 2) == 0
    comps, size_x = v.shape[0], v.shape[1]
    cells = [(c, x) for c in range(comps) for x in range(size_x)]
    get = functools.partial(unpack_y, recv_a, recv_b, even_y)
    at = 0
    for c, x in cells:
        rv[c, x] = get(at)
        at += 1
    for x in range(size_x):
        rnu[x] = get(at)
        at += 1
    for c, x in cells:
        item = get(at)
        rf[0, c, x] = item
        rf[2, c, x] = jnp.where(sub < 4, turn(item, 5), turn(item, 3))
        at += 1
    for (c, x), (d, w) in zip(cells[0::2], cells[1::2]):
        item = get(at)
        rf[1, c, x] = item
        rf[1, d, w] = jnp.where(sub < 4, turn(item, 6), turn(item, 2))
        at += 1
    own, rim = x_items(comps)
    at = 0
    for group, (gv, gnu, gf) in ((own, (v, nu, f)), (rim, (rv, rnu, rf))):
        for name, c, d in group:
            high, low = size_x - d, d - 1
            for ref, x in (
                (send_a, jnp.where(even_x, high, low)),
                (send_b, jnp.where(even_x, low, high)),
            ):
                if name == "v":
                    ref[at] = gv[c, x]
                elif name == "nu":
                    ref[at] = gnu[x]
                else:
                    ref[at] = gf[name, c, x]
            at += 1


def beside_y(first, second, up):
    sub = sub_index()
    if up:
        return jnp.where(sub == 7, turn(second, 7), turn(first, 7))
    return jnp.where(sub == 0, turn(second, 1), turn(first, 1))


def steps_kernel(v, nu, f, rv, rnu, rf, recv_a, recv_b, kept, square, snaps, final, part, ext, enu, ef, coef):
    comps, size_x = v.shape[0], v.shape[1]
    steps = f.shape[0]
    wide = 2 * size_x
    ix, nx = lax.axis_index("gx"), lax.axis_size("gx")
    iy, ny = lax.axis_index("gy"), lax.axis_size("gy")
    even = lax.rem(ix, 2) == 0
    sub = sub_index()
    lane = lax.broadcasted_iota(jnp.int32, (8, 128), 1)
    one = lambda flag: jnp.where(flag, 1.0, 0.0).astype(F32)
    x_top, x_low = one(ix < nx - 1), one(ix > 0)
    y_top, y_low = one(iy < ny - 1), one(iy > 0)

    for x in range(size_x):
        enu[x, 0], enu[x, 1] = nu[x], rnu[x]
        for c in range(comps):
            ext[0, c, x, 0], ext[0, c, x, 1] = v[c, x], rv[c, x]
            for t in range(3):
                ef[t, c, x, 0], ef[t, c, x, 1] = f[t, c, x], rf[t, c, x]
    own, rim = x_items(comps)
    at = 0
    for tile, group in enumerate((own, rim)):
        for name, c, d in group:
            high, low = size_x - 1 + d, wide - d
            for ref, x in (
                (recv_a, jnp.where(even, high, low)),
                (recv_b, jnp.where(even, low, high)),
            ):
                if name == "v":
                    ext[0, c, x, tile] = ref[at]
                elif name == "nu":
                    enu[x, tile] = ref[at]
                else:
                    ef[name, c, x, tile] = ref[at]
            at += 1

    def reach(x):
        return 0 if x < size_x else min(x - size_x + 1, wide - x)

    def tiles(limit):
        for x in range(wide):
            for tile in range(2):
                if reach(x) + tile <= limit:
                    yield x, tile

    for x, tile in tiles(DEPTH - 1):
        here, other = enu[x, tile], enu[x, 1 - tile]
        east = 0.5 * (here + enu[(x + 1) % wide, tile])
        west = 0.5 * (here + enu[(x - 1) % wide, tile])
        north = 0.5 * (here + beside_y(here, other, True))
        south = 0.5 * (here + beside_y(here, other, False))
        ahead = jnp.where(lane == 127, 0.0, pltpu.roll(here, 127, 1))
        behind = jnp.where(lane == 0, 0.0, pltpu.roll(here, 1, 1))
        front = 0.5 * (here + ahead)
        back = 0.5 * (here + behind)
        coef[x, tile, 0] = 1.0 - (((east + west) + (north + south)) + (front + back))
        if x == size_x - 1:
            east = east * x_top
        if x == 0:
            west = west * x_low
        if tile == 0:
            north = jnp.where(sub == 7, north * y_top, north)
            south = jnp.where(sub == 0, south * y_low, south)
        coef[x, tile, 1], coef[x, tile, 2] = east, west
        coef[x, tile, 3], coef[x, tile, 4] = north, south
        coef[x, tile, 5] = jnp.where(lane == 127, 0.0, front)
        coef[x, tile, 6] = jnp.where(lane == 0, 0.0, back)

    for t in range(steps):
        src, dst = t % 2, (t + 1) % 2
        for x, tile in tiles(DEPTH - 1 - t):
            w = [coef[x, tile, i] for i in range(7)]
            for c in range(comps):
                here, other = ext[src, c, x, tile], ext[src, c, x, 1 - tile]
                new = w[0] * here
                new = new + w[1] * ext[src, c, (x + 1) % wide, tile]
                new = new + w[2] * ext[src, c, (x - 1) % wide, tile]
                new = new + w[3] * beside_y(here, other, True)
                new = new + w[4] * beside_y(here, other, False)
                new = new + w[5] * pltpu.roll(here, 127, 1)
                new = new + w[6] * pltpu.roll(here, 1, 1)
                push = ef[t, c, x, tile] if t < 3 else f[t, c, x]
                new = new + push
                if t < steps - 1:
                    ext[dst, c, x, tile] = new
                if tile == 0 and x < size_x:
                    snaps[t, c * size_x + x] = new
                    if t == steps - 1:
                        final[c, x] = new

    rows = kept.shape[0]
    slabs = kept.shape[1]
    n = rows + steps
    column = lax.broadcasted_iota(jnp.int32, (8, n), 1)
    total = square[...]
    old = 0.5 * total[:, :n] + total[:, n:]
    scale = 1.0 / (slabs * 8 * 128 * nx * ny)
    for k0 in range(0, n, 8):
        acc = [[None] * 8 for _ in range(steps)]
        for s in range(slabs):
            new = [snaps[t, s] for t in range(steps)]
            for k in range(8):
                row = kept[k0 + k, s] if k0 + k < rows else new[k0 + k - rows]
                for t in range(steps):
                    if k0 + k >= rows and k0 + k - rows > t:
                        continue
                    term = row * new[t]
                    acc[t][k] = term if acc[t][k] is None else acc[t][k] + term
        block = old[k0 : k0 + 8]
        for t in range(steps):
            full = jnp.stack([jnp.zeros((8, 128), F32) if a is None else a for a in acc[t]], 0)
            summed = jnp.sum(pltpu.einshape("kyz->ykz", full), axis=0)
            entry = jnp.sum(summed, axis=1, keepdims=True)
            if k0 + 8 > rows:
                row_at = lax.broadcasted_iota(jnp.int32, (8, 1), 0) + k0
                entry = jnp.where(row_at == rows + t, 0.5 * entry, entry)
            block = jnp.where(column == rows + t, entry, block)
        part[pl.ds(k0, 8), :] = block * scale


def split(p):
    high = p.astype(BF16)
    return high, (p - high.astype(F32)).astype(BF16)


def to_rows(tiles):
    parts = [pltpu.einshape("kyz->ykz", tiles[k : k + 8]) for k in range(0, tiles.shape[0], 8)]
    return [jnp.concatenate([p[y] for p in parts], 0) for y in range(8)]


def from_rows(rows):
    n = rows[0].shape[0]
    return jnp.concatenate(
        [
            pltpu.einshape("ykz->kyz", jnp.stack([r[k : k + 8] for r in rows], 0))
            for k in range(0, n, 8)
        ],
        0,
    )


def square_kernel(kept, out, *, n):
    rows, slabs = kept.shape[0], kept.shape[1]
    acc = None
    for s in range(slabs):
        tiles = jnp.concatenate([kept[:, s], jnp.zeros((n - rows, 8, 128), F32)], 0)
        lines = to_rows(tiles)
        for y in range(0, 8, 2):
            high, low = split(jnp.concatenate(lines[y : y + 2], 1))
            both = jnp.concatenate([high, low], 0)
            term = lax.dot_general(high, both, (((1,), (1,)), ((), ())), preferred_element_type=F32)
            acc = term if acc is None else acc + term
    out[...] = acc


def factor_of(gram):
    n = gram.shape[0]
    row_at = lax.broadcasted_iota(jnp.int32, (n, n), 0)
    col_at = lax.broadcasted_iota(jnp.int32, (n, n), 1)
    eye = jnp.where(row_at == col_at, 1.0, 0.0).astype(F32)
    w = jnp.concatenate([gram, eye], 1)
    at = lax.broadcasted_iota(jnp.int32, (n, 1), 0)
    for j in range(n - 1):
        row = w[j : j + 1, :]
        ratio = row * (1.0 / row[:, j : j + 1])
        w = w - jnp.where(at > j, w[:, j : j + 1], 0.0) * ratio
    pivot = jnp.sum(w[:, :n] * eye, axis=1, keepdims=True)
    return w * lax.rsqrt(pivot)


def basis_kernel(part, kept, snaps, basis, factor, left):
    n = part.shape[0]
    block = basis.shape[1]

    @pl.when(pl.program_id(0) == 0)
    def _():
        m = part[...]
        w = factor_of(m + m.T)
        row_at = lax.broadcasted_iota(jnp.int32, (n, n), 0)
        col_at = lax.broadcasted_iota(jnp.int32, (n, n), 1)
        factor[...] = jnp.where(row_at <= col_at, w[:, :n], 0.0)
        high, low = split(w[:, n:])
        top = jnp.concatenate([high, high], 1)
        left[...] = jnp.concatenate([top, jnp.concatenate([low, jnp.zeros_like(low)], 1)], 0)

    lhs = left[...]
    base = pl.program_id(0) * block
    for s in range(block):
        lines = to_rows(jnp.concatenate([kept[:, base + s], snaps[:, base + s]], 0))
        out = []
        for y in range(0, 8, 2):
            high, low = split(jnp.concatenate(lines[y : y + 2], 1))
            rhs = jnp.concatenate([high, low], 0)
            r = lax.dot_general(lhs, rhs, (((1,), (0,)), ((), ())), preferred_element_type=F32)
            r = r[:n] + r[n:]
            out += [r[:, :128], r[:, 128:]]
        basis[:, s] = from_rows(out)


def pair_exchange(first, second, axis):
    count = lax.axis_size(axis)
    near = [(i, i ^ 1) for i in range(count)]
    far = [(i, ((i + 1) ^ 1) - 1) for i in range(1, count - 1)]
    return lax.ppermute(first, axis, near), lax.ppermute(second, axis, far)


def sum_over(value, axes):
    sizes = [lax.axis_size(a) for a in axes]
    count = 1
    for size in sizes:
        count *= size
    bits = []
    bit = 1
    while bit < count:
        bits.append(bit)
        bit *= 2
    for bit in reversed(bits):
        value = value + lax.ppermute(value, axes, [(i, i ^ bit) for i in range(count)])
    return value


def local(velocity, viscosity, forcing, earlier):
    comps, size_x = velocity.shape[0], velocity.shape[1]
    steps, rows = forcing.shape[0], earlier.shape[0]
    n, slabs = rows + steps, comps * size_x
    kept = earlier.reshape(rows, slabs, 8, 128)
    half = (2 * slabs + size_x + slabs // 2) // 2
    call = functools.partial(pl.pallas_call, compiler_params=PARAMS)
    send_a, send_b = call(
        pack_y_kernel,
        out_shape=(struct(half, 8, 128),) * 2,
        in_specs=[VMEM] * 3,
        out_specs=(VMEM,) * 2,
        name="pack_y",
    )(velocity, viscosity, forcing)
    recv_a, recv_b = pair_exchange(send_a, send_b, "gy")
    square = call(
        functools.partial(square_kernel, n=n),
        out_shape=struct(n, 2 * n),
        in_specs=[VMEM],
        out_specs=VMEM,
        cost_estimate=pl.CostEstimate(flops=2 * n * 2 * n * slabs * 1024, transcendentals=0, bytes_accessed=rows * slabs * 4096 * 2),
        name="gram_kept",
    )(kept)
    own, rim = x_items(comps)
    wire = struct(len(own) + len(rim), 8, 128)
    rv, rnu, rf, send_a, send_b = call(
        pack_x_kernel,
        out_shape=(
            struct(*velocity.shape),
            struct(*viscosity.shape),
            struct(3, *velocity.shape),
            wire,
            wire,
        ),
        in_specs=[VMEM] * 5,
        out_specs=(VMEM,) * 5,
        name="pack_x",
    )(velocity, viscosity, forcing, recv_a, recv_b)
    recv_a, recv_b = pair_exchange(send_a, send_b, "gx")
    snaps, final, part = call(
        steps_kernel,
        out_shape=(struct(steps, slabs, 8, 128), struct(*velocity.shape), struct(n, n)),
        in_specs=[VMEM] * 10,
        out_specs=(VMEM,) * 3,
        scratch_shapes=[
            pltpu.VMEM((2, comps, 2 * size_x, 2, 8, 128), F32),
            pltpu.VMEM((2 * size_x, 2, 8, 128), F32),
            pltpu.VMEM((3, comps, 2 * size_x, 2, 8, 128), F32),
            pltpu.VMEM((2 * size_x, 2, 7, 8, 128), F32),
        ],
        name="steps",
    )(velocity, viscosity, forcing, rv, rnu, rf, recv_a, recv_b, kept, square)
    part = sum_over(part, ("gx", "gy"))
    block = 6
    basis, factor = call(
        basis_kernel,
        grid=(slabs // block,),
        out_shape=(struct(n, slabs, 8, 128), struct(n, n)),
        in_specs=[VMEM] * 3,
        out_specs=(
            pl.BlockSpec((n, block, 8, 128), lambda i: (0, i, 0, 0)),
            pl.BlockSpec((n, n), lambda i: (0, 0)),
        ),
        scratch_shapes=[pltpu.VMEM((2 * n, 2 * n), BF16)],
        name="factor_basis",
    )(part, kept, snaps)
    return final, basis.reshape((n,) + velocity.shape), factor


def solution(mesh):
    return jax.shard_map(
        local,
        mesh=mesh,
        in_specs=(
            P(None, "gx", "gy", None),
            P("gx", "gy", None),
            P(None, None, "gx", "gy", None),
            P(None, None, "gx", "gy", None),
        ),
        out_specs=(P(None, "gx", "gy", None), P(None, None, "gx", "gy", None), P()),
        check_vma=False,
    )
```

time: 197 us -> 59.2 us (0.30)
  blocking collectives: 42.6 us -> 0 us
  local copies, waits for them, and re-layouts: 38.9 us -> 5.32 us
  starting transfers between devices: 49 us -> 17.8 us
  Pallas kernels: 0 us -> 22.2 us
  other arithmetic: 19.6 us -> 0.03 us
  matrix products: 17.5 us -> 0 us
  waiting for transfers between devices: 27 us -> 12.7 us
    psum x1 -> x0, blocking collectives: 42.6 us -> none  [factorize(): lower_factor = jnp.linalg.cholesky(lax.psum(local_gram, ('gx', 'gy')))]
    ppermute x20 -> x9, starting transfers between devices: 49 us -> 17.8 us  [the longest x5 13.4 us: sum_over(): lax.ppermute(value, axes, [(i, i ^ bit) for i in range(count)])]
    pallas_call x0 -> x5, Pallas kernels: none -> 22.2 us  [the longest x1 13.3 us: local(): call(basis_kernel, grid=(slabs // block,), out_shape=(struct(n, slabs, 8,...]
    concatenate x3 -> x0, local copies, waits for them, and re-layouts: 17.8 us -> none  [the longest x1 17.8 us: local(): jnp.concatenate([panel_old] + snapshots, 0)]
    ppermute x20 -> x9, waiting for transfers between devices: 27 us -> 12.7 us  [the longest x5 9.73 us: sum_over(): lax.ppermute(value, axes, [(i, i ^ bit) for i in range(count)])]
    unnamed x12 -> x14, local copies, waits for them, and re-layouts: 19.4 us -> 5.32 us
    another operation x4 -> x0, other arithmetic: 11.4 us -> none  [the longest x3 6.52 us: factorize(): lower_factor = jnp.linalg.cholesky(lax.psum(local_gram, ('gx', 'gy')))]
    another operation x1 -> x0, matrix products: 9.33 us -> none  [factorize(): basis = jax.scipy.linalg.solve_triangular(lower_factor, panel, lower=True)]
  transfers between devices with their start and end apart: 20 -> 9, of which waited for: 10 -> 6; matrix products, arithmetic and copies ran while one was open for 5% -> 0% of each run, Pallas kernels for 0% -> 5%
where the time goes in v1:
time: 59.2 us; the launch traced here: 58.8 us
  Pallas kernels  22.2 us (38%)
  starting transfers between devices  17.8 us (30%)
  waiting for transfers between devices  12.7 us (21%)
  local copies, waits for them, and re-layouts  5.32 us (9%)
  between operations  0.73 us (1%)
    ppermute x5, starting transfers between devices, sum_over(): lax.ppermute(value, axes, [(i, i ^ bit) for i in range(count)])  13.4 us
    pallas_call x1, Pallas kernels, local(): call(basis_kernel, grid=(slabs // block,), out_shape=(struct(n, slabs, 8,...  13.3 us
    ppermute x5, waiting for transfers between devices, sum_over(): lax.ppermute(value, axes, [(i, i ^ bit) for i in range(count)])  9.73 us
    pallas_call x1, Pallas kernels, local(): call(steps_kernel, out_shape=(struct(steps, slabs, 8, 128), struct(*veloc...  5.75 us
    unnamed x14, local copies, waits for them, and re-layouts  5.32 us
    ppermute x4, starting transfers between devices, pair_exchange(): return (lax.ppermute(first, axis, near), lax.ppermute(second, axis, far))  4.41 us
    ppermute x4, waiting for transfers between devices, pair_exchange(): return (lax.ppermute(first, axis, near), lax.ppermute(second, axis, far))  3.01 us
    pallas_call x1, Pallas kernels, local(): call(functools.partial(square_kernel, n=n), out_shape=struct(n, 2 * n), i...  2.98 us
  transfers between devices with their start and end apart: 9, of which 6 were waited for; matrix products, arithmetic and copies ran while one was open for 0% of the time, Pallas kernels for 5%

profile of v1, /device:TPU:0, one launch (start us, length us, event | category | flops | bytes accessed | tf_op | source)
XLA Modules:
  0.0 58.8 jit_solution(15451280837481536963)
XLA Ops:
  0.6 1.0 %copy-done.1 = f32[4,3,8,8,128]{4,3,2,1,0:T(8,128)S(1)} copy-done((f32[4,3,8,8,128]{4,3,2,1,0:T(8,128)S(1)}, f32[4,3,8,8,128]{4,3,2,1,0:T(8,128)}, u32[]{:S(2)}) %copy-start.1) | copy-done | bytes 393240
  1.6 0.9 %copy-done.3 = f32[3,8,8,128]{3,2,1,0:T(8,128)S(1)} copy-done((f32[3,8,8,128]{3,2,1,0:T(8,128)S(1)}, f32[3,8,8,128]{3,2,1,0:T(8,128)}, u32[]{:S(2)}) %copy-start.3) | copy-done | bytes 98328
  2.5 0.8 %copy-done.5 = f32[8,8,128]{2,1,0:T(8,128)S(1)} copy-done((f32[8,8,128]{2,1,0:T(8,128)S(1)}, f32[8,8,128]{2,1,0:T(8,128)}, u32[]{:S(2)}) %copy-start.5) | copy-done | bytes 32792
  3.3 0.1 pack_y.1
  3.3 3.0 %collective-permute-start = (f32[34,8,128]{2,1,0:T(8,128)S(1)}, f32[34,8,128]{2,1,0:T(8,128)S(1)}, u32[]{:S(2)}, u32[]{:S(2)}) collective-permute-start(f32[34,8,128]{2,1,0:T(8,128)S(1)} %get-tuple-element.15), channel_id=1, source_target_pairs={{0,1},{1,0},{2,3},{3,2},{4,5},{5,4},{6,7},{7,6},{8,9},{9,8},{10,11... | collective-permute-start | bytes 417800 | tf_op jit(solution)/shard_map/ppermute | solution.py:333
  6.3 0.7 %collective-permute-start.1 = (f32[34,8,128]{2,1,0:T(8,128)S(1)}, f32[34,8,128]{2,1,0:T(8,128)S(1)}, u32[]{:S(2)}, u32[]{:S(2)}) collective-permute-start(f32[34,8,128]{2,1,0:T(8,128)S(1)} %get-tuple-element.16), channel_id=1, source_target_pairs={{1,2},{2,1},{3,4},{4,3},{5,6},{6,5},{9,10},{10,9},{11,12},{12,11},... | collective-permute-start | bytes 417800 | tf_op jit(solution)/shard_map/ppermute | solution.py:333
  7.0 3.0 %collective-permute-done.recv_a = f32[34,8,128]{2,1,0:T(8,128)S(1)} collective-permute-done((f32[34,8,128]{2,1,0:T(8,128)S(1)}, f32[34,8,128]{2,1,0:T(8,128)S(1)}, u32[]{:S(2)}, u32[]{:S(2)}) %collective-permute-start) | collective-permute-done | bytes 139296 | tf_op jit(solution)/shard_map/ppermute | solution.py:333
  10.0 0.1 pack_x.1
  10.1 0.1 collective-permute-start.2
  10.2 0.7 %collective-permute-start.3 = (f32[55,8,128]{2,1,0:T(8,128)S(1)}, f32[55,8,128]{2,1,0:T(8,128)S(1)}, u32[]{:S(2)}, u32[]{:S(2)}) collective-permute-start(f32[55,8,128]{2,1,0:T(8,128)S(1)} %get-tuple-element.21), channel_id=1, source_target_pairs={{8,16},{16,8},{9,17},{17,9},{10,18},{18,10},{11,19},{19,11},{12,20... | collective-permute-start | bytes 675848 | tf_op jit(solution)/shard_map/ppermute | solution.py:333
  10.9 2.7 %copy-done = f32[60,3,8,8,128]{4,3,2,1,0:T(8,128)S(1)} copy-done((f32[60,3,8,8,128]{4,3,2,1,0:T(8,128)S(1)}, f32[60,3,8,8,128]{4,3,2,1,0:T(8,128)}, u32[]{:S(2)}) %copy-start) | copy-done | bytes 5898264
  13.6 3.0 %gram_kept.1.square = f32[64,128]{1,0:T(8,128)S(1)} custom-call(f32[60,24,8,128]{3,2,1,0:T(8,128)S(1)} %bitcast.4), custom_call_target="tpu_custom_call" | custom-call | flops 402653184 | bytes 11796480 | tf_op jit(solution)/shard_map/gram_kept/pallas_call | solution.py:366
  16.6 5.7 %steps.1 = (f32[4,24,8,128]{3,2,1,0:T(8,128)S(1)}, f32[3,8,8,128]{3,2,1,0:T(8,128)}, f32[64,64]{1,0:T(8,128)S(1)}) custom-call(f32[3,8,8,128]{3,2,1,0:T(8,128)S(1)} %copy-done.4, f32[8,8,128]{2,1,0:T(8,128)S(1)} %copy-done.6, f32[4,3,8,8,128]{4,3,2,1,0:T(8,128)S(1)} %copy-done.2, f32[3,8,8,128]{3,2,1,0:T(8,128)S(1)} %get-tuple-element.17.rv, ...), custom_call_target="tpu_custom_call" | custom-call | tf_op jit(solution)/shard_map/steps/pallas_call | solution.py:390
  22.3 3.4 %collective-permute-start.4 = (f32[64,64]{1,0:T(8,128)S(1)}, f32[64,64]{1,0:T(8,128)S(1)}, u32[]{:S(2)}, u32[]{:S(2)}) collective-permute-start(f32[64,64]{1,0:T(8,128)S(1)} %get-tuple-element.23), channel_id=1, source_target_pairs={{0,16},{1,17},{2,18},{3,19},{4,20},{5,21},{6,22},{7,23},{8,24},{9,... | collective-permute-start | bytes 49160 | tf_op jit(solution)/shard_map/ppermute | solution.py:347
  25.7 1.9 %collective-permute-done.4 = f32[64,64]{1,0:T(8,128)S(1)} collective-permute-done((f32[64,64]{1,0:T(8,128)S(1)}, f32[64,64]{1,0:T(8,128)S(1)}, u32[]{:S(2)}, u32[]{:S(2)}) %collective-permute-start.4) | collective-permute-done | bytes 16416 | tf_op jit(solution)/shard_map/ppermute | solution.py:347
  27.6 0.6 %collective-permute-start.5 = (f32[64,64]{1,0:T(8,128)S(1)}, f32[64,64]{1,0:T(8,128)S(1)}, u32[]{:S(2)}, u32[]{:S(2)}) collective-permute-start(f32[64,64]{1,0:T(8,128)S(1)} %add.15), channel_id=1, source_target_pairs={{0,8},{1,9},{2,10},{3,11},{4,12},{5,13},{6,14},{7,15},{8,0},{9,1},... | collective-permute-start | bytes 49160 | tf_op jit(solution)/shard_map/ppermute | solution.py:347
  28.3 0.9 %collective-permute-done.5 = f32[64,64]{1,0:T(8,128)S(1)} collective-permute-done((f32[64,64]{1,0:T(8,128)S(1)}, f32[64,64]{1,0:T(8,128)S(1)}, u32[]{:S(2)}, u32[]{:S(2)}) %collective-permute-start.5) | collective-permute-done | bytes 16416 | tf_op jit(solution)/shard_map/ppermute | solution.py:347
  29.1 6.6 %collective-permute-start.6 = (f32[64,64]{1,0:T(8,128)S(1)}, f32[64,64]{1,0:T(8,128)S(1)}, u32[]{:S(2)}, u32[]{:S(2)}) collective-permute-start(f32[64,64]{1,0:T(8,128)S(1)} %add.16), channel_id=1, source_target_pairs={{0,4},{1,5},{2,6},{3,7},{4,0},{5,1},{6,2},{7,3},{8,12},{9,13},{10,... | collective-permute-start | bytes 49160 | tf_op jit(solution)/shard_map/ppermute | solution.py:347
  35.7 1.9 %collective-permute-done.6 = f32[64,64]{1,0:T(8,128)S(1)} collective-permute-done((f32[64,64]{1,0:T(8,128)S(1)}, f32[64,64]{1,0:T(8,128)S(1)}, u32[]{:S(2)}, u32[]{:S(2)}) %collective-permute-start.6) | collective-permute-done | bytes 16416 | tf_op jit(solution)/shard_map/ppermute | solution.py:347
  37.6 1.9 %collective-permute-start.7 = (f32[64,64]{1,0:T(8,128)S(1)}, f32[64,64]{1,0:T(8,128)S(1)}, u32[]{:S(2)}, u32[]{:S(2)}) collective-permute-start(f32[64,64]{1,0:T(8,128)S(1)} %add.17), channel_id=1, source_target_pairs={{0,2},{1,3},{2,0},{3,1},{4,6},{5,7},{6,4},{7,5},{8,10},{9,11},{10,... | collective-permute-start | bytes 49160 | tf_op jit(solution)/shard_map/ppermute | solution.py:347
  39.5 2.0 %collective-permute-done.7 = f32[64,64]{1,0:T(8,128)S(1)} collective-permute-done((f32[64,64]{1,0:T(8,128)S(1)}, f32[64,64]{1,0:T(8,128)S(1)}, u32[]{:S(2)}, u32[]{:S(2)}) %collective-permute-start.7) | collective-permute-done | bytes 16416 | tf_op jit(solution)/shard_map/ppermute | solution.py:347
  41.6 0.9 %collective-permute-start.8 = (f32[64,64]{1,0:T(8,128)S(1)}, f32[64,64]{1,0:T(8,128)S(1)}, u32[]{:S(2)}, u32[]{:S(2)}) collective-permute-start(f32[64,64]{1,0:T(8,128)S(1)} %add.18), channel_id=1, source_target_pairs={{0,1},{1,0},{2,3},{3,2},{4,5},{5,4},{6,7},{7,6},{8,9},{9,8},{10,11... | collective-permute-start | bytes 49160 | tf_op jit(solution)/shard_map/ppermute | solution.py:347
  42.4 3.1 %collective-permute-done.8 = f32[64,64]{1,0:T(8,128)S(1)} collective-permute-done((f32[64,64]{1,0:T(8,128)S(1)}, f32[64,64]{1,0:T(8,128)S(1)}, u32[]{:S(2)}, u32[]{:S(2)}) %collective-permute-start.8) | collective-permute-done | bytes 16416 | tf_op jit(solution)/shard_map/ppermute | solution.py:347
  45.5 13.3 %factor_basis.1 = (f32[64,24,8,128]{3,2,1,0:T(8,128)}, f32[64,64]{1,0:T(8,128)}) custom-call(f32[64,64]{1,0:T(8,128)S(1)} %add.19.part, f32[60,24,8,128]{3,2,1,0:T(8,128)} %bitcast.3, f32[4,24,8,128]{3,2,1,0:T(8,128)S(1)} %get-tuple-element.24.snaps), custom_call_target="tpu_custom_call" | custom-call | tf_op jit(solution)/shard_map/factor_basis/pallas_call | solution.py:405
  (18 shorter events, 0.1 us)
Async XLA Ops:
  0.6 1.0 %copy-start.1 = (f32[4,3,8,8,128]{4,3,2,1,0:T(8,128)S(1)}, f32[4,3,8,8,128]{4,3,2,1,0:T(8,128)}, u32[]{:S(2)}) copy-start(f32[4,3,8,8,128]{4,3,2,1,0:T(8,128)} %f.5) | copy-start | bytes 1179652
  1.6 0.9 %copy-start.3 = (f32[3,8,8,128]{3,2,1,0:T(8,128)S(1)}, f32[3,8,8,128]{3,2,1,0:T(8,128)}, u32[]{:S(2)}) copy-start(f32[3,8,8,128]{3,2,1,0:T(8,128)} %v.5) | copy-start | bytes 294916
  2.5 0.8 %copy-start.5 = (f32[8,8,128]{2,1,0:T(8,128)S(1)}, f32[8,8,128]{2,1,0:T(8,128)}, u32[]{:S(2)}) copy-start(f32[8,8,128]{2,1,0:T(8,128)} %nu.5) | copy-start | bytes 98308
  3.3 13.3 %copy-start.2 = (f32[4,3,8,8,128]{4,3,2,1,0:T(8,128)S(1)}, f32[4,3,8,8,128]{4,3,2,1,0:T(8,128)}, u32[]{:S(2)}) copy-start(f32[4,3,8,8,128]{4,3,2,1,0:T(8,128)} %f.5) | copy-start | bytes 1179652
  3.3 13.3 %copy-start.4 = (f32[3,8,8,128]{3,2,1,0:T(8,128)S(1)}, f32[3,8,8,128]{3,2,1,0:T(8,128)}, u32[]{:S(2)}) copy-start(f32[3,8,8,128]{3,2,1,0:T(8,128)} %v.5) | copy-start | bytes 294916
  3.3 13.3 %copy-start.6 = (f32[8,8,128]{2,1,0:T(8,128)S(1)}, f32[8,8,128]{2,1,0:T(8,128)}, u32[]{:S(2)}) copy-start(f32[8,8,128]{2,1,0:T(8,128)} %nu.5) | copy-start | bytes 98308
  3.3 6.7 %collective-permute-start = (f32[34,8,128]{2,1,0:T(8,128)S(1)}, f32[34,8,128]{2,1,0:T(8,128)S(1)}, u32[]{:S(2)}, u32[]{:S(2)}) collective-permute-start(f32[34,8,128]{2,1,0:T(8,128)S(1)} %get-tuple-element.15), channel_id=1, source_target_pairs={{0,1},{1,0},{2,3},{3,2},{4,5},{5,4},{6,7},{7,6},{8,9},{9,8},{10,11... | collective-permute-start | bytes 417800 | tf_op jit(solution)/shard_map/ppermute | solution.py:333
  6.3 3.7 %collective-permute-start.1 = (f32[34,8,128]{2,1,0:T(8,128)S(1)}, f32[34,8,128]{2,1,0:T(8,128)S(1)}, u32[]{:S(2)}, u32[]{:S(2)}) collective-permute-start(f32[34,8,128]{2,1,0:T(8,128)S(1)} %get-tuple-element.16), channel_id=1, source_target_pairs={{1,2},{2,1},{3,4},{4,3},{5,6},{6,5},{9,10},{10,9},{11,12},{12,11},... | collective-permute-start | bytes 417800 | tf_op jit(solution)/shard_map/ppermute | solution.py:333
  10.1 6.4 %collective-permute-start.2 = (f32[55,8,128]{2,1,0:T(8,128)S(1)}, f32[55,8,128]{2,1,0:T(8,128)S(1)}, u32[]{:S(2)}, u32[]{:S(2)}) collective-permute-start(f32[55,8,128]{2,1,0:T(8,128)S(1)} %get-tuple-element.20), channel_id=1, source_target_pairs={{0,8},{8,0},{16,24},{24,16},{1,9},{9,1},{17,25},{25,17},{2,10},{10... | collective-permute-start | bytes 675848 | tf_op jit(solution)/shard_map/ppermute | solution.py:333
  10.2 6.4 %collective-permute-start.3 = (f32[55,8,128]{2,1,0:T(8,128)S(1)}, f32[55,8,128]{2,1,0:T(8,128)S(1)}, u32[]{:S(2)}, u32[]{:S(2)}) collective-permute-start(f32[55,8,128]{2,1,0:T(8,128)S(1)} %get-tuple-element.21), channel_id=1, source_target_pairs={{8,16},{16,8},{9,17},{17,9},{10,18},{18,10},{11,19},{19,11},{12,20... | collective-permute-start | bytes 675848 | tf_op jit(solution)/shard_map/ppermute | solution.py:333
  10.9 2.7 %copy-start = (f32[60,3,8,8,128]{4,3,2,1,0:T(8,128)S(1)}, f32[60,3,8,8,128]{4,3,2,1,0:T(8,128)}, u32[]{:S(2)}) copy-start(f32[60,3,8,8,128]{4,3,2,1,0:T(8,128)} %param.7) | copy-start | bytes 17694724
  22.3 5.3 %collective-permute-start.4 = (f32[64,64]{1,0:T(8,128)S(1)}, f32[64,64]{1,0:T(8,128)S(1)}, u32[]{:S(2)}, u32[]{:S(2)}) collective-permute-start(f32[64,64]{1,0:T(8,128)S(1)} %get-tuple-element.23), channel_id=1, source_target_pairs={{0,16},{1,17},{2,18},{3,19},{4,20},{5,21},{6,22},{7,23},{8,24},{9,... | collective-permute-start | bytes 49160 | tf_op jit(solution)/shard_map/ppermute | solution.py:347
  27.6 1.5 %collective-permute-start.5 = (f32[64,64]{1,0:T(8,128)S(1)}, f32[64,64]{1,0:T(8,128)S(1)}, u32[]{:S(2)}, u32[]{:S(2)}) collective-permute-start(f32[64,64]{1,0:T(8,128)S(1)} %add.15), channel_id=1, source_target_pairs={{0,8},{1,9},{2,10},{3,11},{4,12},{5,13},{6,14},{7,15},{8,0},{9,1},... | collective-permute-start | bytes 49160 | tf_op jit(solution)/shard_map/ppermute | solution.py:347
  29.1 8.5 %collective-permute-start.6 = (f32[64,64]{1,0:T(8,128)S(1)}, f32[64,64]{1,0:T(8,128)S(1)}, u32[]{:S(2)}, u32[]{:S(2)}) collective-permute-start(f32[64,64]{1,0:T(8,128)S(1)} %add.16), channel_id=1, source_target_pairs={{0,4},{1,5},{2,6},{3,7},{4,0},{5,1},{6,2},{7,3},{8,12},{9,13},{10,... | collective-permute-start | bytes 49160 | tf_op jit(solution)/shard_map/ppermute | solution.py:347
  37.6 3.9 %collective-permute-start.7 = (f32[64,64]{1,0:T(8,128)S(1)}, f32[64,64]{1,0:T(8,128)S(1)}, u32[]{:S(2)}, u32[]{:S(2)}) collective-permute-start(f32[64,64]{1,0:T(8,128)S(1)} %add.17), channel_id=1, source_target_pairs={{0,2},{1,3},{2,0},{3,1},{4,6},{5,7},{6,4},{7,5},{8,10},{9,11},{10,... | collective-permute-start | bytes 49160 | tf_op jit(solution)/shard_map/ppermute | solution.py:347
  41.6 3.9 %collective-permute-start.8 = (f32[64,64]{1,0:T(8,128)S(1)}, f32[64,64]{1,0:T(8,128)S(1)}, u32[]{:S(2)}, u32[]{:S(2)}) collective-permute-start(f32[64,64]{1,0:T(8,128)S(1)} %add.18), channel_id=1, source_target_pairs={{0,1},{1,0},{2,3},{3,2},{4,5},{5,4},{6,7},{7,6},{8,9},{9,8},{10,11... | collective-permute-start | bytes 49160 | tf_op jit(solution)/shard_map/ppermute | solution.py:347

commit v2 on v1

--- a/solution.py
+++ b/solution.py
@@ -10,7 +10,11 @@
 BF16 = jnp.bfloat16
 DEPTH = 4
 VMEM = pl.BlockSpec(memory_space=pltpu.VMEM)
-PARAMS = pltpu.CompilerParams(vmem_limit_bytes=48 << 20)
+HBM = pl.BlockSpec(memory_space=pltpu.HBM)
+
+
+def limit(mib):
+    return pltpu.CompilerParams(vmem_limit_bytes=mib << 20)
 
 
 def struct(*shape):
@@ -43,7 +47,13 @@
     return items
 
 
-def pack_y_kernel(v, nu, f, send_a, send_b):
+def pack_y_kernel(v_in, nu_in, f_in, v, nu, f, send_a, send_b, sems):
+    pairs = ((f_in, f), (v_in, v), (nu_in, nu))
+    copies = [pltpu.make_async_copy(a, b, sems.at[i]) for i, (a, b) in enumerate(pairs)]
+    for copy in copies:
+        copy.start()
+    for copy in copies:
+        copy.wait()
     sub = sub_index()
     even = lax.rem(lax.axis_index("gy"), 2) == 0
     upper, lower = (y_items(v, nu, f, True), y_items(v, nu, f, False))
@@ -78,7 +88,7 @@
     return own, rim
 
 
-def pack_x_kernel(v, nu, f, recv_a, recv_b, rv, rnu, rf, send_a, send_b):
+def pack_x_kernel(v, nu, f, recv_a, recv_b, after, rv, rnu, rf, send_a, send_b):
     sub = sub_index()
     even_y = lax.rem(lax.axis_index("gy"), 2) == 0
     even_x = lax.rem(lax.axis_index("gx"), 2) == 0
@@ -127,7 +137,7 @@
     return jnp.where(sub == 0, turn(second, 1), turn(first, 1))
 
 
-def steps_kernel(v, nu, f, rv, rnu, rf, recv_a, recv_b, kept, square, snaps, final, part, ext, enu, ef, coef):
+def steps_kernel(v, nu, f, rv, rnu, rf, recv_a, recv_b, kept, square_a, square_b, snaps, final, part, ext, enu, ef, coef):
     comps, size_x = v.shape[0], v.shape[1]
     steps = f.shape[0]
     wide = 2 * size_x
@@ -221,7 +231,7 @@
     slabs = kept.shape[1]
     n = rows + steps
     column = lax.broadcasted_iota(jnp.int32, (8, n), 1)
-    total = square[...]
+    total = square_a[...] + square_b[...]
     old = 0.5 * total[:, :n] + total[:, n:]
     scale = 1.0 / (slabs * 8 * 128 * nx * ny)
     for k0 in range(0, n, 8):
@@ -268,10 +278,12 @@
     )
 
 
-def square_kernel(kept, out, *, n):
-    rows, slabs = kept.shape[0], kept.shape[1]
+def square_of(kept, slabs, n, ready=None):
+    rows = kept.shape[0]
     acc = None
-    for s in range(slabs):
+    for s in slabs:
+        if ready is not None:
+            ready(s)
         tiles = jnp.concatenate([kept[:, s], jnp.zeros((n - rows, 8, 128), F32)], 0)
         lines = to_rows(tiles)
         for y in range(0, 8, 2):
@@ -279,72 +291,118 @@
             both = jnp.concatenate([high, low], 0)
             term = lax.dot_general(high, both, (((1,), (1,)), ((), ())), preferred_element_type=F32)
             acc = term if acc is None else acc + term
-    out[...] = acc
+    return acc
+
+
+def square_first_kernel(kept_in, kept, out, sems, *, n, count):
+    slabs = kept.shape[1]
+    step = slabs // sems.shape[0]
+    copies = []
+    for i in range(sems.shape[0]):
+        at = (slice(None), pl.ds(i * step, step))
+        copies.append(pltpu.make_async_copy(kept_in.at[at], kept.at[at], sems.at[i]))
+    for copy in copies:
+        copy.start()
+
+    def ready(s):
+        if s % step == 0:
+            copies[s // step].wait()
+
+    out[...] = square_of(kept, range(count), n, ready)
+    for i in range(-(-count // step), len(copies)):
+        copies[i].wait()
+
+
+def square_rest_kernel(kept, out, *, n, count):
+    out[...] = square_of(kept, range(count, kept.shape[1]), n)
 
 
 def factor_of(gram):
     n = gram.shape[0]
+    count = n // 8
+    sub = sub_index()
     row_at = lax.broadcasted_iota(jnp.int32, (n, n), 0)
     col_at = lax.broadcasted_iota(jnp.int32, (n, n), 1)
     eye = jnp.where(row_at == col_at, 1.0, 0.0).astype(F32)
-    w = jnp.concatenate([gram, eye], 1)
-    at = lax.broadcasted_iota(jnp.int32, (n, 1), 0)
-    for j in range(n - 1):
-        row = w[j : j + 1, :]
-        ratio = row * (1.0 / row[:, j : j + 1])
-        w = w - jnp.where(at > j, w[:, j : j + 1], 0.0) * ratio
-    pivot = jnp.sum(w[:, :n] * eye, axis=1, keepdims=True)
-    return w * lax.rsqrt(pivot)
-
-
-def basis_kernel(part, kept, snaps, basis, factor, left):
+    whole = jnp.concatenate([gram, eye], 1)
+    w = [whole[8 * c : 8 * c + 8] for c in range(count)]
+
+    def spread(tile, j):
+        return jnp.broadcast_to(tile[:, j : j + 1], tile.shape)
+
+    def pick(tile, q):
+        return jnp.broadcast_to(tile[q : q + 1, :], tile.shape)
+
+    for b in range(count):
+        cols = {c: [spread(w[c], 8 * b + q) for q in range(8)] for c in range(b, count)}
+        pivots = jnp.ones(w[b].shape, F32)
+        for q in range(8):
+            head = [pick(cols[b][r], q) for r in range(q, 8)]
+            inverse = 1.0 / head[0]
+            pivots = jnp.where(sub == q, head[0], pivots)
+            line = pick(w[b], q)
+            for c in range(b, count):
+                ratio = cols[c][q] * inverse
+                if c == b:
+                    ratio = jnp.where(sub > q, ratio, 0.0)
+                w[c] = w[c] - ratio * line
+                for r in range(q + 1, 8):
+                    cols[c][r] = cols[c][r] - ratio * head[r - q]
+        w[b] = w[b] * lax.rsqrt(pivots)
+    return jnp.concatenate(w, 0)
+
+
+def basis_kernel(part, kept, snaps, basis, factor, out, sems):
     n = part.shape[0]
-    block = basis.shape[1]
-
-    @pl.when(pl.program_id(0) == 0)
-    def _():
-        m = part[...]
-        w = factor_of(m + m.T)
-        row_at = lax.broadcasted_iota(jnp.int32, (n, n), 0)
-        col_at = lax.broadcasted_iota(jnp.int32, (n, n), 1)
-        factor[...] = jnp.where(row_at <= col_at, w[:, :n], 0.0)
-        high, low = split(w[:, n:])
-        top = jnp.concatenate([high, high], 1)
-        left[...] = jnp.concatenate([top, jnp.concatenate([low, jnp.zeros_like(low)], 1)], 0)
-
-    lhs = left[...]
-    base = pl.program_id(0) * block
-    for s in range(block):
-        lines = to_rows(jnp.concatenate([kept[:, base + s], snaps[:, base + s]], 0))
-        out = []
+    slabs = kept.shape[1]
+    block = slabs // sems.shape[0]
+    m = part[...]
+    w = factor_of(m + m.T)
+    row_at = lax.broadcasted_iota(jnp.int32, (n, n), 0)
+    col_at = lax.broadcasted_iota(jnp.int32, (n, n), 1)
+    factor[...] = jnp.where(row_at <= col_at, w[:, :n], 0.0)
+    high, low = split(w[:, n:])
+    lhs = jnp.concatenate([high, high, low], 1)
+    copies = []
+    for s in range(slabs):
+        lines = to_rows(jnp.concatenate([kept[:, s], snaps[:, s]], 0))
+        pieces = []
         for y in range(0, 8, 2):
             high, low = split(jnp.concatenate(lines[y : y + 2], 1))
-            rhs = jnp.concatenate([high, low], 0)
+            rhs = jnp.concatenate([high, low, high], 0)
             r = lax.dot_general(lhs, rhs, (((1,), (0,)), ((), ())), preferred_element_type=F32)
-            r = r[:n] + r[n:]
-            out += [r[:, :128], r[:, 128:]]
-        basis[:, s] = from_rows(out)
+            pieces += [r[:, :128], r[:, 128:]]
+        out[:, s] = from_rows(pieces)
+        if (s + 1) % block == 0:
+            at = (slice(None), pl.ds(s + 1 - block, block))
+            copy = pltpu.make_async_copy(out.at[at], basis.at[at], sems.at[s // block])
+            copy.start()
+            copies.append(copy)
+    for copy in copies:
+        copy.wait()
 
 
 def pair_exchange(first, second, axis):
     count = lax.axis_size(axis)
     near = [(i, i ^ 1) for i in range(count)]
     far = [(i, ((i + 1) ^ 1) - 1) for i in range(1, count - 1)]
-    return lax.ppermute(first, axis, near), lax.ppermute(second, axis, far)
+    distant = lax.ppermute(second, axis, far)
+    return lax.ppermute(first, axis, near), distant
 
 
 def sum_over(value, axes):
-    sizes = [lax.axis_size(a) for a in axes]
     count = 1
-    for size in sizes:
-        count *= size
+    for axis in axes:
+        count *= lax.axis_size(axis)
     bits = []
-    bit = 1
-    while bit < count:
-        bits.append(bit)
-        bit *= 2
-    for bit in reversed(bits):
-        value = value + lax.ppermute(value, axes, [(i, i ^ bit) for i in range(count)])
+    while 2 ** len(bits) < count:
+        bits.append(2 ** len(bits))
+    bits = bits[::-1]
+    for group in [bits[i : i + 2] for i in range(0, len(bits), 2)]:
+        masks = group + ([group[0] ^ group[1]] if len(group) == 2 else [])
+        others = [lax.ppermute(value, axes, [(i, i ^ m) for i in range(count)]) for m in masks]
+        for other in others:
+            value = value + other
     return value
 
 
@@ -352,25 +410,34 @@
     comps, size_x = velocity.shape[0], velocity.shape[1]
     steps, rows = forcing.shape[0], earlier.shape[0]
     n, slabs = rows + steps, comps * size_x
-    kept = earlier.reshape(rows, slabs, 8, 128)
     half = (2 * slabs + size_x + slabs // 2) // 2
-    call = functools.partial(pl.pallas_call, compiler_params=PARAMS)
-    send_a, send_b = call(
+    call = pl.pallas_call
+    v, nu, f, send_a, send_b = call(
         pack_y_kernel,
-        out_shape=(struct(half, 8, 128),) * 2,
-        in_specs=[VMEM] * 3,
+        out_shape=(
+            struct(*velocity.shape),
+            struct(*viscosity.shape),
+            struct(*forcing.shape),
+            struct(half, 8, 128),
+            struct(half, 8, 128),
+        ),
+        in_specs=[HBM] * 3,
+        out_specs=(VMEM,) * 5,
+        scratch_shapes=[pltpu.SemaphoreType.DMA((3,))],
+        compiler_params=limit(8),
+        name="pack_y",
+    )(*[pltpu.with_memory_space_constraint(a, pltpu.HBM) for a in (velocity, viscosity, forcing)])
+    recv_a, recv_b = pair_exchange(send_a, send_b, "gy")
+    first = slabs * 2 // 3
+    kept, square_a = call(
+        functools.partial(square_first_kernel, n=n, count=first),
+        out_shape=(struct(rows, slabs, 8, 128), struct(n, 2 * n)),
+        in_specs=[HBM],
         out_specs=(VMEM,) * 2,
-        name="pack_y",
-    )(velocity, viscosity, forcing)
-    recv_a, recv_b = pair_exchange(send_a, send_b, "gy")
-    square = call(
-        functools.partial(square_kernel, n=n),
-        out_shape=struct(n, 2 * n),
-        in_specs=[VMEM],
-        out_specs=VMEM,
-        cost_estimate=pl.CostEstimate(flops=2 * n * 2 * n * slabs * 1024, transcendentals=0, bytes_accessed=rows * slabs * 4096 * 2),
-        name="gram_kept",
-    )(kept)
+        scratch_shapes=[pltpu.SemaphoreType.DMA((6,))],
+        compiler_params=limit(8),
+        name="gram_first",
+    )(pltpu.with_memory_space_constraint(earlier.reshape(rows, slabs, 8, 128), pltpu.HBM))
     own, rim = x_items(comps)
     wire = struct(len(own) + len(rim), 8, 128)
     rv, rnu, rf, send_a, send_b = call(
@@ -382,15 +449,24 @@
             wire,
             wire,
         ),
-        in_specs=[VMEM] * 5,
+        in_specs=[VMEM] * 5 + [pl.BlockSpec(memory_space=pl.ANY)],
         out_specs=(VMEM,) * 5,
+        compiler_params=limit(8),
         name="pack_x",
-    )(velocity, viscosity, forcing, recv_a, recv_b)
+    )(v, nu, f, recv_a, recv_b, square_a)
     recv_a, recv_b = pair_exchange(send_a, send_b, "gx")
+    square_b = call(
+        functools.partial(square_rest_kernel, n=n, count=first),
+        out_shape=struct(n, 2 * n),
+        in_specs=[VMEM],
+        out_specs=VMEM,
+        compiler_params=limit(8),
+        name="gram_rest",
+    )(kept)
     snaps, final, part = call(
         steps_kernel,
         out_shape=(struct(steps, slabs, 8, 128), struct(*velocity.shape), struct(n, n)),
-        in_specs=[VMEM] * 10,
+        in_specs=[VMEM] * 11,
         out_specs=(VMEM,) * 3,
         scratch_shapes=[
             pltpu.VMEM((2, comps, 2 * size_x, 2, 8, 128), F32),
@@ -398,20 +474,17 @@
             pltpu.VMEM((3, comps, 2 * size_x, 2, 8, 128), F32),
             pltpu.VMEM((2 * size_x, 2, 7, 8, 128), F32),
         ],
+        compiler_params=limit(12),
         name="steps",
-    )(velocity, viscosity, forcing, rv, rnu, rf, recv_a, recv_b, kept, square)
+    )(v, nu, f, rv, rnu, rf, recv_a, recv_b, kept, square_a, square_b)
     part = sum_over(part, ("gx", "gy"))
-    block = 6
     basis, factor = call(
         basis_kernel,
-        grid=(slabs // block,),
         out_shape=(struct(n, slabs, 8, 128), struct(n, n)),
         in_specs=[VMEM] * 3,
-        out_specs=(
-            pl.BlockSpec((n, block, 8, 128), lambda i: (0, i, 0, 0)),
-            pl.BlockSpec((n, n), lambda i: (0, 0)),
-        ),
-        scratch_shapes=[pltpu.VMEM((2 * n, 2 * n), BF16)],
+        out_specs=(HBM, VMEM),
+        scratch_shapes=[pltpu.VMEM((n, slabs, 8, 128), F32), pltpu.SemaphoreType.DMA((slabs // 3,))],
+        compiler_params=limit(16),
         name="factor_basis",
     )(part, kept, snaps)
     return final, basis.reshape((n,) + velocity.shape), factor

time: 59.2 us -> 48.6 us (0.82)
  Pallas kernels: 22.2 us -> 16.5 us
  local copies, waits for them, and re-layouts: 5.32 us -> 0 us
  starting transfers between devices: 17.8 us -> 20.6 us
  waiting for transfers between devices: 12.7 us -> 10.6 us
    unnamed x14 -> x0, local copies, waits for them, and re-layouts: 5.32 us -> none
    pallas_call x3 -> x4, Pallas kernels: 16.4 us -> 13.4 us  [the longest x1 7.19 us: local(): call(basis_kernel, out_shape=(struct(n, slabs, 8, 128), struct(n, n)), in...]
    ppermute x9 -> x11, starting transfers between devices: 17.8 us -> 20.6 us  [the longest x7 16.2 us: sum_over(): lax.ppermute(value, axes, [(i, i ^ m) for i in range(count)])]
    pallas_call x1, Pallas kernels: 5.75 us -> 3.06 us  [local(): call(steps_kernel, out_shape=(struct(steps, slabs, 8, 128), struct(*veloc...]
    ppermute x9 -> x11, waiting for transfers between devices: 12.7 us -> 10.6 us  [the longest x7 10.6 us: sum_over(): lax.ppermute(value, axes, [(i, i ^ m) for i in range(count)])]
  transfers between devices with their start and end apart: 9 -> 11, of which waited for: 6 -> 6; matrix products, arithmetic and copies ran while one was open for 0% -> 0% of each run, Pallas kernels for 5% -> 11%
where the time goes in v2:
time: 48.6 us; the launch traced here: 48.4 us
  starting transfers between devices  20.6 us (42%)
  Pallas kernels  16.5 us (34%)
  waiting for transfers between devices  10.6 us (22%)
  between operations  0.72 us (1%)
    ppermute x7, starting transfers between devices, sum_over(): lax.ppermute(value, axes, [(i, i ^ m) for i in range(count)])  16.2 us
    ppermute x7, waiting for transfers between devices, sum_over(): lax.ppermute(value, axes, [(i, i ^ m) for i in range(count)])  10.6 us
    pallas_call x1, Pallas kernels, local(): call(basis_kernel, out_shape=(struct(n, slabs, 8, 128), struct(n, n)), in...  7.19 us
    pallas_call x1, Pallas kernels, local(): call(functools.partial(square_first_kernel, n=n, count=first), out_shape=...  4.03 us
    ppermute x2, starting transfers between devices, pair_exchange(): return (lax.ppermute(first, axis, near), distant)  3.07 us
    pallas_call x1, Pallas kernels, local(): call(steps_kernel, out_shape=(struct(steps, slabs, 8, 128), struct(*veloc...  3.06 us
    ppermute x2, starting transfers between devices, pair_exchange(): distant = lax.ppermute(second, axis, far)  1.33 us
    pallas_call x1, Pallas kernels, local(): call(pack_y_kernel, out_shape=(struct(*velocity.shape), struct(*viscosity...  1.09 us
  transfers between devices with their start and end apart: 11, of which 6 were waited for; matrix products, arithmetic and copies ran while one was open for 0% of the time, Pallas kernels for 11%

profile of v2, /device:TPU:0, one launch (start us, length us, event | category | flops | bytes accessed | tf_op | source)
XLA Modules:
  0.0 48.4 jit_solution(12746787797199259264)
XLA Ops:
  0.6 1.1 %pack_y.1 = (f32[3,8,8,128]{3,2,1,0:T(8,128)S(1)}, f32[8,8,128]{2,1,0:T(8,128)S(1)}, f32[4,3,8,8,128]{4,3,2,1,0:T(8,128)S(1)}, f32[34,8,128]{2,1,0:T(8,128)S(1)}, f32[34,8,128]{2,1,0:T(8,128)S(1)}) custom-call(f32[3,8,8,128]{3,2,1,0:T(8,128)} %v_in.1, f32[8,8,128]{2,1,0:T(8,128)} %nu_in.1, f32[4,3,8,8,128]{4,3,2,1,0:T(8,128)} %f_in.1), custom_call_target="tpu_custom_call" | custom-call | tf_op jit(solution)/shard_map/pack_y/pallas_call | solution.py:415
  1.7 3.0 %collective-permute-start = (f32[34,8,128]{2,1,0:T(8,128)S(1)}, f32[34,8,128]{2,1,0:T(8,128)S(1)}, u32[]{:S(2)}, u32[]{:S(2)}) collective-permute-start(f32[34,8,128]{2,1,0:T(8,128)S(1)} %get-tuple-element.23), channel_id=1, source_target_pairs={{0,1},{1,0},{2,3},{3,2},{4,5},{5,4},{6,7},{7,6},{8,9},{9,8},{10,11... | collective-permute-start | bytes 417800 | tf_op jit(solution)/shard_map/ppermute | solution.py:390
  4.7 0.7 %collective-permute-start.1 = (f32[34,8,128]{2,1,0:T(8,128)S(1)}, f32[34,8,128]{2,1,0:T(8,128)S(1)}, u32[]{:S(2)}, u32[]{:S(2)}) collective-permute-start(f32[34,8,128]{2,1,0:T(8,128)S(1)} %get-tuple-element.24), channel_id=1, source_target_pairs={{1,2},{2,1},{3,4},{4,3},{5,6},{6,5},{9,10},{10,9},{11,12},{12,11},... | collective-permute-start | bytes 417800 | tf_op jit(solution)/shard_map/ppermute | solution.py:389
  5.4 4.0 %gram_first.1 = (f32[60,24,8,128]{3,2,1,0:T(8,128)S(1)}, f32[64,128]{1,0:T(8,128)S(1)}) custom-call(f32[60,24,8,128]{3,2,1,0:T(8,128)} %bitcast.2), custom_call_target="tpu_custom_call" | custom-call | tf_op jit(solution)/shard_map/gram_first/pallas_call | solution.py:432
  9.4 0.0 collective-permute-done.recv_a
  9.4 0.0 collective-permute-done.1.recv_b
  9.5 0.1 pack_x.1
  9.6 0.1 collective-permute-start.2
  9.6 0.7 %collective-permute-start.3 = (f32[55,8,128]{2,1,0:T(8,128)S(1)}, f32[55,8,128]{2,1,0:T(8,128)S(1)}, u32[]{:S(2)}, u32[]{:S(2)}) collective-permute-start(f32[55,8,128]{2,1,0:T(8,128)S(1)} %get-tuple-element.30), channel_id=1, source_target_pairs={{8,16},{16,8},{9,17},{17,9},{10,18},{18,10},{11,19},{19,11},{12,20... | collective-permute-start | bytes 675848 | tf_op jit(solution)/shard_map/ppermute | solution.py:389
  10.3 1.1 %gram_rest.1.square_b = f32[64,128]{1,0:T(8,128)S(1)} custom-call(f32[60,24,8,128]{3,2,1,0:T(8,128)S(1)} %get-tuple-element.31.kept), custom_call_target="tpu_custom_call" | custom-call | tf_op jit(solution)/shard_map/gram_rest/pallas_call | solution.py:458
  11.4 3.1 %steps.1 = (f32[4,24,8,128]{3,2,1,0:T(8,128)S(1)}, f32[3,8,8,128]{3,2,1,0:T(8,128)}, f32[64,64]{1,0:T(8,128)S(1)}) custom-call(f32[3,8,8,128]{3,2,1,0:T(8,128)S(1)} %get-tuple-element.20.v, f32[8,8,128]{2,1,0:T(8,128)S(1)} %get-tuple-element.21.nu, f32[4,3,8,8,128]{4,3,2,1,0:T(8,128)S(1)} %get-tuple-element.22.f, f32[3,8,8,128]{3,2,1,0:T(8,128)S(1)} %get-tuple-element.26.rv, ...), custom_call_target="tpu_custom_call" | custom-call | tf_op jit(solution)/shard_map/steps/pallas_call | solution.py:466
  14.5 1.6 %collective-permute-start.6 = (f32[64,64]{1,0:T(8,128)S(1)}, f32[64,64]{1,0:T(8,128)S(1)}, u32[]{:S(2)}, u32[]{:S(2)}) collective-permute-start(f32[64,64]{1,0:T(8,128)S(1)} %get-tuple-element.33), channel_id=1, source_target_pairs={{0,24},{1,25},{2,26},{3,27},{4,28},{5,29},{6,30},{7,31},{8,16},{9,... | collective-permute-start | bytes 49160 | tf_op jit(solution)/shard_map/ppermute | solution.py:403
  16.1 5.5 %collective-permute-start.5 = (f32[64,64]{1,0:T(8,128)S(1)}, f32[64,64]{1,0:T(8,128)S(1)}, u32[]{:S(2)}, u32[]{:S(2)}) collective-permute-start(f32[64,64]{1,0:T(8,128)S(1)} %get-tuple-element.33), channel_id=1, source_target_pairs={{0,8},{1,9},{2,10},{3,11},{4,12},{5,13},{6,14},{7,15},{8,0},{9,1},... | collective-permute-start | bytes 49160 | tf_op jit(solution)/shard_map/ppermute | solution.py:403
  21.7 0.8 %collective-permute-start.4 = (f32[64,64]{1,0:T(8,128)S(1)}, f32[64,64]{1,0:T(8,128)S(1)}, u32[]{:S(2)}, u32[]{:S(2)}) collective-permute-start(f32[64,64]{1,0:T(8,128)S(1)} %get-tuple-element.33), channel_id=1, source_target_pairs={{0,16},{1,17},{2,18},{3,19},{4,20},{5,21},{6,22},{7,23},{8,24},{9,... | collective-permute-start | bytes 49160 | tf_op jit(solution)/shard_map/ppermute | solution.py:403
  22.5 0.1 collective-permute-done.5
  22.5 3.1 %collective-permute-done.4 = f32[64,64]{1,0:T(8,128)S(1)} collective-permute-done((f32[64,64]{1,0:T(8,128)S(1)}, f32[64,64]{1,0:T(8,128)S(1)}, u32[]{:S(2)}, u32[]{:S(2)}) %collective-permute-start.4) | collective-permute-done | bytes 16416 | tf_op jit(solution)/shard_map/ppermute | solution.py:403
  25.6 6.8 %collective-permute-start.9 = (f32[64,64]{1,0:T(8,128)S(1)}, f32[64,64]{1,0:T(8,128)S(1)}, u32[]{:S(2)}, u32[]{:S(2)}) collective-permute-start(f32[64,64]{1,0:T(8,128)S(1)} %add_add_fusion.1), channel_id=1, source_target_pairs={{0,6},{1,7},{2,4},{3,5},{4,2},{5,3},{6,0},{7,1},{8,14},{9,15},{10,... | collective-permute-start | bytes 49160 | tf_op jit(solution)/shard_map/ppermute | solution.py:403
  32.4 0.6 %collective-permute-start.7 = (f32[64,64]{1,0:T(8,128)S(1)}, f32[64,64]{1,0:T(8,128)S(1)}, u32[]{:S(2)}, u32[]{:S(2)}) collective-permute-start(f32[64,64]{1,0:T(8,128)S(1)} %add_add_fusion.1), channel_id=1, source_target_pairs={{0,4},{1,5},{2,6},{3,7},{4,0},{5,1},{6,2},{7,3},{8,12},{9,13},{10,... | collective-permute-start | bytes 49160 | tf_op jit(solution)/shard_map/ppermute | solution.py:403
  33.1 1.3 %collective-permute-done.9 = f32[64,64]{1,0:T(8,128)S(1)} collective-permute-done((f32[64,64]{1,0:T(8,128)S(1)}, f32[64,64]{1,0:T(8,128)S(1)}, u32[]{:S(2)}, u32[]{:S(2)}) %collective-permute-start.9) | collective-permute-done | bytes 16416 | tf_op jit(solution)/shard_map/ppermute | solution.py:403
  34.4 2.0 %collective-permute-done.8 = f32[64,64]{1,0:T(8,128)S(1)} collective-permute-done((f32[64,64]{1,0:T(8,128)S(1)}, f32[64,64]{1,0:T(8,128)S(1)}, u32[]{:S(2)}, u32[]{:S(2)}) %collective-permute-start.8) | collective-permute-done | bytes 16416 | tf_op jit(solution)/shard_map/ppermute | solution.py:403
  36.4 0.9 %collective-permute-done.7 = f32[64,64]{1,0:T(8,128)S(1)} collective-permute-done((f32[64,64]{1,0:T(8,128)S(1)}, f32[64,64]{1,0:T(8,128)S(1)}, u32[]{:S(2)}, u32[]{:S(2)}) %collective-permute-start.7) | collective-permute-done | bytes 16416 | tf_op jit(solution)/shard_map/ppermute | solution.py:403
  37.3 0.7 %collective-permute-start.10 = (f32[64,64]{1,0:T(8,128)S(1)}, f32[64,64]{1,0:T(8,128)S(1)}, u32[]{:S(2)}, u32[]{:S(2)}) collective-permute-start(f32[64,64]{1,0:T(8,128)S(1)} %add_add_fusion), channel_id=1, source_target_pairs={{0,1},{1,0},{2,3},{3,2},{4,5},{5,4},{6,7},{7,6},{8,9},{9,8},{10,11... | collective-permute-start | bytes 49160 | tf_op jit(solution)/shard_map/ppermute | solution.py:403
  38.0 3.3 %collective-permute-done.10 = f32[64,64]{1,0:T(8,128)S(1)} collective-permute-done((f32[64,64]{1,0:T(8,128)S(1)}, f32[64,64]{1,0:T(8,128)S(1)}, u32[]{:S(2)}, u32[]{:S(2)}) %collective-permute-start.10) | collective-permute-done | bytes 16416 | tf_op jit(solution)/shard_map/ppermute | solution.py:403
  41.3 7.2 %factor_basis.1 = (f32[64,24,8,128]{3,2,1,0:T(8,128)}, f32[64,64]{1,0:T(8,128)}) custom-call(f32[64,64]{1,0:T(8,128)S(1)} %add.27.part, f32[60,24,8,128]{3,2,1,0:T(8,128)S(1)} %get-tuple-element.31.kept, f32[4,24,8,128]{3,2,1,0:T(8,128)S(1)} %get-tuple-element.34.snaps), custom_call_target="tpu_custom_call" | custom-call | tf_op jit(solution)/shard_map/factor_basis/pallas_call | solution.py:481
  (7 shorter events, 0.0 us)
Async XLA Ops:
  1.7 7.7 %collective-permute-start = (f32[34,8,128]{2,1,0:T(8,128)S(1)}, f32[34,8,128]{2,1,0:T(8,128)S(1)}, u32[]{:S(2)}, u32[]{:S(2)}) collective-permute-start(f32[34,8,128]{2,1,0:T(8,128)S(1)} %get-tuple-element.23), channel_id=1, source_target_pairs={{0,1},{1,0},{2,3},{3,2},{4,5},{5,4},{6,7},{7,6},{8,9},{9,8},{10,11... | collective-permute-start | bytes 417800 | tf_op jit(solution)/shard_map/ppermute | solution.py:390
  4.7 4.7 %collective-permute-start.1 = (f32[34,8,128]{2,1,0:T(8,128)S(1)}, f32[34,8,128]{2,1,0:T(8,128)S(1)}, u32[]{:S(2)}, u32[]{:S(2)}) collective-permute-start(f32[34,8,128]{2,1,0:T(8,128)S(1)} %get-tuple-element.24), channel_id=1, source_target_pairs={{1,2},{2,1},{3,4},{4,3},{5,6},{6,5},{9,10},{10,9},{11,12},{12,11},... | collective-permute-start | bytes 417800 | tf_op jit(solution)/shard_map/ppermute | solution.py:389
  9.6 1.9 %collective-permute-start.2 = (f32[55,8,128]{2,1,0:T(8,128)S(1)}, f32[55,8,128]{2,1,0:T(8,128)S(1)}, u32[]{:S(2)}, u32[]{:S(2)}) collective-permute-start(f32[55,8,128]{2,1,0:T(8,128)S(1)} %get-tuple-element.29), channel_id=1, source_target_pairs={{0,8},{8,0},{16,24},{24,16},{1,9},{9,1},{17,25},{25,17},{2,10},{10... | collective-permute-start | bytes 675848 | tf_op jit(solution)/shard_map/ppermute | solution.py:390
  9.6 1.8 %collective-permute-start.3 = (f32[55,8,128]{2,1,0:T(8,128)S(1)}, f32[55,8,128]{2,1,0:T(8,128)S(1)}, u32[]{:S(2)}, u32[]{:S(2)}) collective-permute-start(f32[55,8,128]{2,1,0:T(8,128)S(1)} %get-tuple-element.30), channel_id=1, source_target_pairs={{8,16},{16,8},{9,17},{17,9},{10,18},{18,10},{11,19},{19,11},{12,20... | collective-permute-start | bytes 675848 | tf_op jit(solution)/shard_map/ppermute | solution.py:389
  14.5 8.0 %collective-permute-start.6 = (f32[64,64]{1,0:T(8,128)S(1)}, f32[64,64]{1,0:T(8,128)S(1)}, u32[]{:S(2)}, u32[]{:S(2)}) collective-permute-start(f32[64,64]{1,0:T(8,128)S(1)} %get-tuple-element.33), channel_id=1, source_target_pairs={{0,24},{1,25},{2,26},{3,27},{4,28},{5,29},{6,30},{7,31},{8,16},{9,... | collective-permute-start | bytes 49160 | tf_op jit(solution)/shard_map/ppermute | solution.py:403
  16.1 6.4 %collective-permute-start.5 = (f32[64,64]{1,0:T(8,128)S(1)}, f32[64,64]{1,0:T(8,128)S(1)}, u32[]{:S(2)}, u32[]{:S(2)}) collective-permute-start(f32[64,64]{1,0:T(8,128)S(1)} %get-tuple-element.33), channel_id=1, source_target_pairs={{0,8},{1,9},{2,10},{3,11},{4,12},{5,13},{6,14},{7,15},{8,0},{9,1},... | collective-permute-start | bytes 49160 | tf_op jit(solution)/shard_map/ppermute | solution.py:403
  21.7 3.9 %collective-permute-start.4 = (f32[64,64]{1,0:T(8,128)S(1)}, f32[64,64]{1,0:T(8,128)S(1)}, u32[]{:S(2)}, u32[]{:S(2)}) collective-permute-start(f32[64,64]{1,0:T(8,128)S(1)} %get-tuple-element.33), channel_id=1, source_target_pairs={{0,16},{1,17},{2,18},{3,19},{4,20},{5,21},{6,22},{7,23},{8,24},{9,... | collective-permute-start | bytes 49160 | tf_op jit(solution)/shard_map/ppermute | solution.py:403
  25.6 8.8 %collective-permute-start.9 = (f32[64,64]{1,0:T(8,128)S(1)}, f32[64,64]{1,0:T(8,128)S(1)}, u32[]{:S(2)}, u32[]{:S(2)}) collective-permute-start(f32[64,64]{1,0:T(8,128)S(1)} %add_add_fusion.1), channel_id=1, source_target_pairs={{0,6},{1,7},{2,4},{3,5},{4,2},{5,3},{6,0},{7,1},{8,14},{9,15},{10,... | collective-permute-start | bytes 49160 | tf_op jit(solution)/shard_map/ppermute | solution.py:403
  32.4 3.9 %collective-permute-start.8 = (f32[64,64]{1,0:T(8,128)S(1)}, f32[64,64]{1,0:T(8,128)S(1)}, u32[]{:S(2)}, u32[]{:S(2)}) collective-permute-start(f32[64,64]{1,0:T(8,128)S(1)} %add_add_fusion.1), channel_id=1, source_target_pairs={{0,2},{1,3},{2,0},{3,1},{4,6},{5,7},{6,4},{7,5},{8,10},{9,11},{10,... | collective-permute-start | bytes 49160 | tf_op jit(solution)/shard_map/ppermute | solution.py:403
  32.4 4.8 %collective-permute-start.7 = (f32[64,64]{1,0:T(8,128)S(1)}, f32[64,64]{1,0:T(8,128)S(1)}, u32[]{:S(2)}, u32[]{:S(2)}) collective-permute-start(f32[64,64]{1,0:T(8,128)S(1)} %add_add_fusion.1), channel_id=1, source_target_pairs={{0,4},{1,5},{2,6},{3,7},{4,0},{5,1},{6,2},{7,3},{8,12},{9,13},{10,... | collective-permute-start | bytes 49160 | tf_op jit(solution)/shard_map/ppermute | solution.py:403
  37.3 4.0 %collective-permute-start.10 = (f32[64,64]{1,0:T(8,128)S(1)}, f32[64,64]{1,0:T(8,128)S(1)}, u32[]{:S(2)}, u32[]{:S(2)}) collective-permute-start(f32[64,64]{1,0:T(8,128)S(1)} %add_add_fusion), channel_id=1, source_target_pairs={{0,1},{1,0},{2,3},{3,2},{4,5},{5,4},{6,7},{7,6},{8,9},{9,8},{10,11... | collective-permute-start | bytes 49160 | tf_op jit(solution)/shard_map/ppermute | solution.py:403

commit v3 on v2

--- a/solution.py
+++ b/solution.py
@@ -352,9 +352,18 @@
     return jnp.concatenate(w, 0)
 
 
-def basis_kernel(part, kept, snaps, basis, factor, out, sems):
+def halves_kernel(kept, snaps, panel):
+    n = panel.shape[1] // 2
+    for s in range(kept.shape[1]):
+        lines = to_rows(jnp.concatenate([kept[:, s], snaps[:, s]], 0))
+        for i in range(4):
+            high, low = split(jnp.concatenate(lines[2 * i : 2 * i + 2], 1))
+            panel[4 * s + i, :n], panel[4 * s + i, n:] = high, low
+
+
+def basis_kernel(part, panel, basis, factor, out, sems):
     n = part.shape[0]
-    slabs = kept.shape[1]
+    slabs = panel.shape[0] // 4
     block = slabs // sems.shape[0]
     m = part[...]
     w = factor_of(m + m.T)
@@ -365,11 +374,10 @@
     lhs = jnp.concatenate([high, high, low], 1)
     copies = []
     for s in range(slabs):
-        lines = to_rows(jnp.concatenate([kept[:, s], snaps[:, s]], 0))
         pieces = []
-        for y in range(0, 8, 2):
-            high, low = split(jnp.concatenate(lines[y : y + 2], 1))
-            rhs = jnp.concatenate([high, low, high], 0)
+        for i in range(4):
+            both = panel[4 * s + i]
+            rhs = jnp.concatenate([both, both[:n]], 0)
             r = lax.dot_general(lhs, rhs, (((1,), (0,)), ((), ())), preferred_element_type=F32)
             pieces += [r[:, :128], r[:, 128:]]
         out[:, s] = from_rows(pieces)
@@ -390,17 +398,22 @@
     return lax.ppermute(first, axis, near), distant
 
 
-def sum_over(value, axes):
-    count = 1
-    for axis in axes:
-        count *= lax.axis_size(axis)
-    bits = []
-    while 2 ** len(bits) < count:
-        bits.append(2 ** len(bits))
-    bits = bits[::-1]
-    for group in [bits[i : i + 2] for i in range(0, len(bits), 2)]:
+def sum_over(value, minor, major):
+    inner, outer = lax.axis_size(minor), lax.axis_size(major)
+    count = inner * outer
+    if count & (count - 1):
+        return lax.psum(value, (major, minor))
+    low = [1 << i for i in range(inner.bit_length() - 1)]
+    high = [inner << i for i in range(outer.bit_length() - 1)]
+    both = min(len(low), len(high))
+    groups = [[high[i], low[i]] for i in range(both)]
+    rest = low[both:] + high[both:]
+    groups += [rest[i : i + 2] for i in range(0, len(rest), 2)]
+    for group in groups:
         masks = group + ([group[0] ^ group[1]] if len(group) == 2 else [])
-        others = [lax.ppermute(value, axes, [(i, i ^ m) for i in range(count)]) for m in masks]
+        others = [
+            lax.ppermute(value, (major, minor), [(i, i ^ m) for i in range(count)]) for m in masks
+        ]
         for other in others:
             value = value + other
     return value
@@ -477,16 +490,24 @@
         compiler_params=limit(12),
         name="steps",
     )(v, nu, f, rv, rnu, rf, recv_a, recv_b, kept, square_a, square_b)
-    part = sum_over(part, ("gx", "gy"))
+    panel = call(
+        halves_kernel,
+        out_shape=jax.ShapeDtypeStruct((4 * slabs, 2 * n, 256), BF16),
+        in_specs=[VMEM] * 2,
+        out_specs=VMEM,
+        compiler_params=limit(8),
+        name="halves",
+    )(kept, snaps)
+    part = sum_over(part, "gy", "gx")
     basis, factor = call(
         basis_kernel,
         out_shape=(struct(n, slabs, 8, 128), struct(n, n)),
-        in_specs=[VMEM] * 3,
+        in_specs=[VMEM] * 2,
         out_specs=(HBM, VMEM),
         scratch_shapes=[pltpu.VMEM((n, slabs, 8, 128), F32), pltpu.SemaphoreType.DMA((slabs // 3,))],
         compiler_params=limit(16),
         name="factor_basis",
-    )(part, kept, snaps)
+    )(part, panel)
     return final, basis.reshape((n,) + velocity.shape), factor
 
 

time: 48.6 us -> 45.1 us (0.928)
  waiting for transfers between devices: 10.6 us -> 5.82 us
  Pallas kernels: 16.5 us -> 17.1 us
  starting transfers between devices: 20.6 us -> 21.1 us
    ppermute x7, waiting for transfers between devices: 10.6 us -> 5.81 us  [sum_over(): lax.ppermute(value, (major, minor), [(i, i ^ m) for i in range(count)])]
    pallas_call x0 -> x1, Pallas kernels: none -> 2.05 us  [local(): call(halves_kernel, out_shape=jax.ShapeDtypeStruct((4 * slabs, 2 * n, 256...]
    pallas_call x1, Pallas kernels: 7.19 us -> 5.67 us  [local(): call(basis_kernel, out_shape=(struct(n, slabs, 8, 128), struct(n, n)), in...]
  transfers between devices with their start and end apart: 11 -> 11, of which waited for: 6 -> 4; matrix products, arithmetic and copies ran while one was open for 0% -> 0% of each run, Pallas kernels for 11% -> 16%
where the time goes in v3:
time: 45.1 us; the launch traced here: 45 us
  starting transfers between devices  21.1 us (47%)
  Pallas kernels  17.1 us (38%)
  waiting for transfers between devices  5.82 us (13%)
  between operations  0.91 us (2%)
    ppermute x7, starting transfers between devices, sum_over(): lax.ppermute(value, (major, minor), [(i, i ^ m) for i in range(count)])  16.5 us
    ppermute x7, waiting for transfers between devices, sum_over(): lax.ppermute(value, (major, minor), [(i, i ^ m) for i in range(count)])  5.81 us
    pallas_call x1, Pallas kernels, local(): call(basis_kernel, out_shape=(struct(n, slabs, 8, 128), struct(n, n)), in...  5.67 us
    pallas_call x1, Pallas kernels, local(): call(functools.partial(square_first_kernel, n=n, count=first), out_shape=...  4.03 us
    ppermute x2, starting transfers between devices, pair_exchange(): return (lax.ppermute(first, axis, near), distant)  3.07 us
    pallas_call x1, Pallas kernels, local(): call(steps_kernel, out_shape=(struct(steps, slabs, 8, 128), struct(*veloc...  3.07 us
    pallas_call x1, Pallas kernels, local(): call(halves_kernel, out_shape=jax.ShapeDtypeStruct((4 * slabs, 2 * n, 256...  2.05 us
    ppermute x2, starting transfers between devices, pair_exchange(): distant = lax.ppermute(second, axis, far)  1.51 us
  transfers between devices with their start and end apart: 11, of which 4 were waited for; matrix products, arithmetic and copies ran while one was open for 0% of the time, Pallas kernels for 16%

profile of v3, /device:TPU:0, one launch (start us, length us, event | category | flops | bytes accessed | tf_op | source)
XLA Modules:
  0.0 45.0 jit_solution(8828285253676581664)
XLA Ops:
  0.6 1.1 %pack_y.1 = (f32[3,8,8,128]{3,2,1,0:T(8,128)S(1)}, f32[8,8,128]{2,1,0:T(8,128)S(1)}, f32[4,3,8,8,128]{4,3,2,1,0:T(8,128)S(1)}, f32[34,8,128]{2,1,0:T(8,128)S(1)}, f32[34,8,128]{2,1,0:T(8,128)S(1)}) custom-call(f32[3,8,8,128]{3,2,1,0:T(8,128)} %v_in.1, f32[8,8,128]{2,1,0:T(8,128)} %nu_in.1, f32[4,3,8,8,128]{4,3,2,1,0:T(8,128)} %f_in.1), custom_call_target="tpu_custom_call" | custom-call | tf_op jit(solution)/shard_map/pack_y/pallas_call | solution.py:428
  1.7 3.0 %collective-permute-start = (f32[34,8,128]{2,1,0:T(8,128)S(1)}, f32[34,8,128]{2,1,0:T(8,128)S(1)}, u32[]{:S(2)}, u32[]{:S(2)}) collective-permute-start(f32[34,8,128]{2,1,0:T(8,128)S(1)} %get-tuple-element.23), channel_id=1, source_target_pairs={{0,1},{1,0},{2,3},{3,2},{4,5},{5,4},{6,7},{7,6},{8,9},{9,8},{10,11... | collective-permute-start | bytes 417800 | tf_op jit(solution)/shard_map/ppermute | solution.py:398
  4.7 0.7 %collective-permute-start.1 = (f32[34,8,128]{2,1,0:T(8,128)S(1)}, f32[34,8,128]{2,1,0:T(8,128)S(1)}, u32[]{:S(2)}, u32[]{:S(2)}) collective-permute-start(f32[34,8,128]{2,1,0:T(8,128)S(1)} %get-tuple-element.24), channel_id=1, source_target_pairs={{1,2},{2,1},{3,4},{4,3},{5,6},{6,5},{9,10},{10,9},{11,12},{12,11},... | collective-permute-start | bytes 417800 | tf_op jit(solution)/shard_map/ppermute | solution.py:397
  5.4 4.0 %gram_first.1 = (f32[60,24,8,128]{3,2,1,0:T(8,128)S(1)}, f32[64,128]{1,0:T(8,128)S(1)}) custom-call(f32[60,24,8,128]{3,2,1,0:T(8,128)} %bitcast.2), custom_call_target="tpu_custom_call" | custom-call | tf_op jit(solution)/shard_map/gram_first/pallas_call | solution.py:445
  9.4 0.0 collective-permute-done.recv_a
  9.5 0.1 pack_x.1
  9.6 0.1 collective-permute-start.2
  9.6 0.9 %collective-permute-start.3 = (f32[55,8,128]{2,1,0:T(8,128)S(1)}, f32[55,8,128]{2,1,0:T(8,128)S(1)}, u32[]{:S(2)}, u32[]{:S(2)}) collective-permute-start(f32[55,8,128]{2,1,0:T(8,128)S(1)} %get-tuple-element.30), channel_id=1, source_target_pairs={{8,16},{16,8},{9,17},{17,9},{10,18},{18,10},{11,19},{19,11},{12,20... | collective-permute-start | bytes 675848 | tf_op jit(solution)/shard_map/ppermute | solution.py:397
  10.5 1.1 %gram_rest.1.square_b = f32[64,128]{1,0:T(8,128)S(1)} custom-call(f32[60,24,8,128]{3,2,1,0:T(8,128)S(1)} %get-tuple-element.31.kept), custom_call_target="tpu_custom_call" | custom-call | tf_op jit(solution)/shard_map/gram_rest/pallas_call | solution.py:471
  11.6 0.0 collective-permute-done.2.recv_a
  11.6 3.1 %steps.1 = (f32[4,24,8,128]{3,2,1,0:T(8,128)S(1)}, f32[3,8,8,128]{3,2,1,0:T(8,128)}, f32[64,64]{1,0:T(8,128)S(1)}) custom-call(f32[3,8,8,128]{3,2,1,0:T(8,128)S(1)} %get-tuple-element.20.v, f32[8,8,128]{2,1,0:T(8,128)S(1)} %get-tuple-element.21.nu, f32[4,3,8,8,128]{4,3,2,1,0:T(8,128)S(1)} %get-tuple-element.22.f, f32[3,8,8,128]{3,2,1,0:T(8,128)S(1)} %get-tuple-element.26.rv, ...), custom_call_target="tpu_custom_call" | custom-call | tf_op jit(solution)/shard_map/steps/pallas_call | solution.py:479
  14.7 9.7 %collective-permute-start.6 = (f32[64,64]{1,0:T(8,128)S(1)}, f32[64,64]{1,0:T(8,128)S(1)}, u32[]{:S(2)}, u32[]{:S(2)}) collective-permute-start(f32[64,64]{1,0:T(8,128)S(1)} %get-tuple-element.33), channel_id=1, source_target_pairs={{0,9},{1,8},{2,11},{3,10},{4,13},{5,12},{6,15},{7,14},{8,1},{9,0},... | collective-permute-start | bytes 49160 | tf_op jit(solution)/shard_map/ppermute | solution.py:415
  24.4 0.2 collective-permute-start.4
  24.6 1.4 %collective-permute-done.6 = f32[64,64]{1,0:T(8,128)S(1)} collective-permute-done((f32[64,64]{1,0:T(8,128)S(1)}, f32[64,64]{1,0:T(8,128)S(1)}, u32[]{:S(2)}, u32[]{:S(2)}) %collective-permute-start.6) | collective-permute-done | bytes 16416 | tf_op jit(solution)/shard_map/ppermute | solution.py:415
  26.0 2.3 %collective-permute-done.5 = f32[64,64]{1,0:T(8,128)S(1)} collective-permute-done((f32[64,64]{1,0:T(8,128)S(1)}, f32[64,64]{1,0:T(8,128)S(1)}, u32[]{:S(2)}, u32[]{:S(2)}) %collective-permute-start.5) | collective-permute-done | bytes 16416 | tf_op jit(solution)/shard_map/ppermute | solution.py:415
  28.3 1.7 %collective-permute-start.9 = (f32[64,64]{1,0:T(8,128)S(1)}, f32[64,64]{1,0:T(8,128)S(1)}, u32[]{:S(2)}, u32[]{:S(2)}) collective-permute-start(f32[64,64]{1,0:T(8,128)S(1)} %add_add_fusion.1), channel_id=1, source_target_pairs={{0,18},{1,19},{2,16},{3,17},{4,22},{5,23},{6,20},{7,21},{8,26},{9,... | collective-permute-start | bytes 49160 | tf_op jit(solution)/shard_map/ppermute | solution.py:415
  30.0 0.0 collective-permute-start.8
  30.1 1.8 %collective-permute-start.7 = (f32[64,64]{1,0:T(8,128)S(1)}, f32[64,64]{1,0:T(8,128)S(1)}, u32[]{:S(2)}, u32[]{:S(2)}) collective-permute-start(f32[64,64]{1,0:T(8,128)S(1)} %add_add_fusion.1), channel_id=1, source_target_pairs={{0,16},{1,17},{2,18},{3,19},{4,20},{5,21},{6,22},{7,23},{8,24},{9,... | collective-permute-start | bytes 49160 | tf_op jit(solution)/shard_map/ppermute | solution.py:415
  31.9 1.3 %collective-permute-done.9 = f32[64,64]{1,0:T(8,128)S(1)} collective-permute-done((f32[64,64]{1,0:T(8,128)S(1)}, f32[64,64]{1,0:T(8,128)S(1)}, u32[]{:S(2)}, u32[]{:S(2)}) %collective-permute-start.9) | collective-permute-done | bytes 16416 | tf_op jit(solution)/shard_map/ppermute | solution.py:415
  33.2 0.7 %collective-permute-done.8 = f32[64,64]{1,0:T(8,128)S(1)} collective-permute-done((f32[64,64]{1,0:T(8,128)S(1)}, f32[64,64]{1,0:T(8,128)S(1)}, u32[]{:S(2)}, u32[]{:S(2)}) %collective-permute-start.8) | collective-permute-done | bytes 16416 | tf_op jit(solution)/shard_map/ppermute | solution.py:415
  33.9 0.0 collective-permute-done.7
  34.0 3.1 %collective-permute-start.10 = (f32[64,64]{1,0:T(8,128)S(1)}, f32[64,64]{1,0:T(8,128)S(1)}, u32[]{:S(2)}, u32[]{:S(2)}) collective-permute-start(f32[64,64]{1,0:T(8,128)S(1)} %add_add_fusion), channel_id=1, source_target_pairs={{0,4},{1,5},{2,6},{3,7},{4,0},{5,1},{6,2},{7,3},{8,12},{9,13},{10,... | collective-permute-start | bytes 49160 | tf_op jit(solution)/shard_map/ppermute | solution.py:415
  37.1 2.0 %halves.1.panel = bf16[96,128,256]{2,1,0:T(8,128)(2,1)S(1)} custom-call(f32[60,24,8,128]{3,2,1,0:T(8,128)S(1)} %get-tuple-element.31.kept, f32[4,24,8,128]{3,2,1,0:T(8,128)S(1)} %get-tuple-element.34.snaps), custom_call_target="tpu_custom_call" | custom-call | tf_op jit(solution)/shard_map/halves/pallas_call | solution.py:493
  39.1 5.7 %factor_basis.1 = (f32[64,24,8,128]{3,2,1,0:T(8,128)}, f32[64,64]{1,0:T(8,128)}) custom-call(f32[64,64]{1,0:T(8,128)S(1)} %add.27.part, bf16[96,128,256]{2,1,0:T(8,128)(2,1)S(1)} %halves.1.panel), custom_call_target="tpu_custom_call" | custom-call | tf_op jit(solution)/shard_map/factor_basis/pallas_call | solution.py:502
  (8 shorter events, 0.0 us)
Async XLA Ops:
  1.7 7.7 %collective-permute-start = (f32[34,8,128]{2,1,0:T(8,128)S(1)}, f32[34,8,128]{2,1,0:T(8,128)S(1)}, u32[]{:S(2)}, u32[]{:S(2)}) collective-permute-start(f32[34,8,128]{2,1,0:T(8,128)S(1)} %get-tuple-element.23), channel_id=1, source_target_pairs={{0,1},{1,0},{2,3},{3,2},{4,5},{5,4},{6,7},{7,6},{8,9},{9,8},{10,11... | collective-permute-start | bytes 417800 | tf_op jit(solution)/shard_map/ppermute | solution.py:398
  4.7 4.7 %collective-permute-start.1 = (f32[34,8,128]{2,1,0:T(8,128)S(1)}, f32[34,8,128]{2,1,0:T(8,128)S(1)}, u32[]{:S(2)}, u32[]{:S(2)}) collective-permute-start(f32[34,8,128]{2,1,0:T(8,128)S(1)} %get-tuple-element.24), channel_id=1, source_target_pairs={{1,2},{2,1},{3,4},{4,3},{5,6},{6,5},{9,10},{10,9},{11,12},{12,11},... | collective-permute-start | bytes 417800 | tf_op jit(solution)/shard_map/ppermute | solution.py:397
  9.6 2.0 %collective-permute-start.2 = (f32[55,8,128]{2,1,0:T(8,128)S(1)}, f32[55,8,128]{2,1,0:T(8,128)S(1)}, u32[]{:S(2)}, u32[]{:S(2)}) collective-permute-start(f32[55,8,128]{2,1,0:T(8,128)S(1)} %get-tuple-element.29), channel_id=1, source_target_pairs={{0,8},{8,0},{16,24},{24,16},{1,9},{9,1},{17,25},{25,17},{2,10},{10... | collective-permute-start | bytes 675848 | tf_op jit(solution)/shard_map/ppermute | solution.py:398
  9.6 2.0 %collective-permute-start.3 = (f32[55,8,128]{2,1,0:T(8,128)S(1)}, f32[55,8,128]{2,1,0:T(8,128)S(1)}, u32[]{:S(2)}, u32[]{:S(2)}) collective-permute-start(f32[55,8,128]{2,1,0:T(8,128)S(1)} %get-tuple-element.30), channel_id=1, source_target_pairs={{8,16},{16,8},{9,17},{17,9},{10,18},{18,10},{11,19},{19,11},{12,20... | collective-permute-start | bytes 675848 | tf_op jit(solution)/shard_map/ppermute | solution.py:397
  14.7 11.3 %collective-permute-start.6 = (f32[64,64]{1,0:T(8,128)S(1)}, f32[64,64]{1,0:T(8,128)S(1)}, u32[]{:S(2)}, u32[]{:S(2)}) collective-permute-start(f32[64,64]{1,0:T(8,128)S(1)} %get-tuple-element.33), channel_id=1, source_target_pairs={{0,9},{1,8},{2,11},{3,10},{4,13},{5,12},{6,15},{7,14},{8,1},{9,0},... | collective-permute-start | bytes 49160 | tf_op jit(solution)/shard_map/ppermute | solution.py:415
  24.4 3.9 %collective-permute-start.5 = (f32[64,64]{1,0:T(8,128)S(1)}, f32[64,64]{1,0:T(8,128)S(1)}, u32[]{:S(2)}, u32[]{:S(2)}) collective-permute-start(f32[64,64]{1,0:T(8,128)S(1)} %get-tuple-element.33), channel_id=1, source_target_pairs={{0,1},{1,0},{2,3},{3,2},{4,5},{5,4},{6,7},{7,6},{8,9},{9,8},{10,11... | collective-permute-start | bytes 49160 | tf_op jit(solution)/shard_map/ppermute | solution.py:415
  24.4 3.9 %collective-permute-start.4 = (f32[64,64]{1,0:T(8,128)S(1)}, f32[64,64]{1,0:T(8,128)S(1)}, u32[]{:S(2)}, u32[]{:S(2)}) collective-permute-start(f32[64,64]{1,0:T(8,128)S(1)} %get-tuple-element.33), channel_id=1, source_target_pairs={{0,8},{1,9},{2,10},{3,11},{4,12},{5,13},{6,14},{7,15},{8,0},{9,1},... | collective-permute-start | bytes 49160 | tf_op jit(solution)/shard_map/ppermute | solution.py:415
  28.3 4.9 %collective-permute-start.9 = (f32[64,64]{1,0:T(8,128)S(1)}, f32[64,64]{1,0:T(8,128)S(1)}, u32[]{:S(2)}, u32[]{:S(2)}) collective-permute-start(f32[64,64]{1,0:T(8,128)S(1)} %add_add_fusion.1), channel_id=1, source_target_pairs={{0,18},{1,19},{2,16},{3,17},{4,22},{5,23},{6,20},{7,21},{8,26},{9,... | collective-permute-start | bytes 49160 | tf_op jit(solution)/shard_map/ppermute | solution.py:415
  30.0 3.9 %collective-permute-start.8 = (f32[64,64]{1,0:T(8,128)S(1)}, f32[64,64]{1,0:T(8,128)S(1)}, u32[]{:S(2)}, u32[]{:S(2)}) collective-permute-start(f32[64,64]{1,0:T(8,128)S(1)} %add_add_fusion.1), channel_id=1, source_target_pairs={{0,2},{1,3},{2,0},{3,1},{4,6},{5,7},{6,4},{7,5},{8,10},{9,11},{10,... | collective-permute-start | bytes 49160 | tf_op jit(solution)/shard_map/ppermute | solution.py:415
  30.1 3.9 %collective-permute-start.7 = (f32[64,64]{1,0:T(8,128)S(1)}, f32[64,64]{1,0:T(8,128)S(1)}, u32[]{:S(2)}, u32[]{:S(2)}) collective-permute-start(f32[64,64]{1,0:T(8,128)S(1)} %add_add_fusion.1), channel_id=1, source_target_pairs={{0,16},{1,17},{2,18},{3,19},{4,20},{5,21},{6,22},{7,23},{8,24},{9,... | collective-permute-start | bytes 49160 | tf_op jit(solution)/shard_map/ppermute | solution.py:415
  34.0 5.1 %collective-permute-start.10 = (f32[64,64]{1,0:T(8,128)S(1)}, f32[64,64]{1,0:T(8,128)S(1)}, u32[]{:S(2)}, u32[]{:S(2)}) collective-permute-start(f32[64,64]{1,0:T(8,128)S(1)} %add_add_fusion), channel_id=1, source_target_pairs={{0,4},{1,5},{2,6},{3,7},{4,0},{5,1},{6,2},{7,3},{8,12},{9,13},{10,... | collective-permute-start | bytes 49160 | tf_op jit(solution)/shard_map/ppermute | solution.py:415

commit v4 on v3

--- a/solution.py
+++ b/solution.py
@@ -137,7 +137,7 @@
     return jnp.where(sub == 0, turn(second, 1), turn(first, 1))
 
 
-def steps_kernel(v, nu, f, rv, rnu, rf, recv_a, recv_b, kept, square_a, square_b, snaps, final, part, ext, enu, ef, coef):
+def steps_kernel(v, nu, f, rv, rnu, rf, recv_a, recv_b, kept, square_a, square_b, snaps, final, part, ext, enu, ef, coef, sem):
     comps, size_x = v.shape[0], v.shape[1]
     steps = f.shape[0]
     wide = 2 * size_x
@@ -224,8 +224,9 @@
                     ext[dst, c, x, tile] = new
                 if tile == 0 and x < size_x:
                     snaps[t, c * size_x + x] = new
-                    if t == steps - 1:
-                        final[c, x] = new
+
+    last = pltpu.make_async_copy(snaps.at[steps - 1], final, sem.at[0])
+    last.start()
 
     rows = kept.shape[0]
     slabs = kept.shape[1]
@@ -255,6 +256,7 @@
                 entry = jnp.where(row_at == rows + t, 0.5 * entry, entry)
             block = jnp.where(column == rows + t, entry, block)
         part[pl.ds(k0, 8), :] = block * scale
+    last.wait()
 
 
 def split(p):
@@ -301,31 +303,31 @@
     for i in range(sems.shape[0]):
         at = (slice(None), pl.ds(i * step, step))
         copies.append(pltpu.make_async_copy(kept_in.at[at], kept.at[at], sems.at[i]))
-    for copy in copies:
+    ahead = 3
+    for copy in copies[:ahead]:
         copy.start()
+
+    def arrive(i):
+        copies[i].wait()
+        if i + ahead < len(copies):
+            copies[i + ahead].start()
 
     def ready(s):
         if s % step == 0:
-            copies[s // step].wait()
+            arrive(s // step)
 
     out[...] = square_of(kept, range(count), n, ready)
     for i in range(-(-count // step), len(copies)):
-        copies[i].wait()
+        arrive(i)
 
 
 def square_rest_kernel(kept, out, *, n, count):
     out[...] = square_of(kept, range(count, kept.shape[1]), n)
 
 
-def factor_of(gram):
-    n = gram.shape[0]
-    count = n // 8
-    sub = sub_index()
-    row_at = lax.broadcasted_iota(jnp.int32, (n, n), 0)
-    col_at = lax.broadcasted_iota(jnp.int32, (n, n), 1)
-    eye = jnp.where(row_at == col_at, 1.0, 0.0).astype(F32)
-    whole = jnp.concatenate([gram, eye], 1)
-    w = [whole[8 * c : 8 * c + 8] for c in range(count)]
+def eliminate(w, b):
+    sub = sub_index()
+    count = len(w)
 
     def spread(tile, j):
         return jnp.broadcast_to(tile[:, j : j + 1], tile.shape)
@@ -333,23 +335,21 @@
     def pick(tile, q):
         return jnp.broadcast_to(tile[q : q + 1, :], tile.shape)
 
-    for b in range(count):
-        cols = {c: [spread(w[c], 8 * b + q) for q in range(8)] for c in range(b, count)}
-        pivots = jnp.ones(w[b].shape, F32)
-        for q in range(8):
-            head = [pick(cols[b][r], q) for r in range(q, 8)]
-            inverse = 1.0 / head[0]
-            pivots = jnp.where(sub == q, head[0], pivots)
-            line = pick(w[b], q)
-            for c in range(b, count):
-                ratio = cols[c][q] * inverse
-                if c == b:
-                    ratio = jnp.where(sub > q, ratio, 0.0)
-                w[c] = w[c] - ratio * line
-                for r in range(q + 1, 8):
-                    cols[c][r] = cols[c][r] - ratio * head[r - q]
-        w[b] = w[b] * lax.rsqrt(pivots)
-    return jnp.concatenate(w, 0)
+    cols = {c: [spread(w[c], 8 * b + q) for q in range(8)] for c in range(b, count)}
+    pivots = jnp.ones(w[b].shape, F32)
+    for q in range(8):
+        head = [pick(cols[b][r], q) for r in range(q, 8)]
+        inverse = 1.0 / head[0]
+        pivots = jnp.where(sub == q, head[0], pivots)
+        line = pick(w[b], q)
+        for c in range(b, count):
+            ratio = cols[c][q] * inverse
+            if c == b:
+                ratio = jnp.where(sub > q, ratio, 0.0)
+            w[c] = w[c] - ratio * line
+            for r in range(q + 1, 8):
+                cols[c][r] = cols[c][r] - ratio * head[r - q]
+    w[b] = w[b] * lax.rsqrt(pivots)
 
 
 def halves_kernel(kept, snaps, panel):
@@ -361,31 +361,56 @@
             panel[4 * s + i, :n], panel[4 * s + i, n:] = high, low
 
 
-def basis_kernel(part, panel, basis, factor, out, sems):
+def basis_kernel(part, panel, basis, factor, out, upper, sems, sem):
     n = part.shape[0]
+    mid = n // 2
     slabs = panel.shape[0] // 4
-    block = slabs // sems.shape[0]
+    batches = sems.shape[1]
+    block = slabs // batches
     m = part[...]
-    w = factor_of(m + m.T)
     row_at = lax.broadcasted_iota(jnp.int32, (n, n), 0)
     col_at = lax.broadcasted_iota(jnp.int32, (n, n), 1)
-    factor[...] = jnp.where(row_at <= col_at, w[:, :n], 0.0)
-    high, low = split(w[:, n:])
-    lhs = jnp.concatenate([high, high, low], 1)
+    eye = jnp.where(row_at == col_at, 1.0, 0.0).astype(F32)
+    whole = jnp.concatenate([m + m.T, eye], 1)
+    w = [whole[c : c + 8] for c in range(0, n, 8)]
     copies = []
-    for s in range(slabs):
-        pieces = []
-        for i in range(4):
-            both = panel[4 * s + i]
-            rhs = jnp.concatenate([both, both[:n]], 0)
-            r = lax.dot_general(lhs, rhs, (((1,), (0,)), ((), ())), preferred_element_type=F32)
-            pieces += [r[:, :128], r[:, 128:]]
-        out[:, s] = from_rows(pieces)
-        if (s + 1) % block == 0:
-            at = (slice(None), pl.ds(s + 1 - block, block))
-            copy = pltpu.make_async_copy(out.at[at], basis.at[at], sems.at[s // block])
-            copy.start()
-            copies.append(copy)
+
+    def rows_of(first, last, between):
+        inverse = jnp.concatenate(w[first // 8 : last // 8], 0)[:, n : n + last]
+        high, low = split(inverse)
+        top = jnp.concatenate([high, high], 1)
+        lhs = jnp.concatenate([top, jnp.concatenate([low, jnp.zeros_like(low)], 1)], 0)
+        for s in range(slabs):
+            pieces = []
+            for i in range(4):
+                high, low = panel[4 * s + i, :last], panel[4 * s + i, n : n + last]
+                rhs = jnp.concatenate([high, low], 0)
+                r = lax.dot_general(lhs, rhs, (((1,), (0,)), ((), ())), preferred_element_type=F32)
+                r = r[: last - first] + r[last - first :]
+                pieces += [r[:, :128], r[:, 128:]]
+            out[first:last, s] = from_rows(pieces)
+            between(s)
+            if (s + 1) % block == 0:
+                at = (pl.ds(first, last - first), pl.ds(s + 1 - block, block))
+                sem = sems.at[0 if first == 0 else 1, s // block]
+                copy = pltpu.make_async_copy(out.at[at], basis.at[at], sem)
+                copy.start()
+                copies.append(copy)
+
+    half = mid // 8
+    for b in range(half):
+        eliminate(w, b)
+    pace = slabs // half
+
+    def go_on(s):
+        if (s + 1) % pace == 0 and (s + 1) // pace <= half:
+            eliminate(w, half + (s + 1) // pace - 1)
+
+    rows_of(0, mid, go_on)
+    upper[...] = jnp.where(row_at <= col_at, jnp.concatenate(w, 0)[:, :n], 0.0)
+    copies.append(pltpu.make_async_copy(upper, factor, sem.at[0]))
+    copies[-1].start()
+    rows_of(mid, n, lambda s: None)
     for copy in copies:
         copy.wait()
 
@@ -478,14 +503,15 @@
     )(kept)
     snaps, final, part = call(
         steps_kernel,
-        out_shape=(struct(steps, slabs, 8, 128), struct(*velocity.shape), struct(n, n)),
+        out_shape=(struct(steps, slabs, 8, 128), struct(slabs, 8, 128), struct(n, n)),
         in_specs=[VMEM] * 11,
-        out_specs=(VMEM,) * 3,
+        out_specs=(VMEM, HBM, VMEM),
         scratch_shapes=[
             pltpu.VMEM((2, comps, 2 * size_x, 2, 8, 128), F32),
             pltpu.VMEM((2 * size_x, 2, 8, 128), F32),
             pltpu.VMEM((3, comps, 2 * size_x, 2, 8, 128), F32),
             pltpu.VMEM((2 * size_x, 2, 7, 8, 128), F32),
+            pltpu.SemaphoreType.DMA((1,)),
         ],
         compiler_params=limit(12),
         name="steps",
@@ -503,12 +529,17 @@
         basis_kernel,
         out_shape=(struct(n, slabs, 8, 128), struct(n, n)),
         in_specs=[VMEM] * 2,
-        out_specs=(HBM, VMEM),
-        scratch_shapes=[pltpu.VMEM((n, slabs, 8, 128), F32), pltpu.SemaphoreType.DMA((slabs // 3,))],
+        out_specs=(HBM, HBM),
+        scratch_shapes=[
+            pltpu.VMEM((n, slabs, 8, 128), F32),
+            pltpu.VMEM((n, n), F32),
+            pltpu.SemaphoreType.DMA((2, slabs // 3)),
+            pltpu.SemaphoreType.DMA((1,)),
+        ],
         compiler_params=limit(16),
         name="factor_basis",
     )(part, panel)
-    return final, basis.reshape((n,) + velocity.shape), factor
+    return final.reshape(velocity.shape), basis.reshape((n,) + velocity.shape), factor
 
 
 def solution(mesh):

time: 45.1 us -> 44 us (0.976)
  Pallas kernels: 17.1 us -> 16 us
    pallas_call x1, Pallas kernels: 5.67 us -> 4.59 us  [local(): call(basis_kernel, out_shape=(struct(n, slabs, 8, 128), struct(n, n)), in...]
where the time goes in v4:
time: 44 us; the launch traced here: 43.8 us
  starting transfers between devices  21.1 us (48%)
  Pallas kernels  16 us (36%)
  waiting for transfers between devices  5.82 us (13%)
  between operations  0.75 us (2%)
    ppermute x7, starting transfers between devices, sum_over(): lax.ppermute(value, (major, minor), [(i, i ^ m) for i in range(count)])  16.7 us
    ppermute x7, waiting for transfers between devices, sum_over(): lax.ppermute(value, (major, minor), [(i, i ^ m) for i in range(count)])  5.81 us
    pallas_call x1, Pallas kernels, local(): call(basis_kernel, out_shape=(struct(n, slabs, 8, 128), struct(n, n)), in...  4.59 us
    pallas_call x1, Pallas kernels, local(): call(functools.partial(square_first_kernel, n=n, count=first), out_shape=...  4.03 us
    pallas_call x1, Pallas kernels, local(): call(steps_kernel, out_shape=(struct(steps, slabs, 8, 128), struct(slabs,...  3.09 us
    ppermute x2, starting transfers between devices, pair_exchange(): return (lax.ppermute(first, axis, near), distant)  3.07 us
    pallas_call x1, Pallas kernels, local(): call(halves_kernel, out_shape=jax.ShapeDtypeStruct((4 * slabs, 2 * n, 256...  2.05 us
    ppermute x2, starting transfers between devices, pair_exchange(): distant = lax.ppermute(second, axis, far)  1.33 us
  transfers between devices with their start and end apart: 11, of which 4 were waited for; matrix products, arithmetic and copies ran while one was open for 0% of the time, Pallas kernels for 16%

profile of v4, /device:TPU:0, one launch (start us, length us, event | category | flops | bytes accessed | tf_op | source)
XLA Modules:
  0.0 43.8 jit_solution(7095165011293323315)
XLA Ops:
  0.6 1.1 %pack_y.1 = (f32[3,8,8,128]{3,2,1,0:T(8,128)S(1)}, f32[8,8,128]{2,1,0:T(8,128)S(1)}, f32[4,3,8,8,128]{4,3,2,1,0:T(8,128)S(1)}, f32[34,8,128]{2,1,0:T(8,128)S(1)}, f32[34,8,128]{2,1,0:T(8,128)S(1)}) custom-call(f32[3,8,8,128]{3,2,1,0:T(8,128)} %v_in.1, f32[8,8,128]{2,1,0:T(8,128)} %nu_in.1, f32[4,3,8,8,128]{4,3,2,1,0:T(8,128)} %f_in.1), custom_call_target="tpu_custom_call" | custom-call | tf_op jit(solution)/shard_map/pack_y/pallas_call | solution.py:453
  1.7 3.0 %collective-permute-start = (f32[34,8,128]{2,1,0:T(8,128)S(1)}, f32[34,8,128]{2,1,0:T(8,128)S(1)}, u32[]{:S(2)}, u32[]{:S(2)}) collective-permute-start(f32[34,8,128]{2,1,0:T(8,128)S(1)} %get-tuple-element.23), channel_id=1, source_target_pairs={{0,1},{1,0},{2,3},{3,2},{4,5},{5,4},{6,7},{7,6},{8,9},{9,8},{10,11... | collective-permute-start | bytes 417800 | tf_op jit(solution)/shard_map/ppermute | solution.py:423
  4.7 0.7 %collective-permute-start.1 = (f32[34,8,128]{2,1,0:T(8,128)S(1)}, f32[34,8,128]{2,1,0:T(8,128)S(1)}, u32[]{:S(2)}, u32[]{:S(2)}) collective-permute-start(f32[34,8,128]{2,1,0:T(8,128)S(1)} %get-tuple-element.24), channel_id=1, source_target_pairs={{1,2},{2,1},{3,4},{4,3},{5,6},{6,5},{9,10},{10,9},{11,12},{12,11},... | collective-permute-start | bytes 417800 | tf_op jit(solution)/shard_map/ppermute | solution.py:422
  5.4 4.0 %gram_first.1 = (f32[60,24,8,128]{3,2,1,0:T(8,128)S(1)}, f32[64,128]{1,0:T(8,128)S(1)}) custom-call(f32[60,24,8,128]{3,2,1,0:T(8,128)} %bitcast.3), custom_call_target="tpu_custom_call" | custom-call | tf_op jit(solution)/shard_map/gram_first/pallas_call | solution.py:470
  9.5 0.1 pack_x.1
  9.6 0.1 collective-permute-start.2
  9.6 0.7 %collective-permute-start.3 = (f32[55,8,128]{2,1,0:T(8,128)S(1)}, f32[55,8,128]{2,1,0:T(8,128)S(1)}, u32[]{:S(2)}, u32[]{:S(2)}) collective-permute-start(f32[55,8,128]{2,1,0:T(8,128)S(1)} %get-tuple-element.30), channel_id=1, source_target_pairs={{8,16},{16,8},{9,17},{17,9},{10,18},{18,10},{11,19},{19,11},{12,20... | collective-permute-start | bytes 675848 | tf_op jit(solution)/shard_map/ppermute | solution.py:422
  10.3 1.1 %gram_rest.1.square_b = f32[64,128]{1,0:T(8,128)S(1)} custom-call(f32[60,24,8,128]{3,2,1,0:T(8,128)S(1)} %get-tuple-element.31.kept), custom_call_target="tpu_custom_call" | custom-call | tf_op jit(solution)/shard_map/gram_rest/pallas_call | solution.py:496
  11.4 0.0 collective-permute-done.2.recv_a
  11.4 3.1 %steps.1 = (f32[4,24,8,128]{3,2,1,0:T(8,128)S(1)}, f32[24,8,128]{2,1,0:T(8,128)}, f32[64,64]{1,0:T(8,128)S(1)}) custom-call(f32[3,8,8,128]{3,2,1,0:T(8,128)S(1)} %get-tuple-element.20.v, f32[8,8,128]{2,1,0:T(8,128)S(1)} %get-tuple-element.21.nu, f32[4,3,8,8,128]{4,3,2,1,0:T(8,128)S(1)} %get-tuple-element.22.f, f32[3,8,8,128]{3,2,1,0:T(8,128)S(1)} %get-tuple-element.26.rv, ...), custom_call_target="tpu_custom_call" | custom-call | tf_op jit(solution)/shard_map/steps/pallas_call | solution.py:504
  14.5 9.9 %collective-permute-start.6 = (f32[64,64]{1,0:T(8,128)S(1)}, f32[64,64]{1,0:T(8,128)S(1)}, u32[]{:S(2)}, u32[]{:S(2)}) collective-permute-start(f32[64,64]{1,0:T(8,128)S(1)} %get-tuple-element.33), channel_id=1, source_target_pairs={{0,9},{1,8},{2,11},{3,10},{4,13},{5,12},{6,15},{7,14},{8,1},{9,0},... | collective-permute-start | bytes 49160 | tf_op jit(solution)/shard_map/ppermute | solution.py:440
  24.5 0.0 collective-permute-start.5
  24.5 0.2 collective-permute-start.4
  24.7 1.4 %collective-permute-done.6 = f32[64,64]{1,0:T(8,128)S(1)} collective-permute-done((f32[64,64]{1,0:T(8,128)S(1)}, f32[64,64]{1,0:T(8,128)S(1)}, u32[]{:S(2)}, u32[]{:S(2)}) %collective-permute-start.6) | collective-permute-done | bytes 16416 | tf_op jit(solution)/shard_map/ppermute | solution.py:440
  26.1 2.3 %collective-permute-done.5 = f32[64,64]{1,0:T(8,128)S(1)} collective-permute-done((f32[64,64]{1,0:T(8,128)S(1)}, f32[64,64]{1,0:T(8,128)S(1)}, u32[]{:S(2)}, u32[]{:S(2)}) %collective-permute-start.5) | collective-permute-done | bytes 16416 | tf_op jit(solution)/shard_map/ppermute | solution.py:440
  28.4 1.7 %collective-permute-start.9 = (f32[64,64]{1,0:T(8,128)S(1)}, f32[64,64]{1,0:T(8,128)S(1)}, u32[]{:S(2)}, u32[]{:S(2)}) collective-permute-start(f32[64,64]{1,0:T(8,128)S(1)} %add_add_fusion.1), channel_id=1, source_target_pairs={{0,18},{1,19},{2,16},{3,17},{4,22},{5,23},{6,20},{7,21},{8,26},{9,... | collective-permute-start | bytes 49160 | tf_op jit(solution)/shard_map/ppermute | solution.py:440
  30.1 0.0 collective-permute-start.8
  30.1 1.8 %collective-permute-start.7 = (f32[64,64]{1,0:T(8,128)S(1)}, f32[64,64]{1,0:T(8,128)S(1)}, u32[]{:S(2)}, u32[]{:S(2)}) collective-permute-start(f32[64,64]{1,0:T(8,128)S(1)} %add_add_fusion.1), channel_id=1, source_target_pairs={{0,16},{1,17},{2,18},{3,19},{4,20},{5,21},{6,22},{7,23},{8,24},{9,... | collective-permute-start | bytes 49160 | tf_op jit(solution)/shard_map/ppermute | solution.py:440
  32.0 1.3 %collective-permute-done.9 = f32[64,64]{1,0:T(8,128)S(1)} collective-permute-done((f32[64,64]{1,0:T(8,128)S(1)}, f32[64,64]{1,0:T(8,128)S(1)}, u32[]{:S(2)}, u32[]{:S(2)}) %collective-permute-start.9) | collective-permute-done | bytes 16416 | tf_op jit(solution)/shard_map/ppermute | solution.py:440
  33.3 0.7 %collective-permute-done.8 = f32[64,64]{1,0:T(8,128)S(1)} collective-permute-done((f32[64,64]{1,0:T(8,128)S(1)}, f32[64,64]{1,0:T(8,128)S(1)}, u32[]{:S(2)}, u32[]{:S(2)}) %collective-permute-start.8) | collective-permute-done | bytes 16416 | tf_op jit(solution)/shard_map/ppermute | solution.py:440
  34.0 0.0 collective-permute-done.7
  34.0 3.1 %collective-permute-start.10 = (f32[64,64]{1,0:T(8,128)S(1)}, f32[64,64]{1,0:T(8,128)S(1)}, u32[]{:S(2)}, u32[]{:S(2)}) collective-permute-start(f32[64,64]{1,0:T(8,128)S(1)} %add_add_fusion), channel_id=1, source_target_pairs={{0,4},{1,5},{2,6},{3,7},{4,0},{5,1},{6,2},{7,3},{8,12},{9,13},{10,... | collective-permute-start | bytes 49160 | tf_op jit(solution)/shard_map/ppermute | solution.py:440
  37.1 2.0 %halves.1.panel = bf16[96,128,256]{2,1,0:T(8,128)(2,1)S(1)} custom-call(f32[60,24,8,128]{3,2,1,0:T(8,128)S(1)} %get-tuple-element.31.kept, f32[4,24,8,128]{3,2,1,0:T(8,128)S(1)} %get-tuple-element.34.snaps), custom_call_target="tpu_custom_call" | custom-call | tf_op jit(solution)/shard_map/halves/pallas_call | solution.py:519
  39.2 4.6 %factor_basis.1 = (f32[64,24,8,128]{3,2,1,0:T(8,128)}, f32[64,64]{1,0:T(8,128)}) custom-call(f32[64,64]{1,0:T(8,128)S(1)} %add.27.part, bf16[96,128,256]{2,1,0:T(8,128)(2,1)S(1)} %halves.1.panel), custom_call_target="tpu_custom_call" | custom-call | tf_op jit(solution)/shard_map/factor_basis/pallas_call | solution.py:528
  (8 shorter events, 0.0 us)
Async XLA Ops:
  1.7 7.7 %collective-permute-start = (f32[34,8,128]{2,1,0:T(8,128)S(1)}, f32[34,8,128]{2,1,0:T(8,128)S(1)}, u32[]{:S(2)}, u32[]{:S(2)}) collective-permute-start(f32[34,8,128]{2,1,0:T(8,128)S(1)} %get-tuple-element.23), channel_id=1, source_target_pairs={{0,1},{1,0},{2,3},{3,2},{4,5},{5,4},{6,7},{7,6},{8,9},{9,8},{10,11... | collective-permute-start | bytes 417800 | tf_op jit(solution)/shard_map/ppermute | solution.py:423
  4.7 4.7 %collective-permute-start.1 = (f32[34,8,128]{2,1,0:T(8,128)S(1)}, f32[34,8,128]{2,1,0:T(8,128)S(1)}, u32[]{:S(2)}, u32[]{:S(2)}) collective-permute-start(f32[34,8,128]{2,1,0:T(8,128)S(1)} %get-tuple-element.24), channel_id=1, source_target_pairs={{1,2},{2,1},{3,4},{4,3},{5,6},{6,5},{9,10},{10,9},{11,12},{12,11},... | collective-permute-start | bytes 417800 | tf_op jit(solution)/shard_map/ppermute | solution.py:422
  9.6 1.9 %collective-permute-start.2 = (f32[55,8,128]{2,1,0:T(8,128)S(1)}, f32[55,8,128]{2,1,0:T(8,128)S(1)}, u32[]{:S(2)}, u32[]{:S(2)}) collective-permute-start(f32[55,8,128]{2,1,0:T(8,128)S(1)} %get-tuple-element.29), channel_id=1, source_target_pairs={{0,8},{8,0},{16,24},{24,16},{1,9},{9,1},{17,25},{25,17},{2,10},{10... | collective-permute-start | bytes 675848 | tf_op jit(solution)/shard_map/ppermute | solution.py:423
  9.6 1.8 %collective-permute-start.3 = (f32[55,8,128]{2,1,0:T(8,128)S(1)}, f32[55,8,128]{2,1,0:T(8,128)S(1)}, u32[]{:S(2)}, u32[]{:S(2)}) collective-permute-start(f32[55,8,128]{2,1,0:T(8,128)S(1)} %get-tuple-element.30), channel_id=1, source_target_pairs={{8,16},{16,8},{9,17},{17,9},{10,18},{18,10},{11,19},{19,11},{12,20... | collective-permute-start | bytes 675848 | tf_op jit(solution)/shard_map/ppermute | solution.py:422
  14.5 11.5 %collective-permute-start.6 = (f32[64,64]{1,0:T(8,128)S(1)}, f32[64,64]{1,0:T(8,128)S(1)}, u32[]{:S(2)}, u32[]{:S(2)}) collective-permute-start(f32[64,64]{1,0:T(8,128)S(1)} %get-tuple-element.33), channel_id=1, source_target_pairs={{0,9},{1,8},{2,11},{3,10},{4,13},{5,12},{6,15},{7,14},{8,1},{9,0},... | collective-permute-start | bytes 49160 | tf_op jit(solution)/shard_map/ppermute | solution.py:440
  24.5 3.9 %collective-permute-start.5 = (f32[64,64]{1,0:T(8,128)S(1)}, f32[64,64]{1,0:T(8,128)S(1)}, u32[]{:S(2)}, u32[]{:S(2)}) collective-permute-start(f32[64,64]{1,0:T(8,128)S(1)} %get-tuple-element.33), channel_id=1, source_target_pairs={{0,1},{1,0},{2,3},{3,2},{4,5},{5,4},{6,7},{7,6},{8,9},{9,8},{10,11... | collective-permute-start | bytes 49160 | tf_op jit(solution)/shard_map/ppermute | solution.py:440
  24.5 3.9 %collective-permute-start.4 = (f32[64,64]{1,0:T(8,128)S(1)}, f32[64,64]{1,0:T(8,128)S(1)}, u32[]{:S(2)}, u32[]{:S(2)}) collective-permute-start(f32[64,64]{1,0:T(8,128)S(1)} %get-tuple-element.33), channel_id=1, source_target_pairs={{0,8},{1,9},{2,10},{3,11},{4,12},{5,13},{6,14},{7,15},{8,0},{9,1},... | collective-permute-start | bytes 49160 | tf_op jit(solution)/shard_map/ppermute | solution.py:440
  28.4 4.9 %collective-permute-start.9 = (f32[64,64]{1,0:T(8,128)S(1)}, f32[64,64]{1,0:T(8,128)S(1)}, u32[]{:S(2)}, u32[]{:S(2)}) collective-permute-start(f32[64,64]{1,0:T(8,128)S(1)} %add_add_fusion.1), channel_id=1, source_target_pairs={{0,18},{1,19},{2,16},{3,17},{4,22},{5,23},{6,20},{7,21},{8,26},{9,... | collective-permute-start | bytes 49160 | tf_op jit(solution)/shard_map/ppermute | solution.py:440
  30.1 3.9 %collective-permute-start.8 = (f32[64,64]{1,0:T(8,128)S(1)}, f32[64,64]{1,0:T(8,128)S(1)}, u32[]{:S(2)}, u32[]{:S(2)}) collective-permute-start(f32[64,64]{1,0:T(8,128)S(1)} %add_add_fusion.1), channel_id=1, source_target_pairs={{0,2},{1,3},{2,0},{3,1},{4,6},{5,7},{6,4},{7,5},{8,10},{9,11},{10,... | collective-permute-start | bytes 49160 | tf_op jit(solution)/shard_map/ppermute | solution.py:440
  30.1 3.9 %collective-permute-start.7 = (f32[64,64]{1,0:T(8,128)S(1)}, f32[64,64]{1,0:T(8,128)S(1)}, u32[]{:S(2)}, u32[]{:S(2)}) collective-permute-start(f32[64,64]{1,0:T(8,128)S(1)} %add_add_fusion.1), channel_id=1, source_target_pairs={{0,16},{1,17},{2,18},{3,19},{4,20},{5,21},{6,22},{7,23},{8,24},{9,... | collective-permute-start | bytes 49160 | tf_op jit(solution)/shard_map/ppermute | solution.py:440
  34.0 5.1 %collective-permute-start.10 = (f32[64,64]{1,0:T(8,128)S(1)}, f32[64,64]{1,0:T(8,128)S(1)}, u32[]{:S(2)}, u32[]{:S(2)}) collective-permute-start(f32[64,64]{1,0:T(8,128)S(1)} %add_add_fusion), channel_id=1, source_target_pairs={{0,4},{1,5},{2,6},{3,7},{4,0},{5,1},{6,2},{7,3},{8,12},{9,13},{10,... | collective-permute-start | bytes 49160 | tf_op jit(solution)/shard_map/ppermute | solution.py:440

commit v5 on v4

--- a/solution.py
+++ b/solution.py
@@ -81,11 +81,26 @@
     own += [("nu", 0, d) for d in range(1, 5)]
     for t in range(3):
         own += [(t, c, d) for c in range(comps) for d in range(1, 4 - t)]
-    rim = [("v", c, d) for c in range(comps) for d in range(1, 4)]
-    rim += [("nu", 0, d) for d in range(1, 4)]
-    for t in range(2):
-        rim += [(t, c, d) for c in range(comps) for d in range(1, 3 - t)]
+    fields = [("v", c) for c in range(comps)] + [("nu", 0)]
+    rim = [((name, c, 1), (name, c, 3), 3) for name, c in fields]
+    four = [(name, c, 2) for name, c in fields] + [(0, c, 1) for c in range(comps)]
+    four += [(0, c, 2) for c in range(comps)] + [(1, c, 1) for c in range(comps)]
+    rim += [(one, two, 2) for one, two in zip(four[0::2], four[1::2])]
+    rim += [(one, None, 0) for one in four[len(four) - len(four) % 2 :]]
     return own, rim
+
+
+def merge(first, second, shift):
+    sub = sub_index()
+    if shift == 3:
+        above, below = sub == 3, sub == 4
+    else:
+        above, below = (sub >= 2) & (sub < 4), (sub >= 4) & (sub < 6)
+    return jnp.where(above, turn(second, shift), jnp.where(below, turn(second, 8 - shift), first))
+
+
+def unmerge(tile, shift):
+    return jnp.where(sub_index() < 4, turn(tile, 8 - shift), turn(tile, shift))
 
 
 def pack_x_kernel(v, nu, f, recv_a, recv_b, after, rv, rnu, rf, send_a, send_b):
@@ -113,21 +128,23 @@
         rf[1, d, w] = jnp.where(sub < 4, turn(item, 6), turn(item, 2))
         at += 1
     own, rim = x_items(comps)
-    at = 0
-    for group, (gv, gnu, gf) in ((own, (v, nu, f)), (rim, (rv, rnu, rf))):
-        for name, c, d in group:
-            high, low = size_x - d, d - 1
-            for ref, x in (
-                (send_a, jnp.where(even_x, high, low)),
-                (send_b, jnp.where(even_x, low, high)),
-            ):
-                if name == "v":
-                    ref[at] = gv[c, x]
-                elif name == "nu":
-                    ref[at] = gnu[x]
-                else:
-                    ref[at] = gf[name, c, x]
-            at += 1
+
+    def take(source, item, upward):
+        name, c, d = item
+        field, viscosity, push = source
+        x = jnp.where(upward, size_x - d, d - 1)
+        if name == "v":
+            return field[c, x]
+        return viscosity[x] if name == "nu" else push[name, c, x]
+
+    for send, upward in ((send_a, even_x), (send_b, jnp.logical_not(even_x))):
+        for at, item in enumerate(own):
+            send[at] = take((v, nu, f), item, upward)
+        for at, (one, two, shift) in enumerate(rim):
+            tile = take((rv, rnu, rf), one, upward)
+            if two is not None:
+                tile = merge(tile, take((rv, rnu, rf), two, upward), shift)
+            send[len(own) + at] = tile
 
 
 def beside_y(first, second, up):
@@ -157,21 +174,25 @@
             for t in range(3):
                 ef[t, c, x, 0], ef[t, c, x, 1] = f[t, c, x], rf[t, c, x]
     own, rim = x_items(comps)
-    at = 0
-    for tile, group in enumerate((own, rim)):
-        for name, c, d in group:
-            high, low = size_x - 1 + d, wide - d
-            for ref, x in (
-                (recv_a, jnp.where(even, high, low)),
-                (recv_b, jnp.where(even, low, high)),
-            ):
-                if name == "v":
-                    ext[0, c, x, tile] = ref[at]
-                elif name == "nu":
-                    enu[x, tile] = ref[at]
-                else:
-                    ef[name, c, x, tile] = ref[at]
-            at += 1
+
+    def put(item, tile, above, value):
+        name, c, d = item
+        x = jnp.where(above, size_x - 1 + d, wide - d)
+        if name == "v":
+            ext[0, c, x, tile] = value
+        elif name == "nu":
+            enu[x, tile] = value
+        else:
+            ef[name, c, x, tile] = value
+
+    for recv, above in ((recv_a, even), (recv_b, jnp.logical_not(even))):
+        for at, item in enumerate(own):
+            put(item, 0, above, recv[at])
+        for at, (first, second, shift) in enumerate(rim):
+            value = recv[len(own) + at]
+            put(first, 1, above, value)
+            if second is not None:
+                put(second, 1, above, unmerge(value, shift))
 
     def reach(x):
         return 0 if x < size_x else min(x - size_x + 1, wide - x)

time: 44 us -> 43.5 us (0.989)
  no operation moved by 1% of the time
where the time goes in v5:
time: 43.5 us; the launch traced here: 43.4 us
  starting transfers between devices  20.7 us (48%)
  Pallas kernels  16.1 us (37%)
  waiting for transfers between devices  5.82 us (13%)
  between operations  0.76 us (2%)
    ppermute x7, starting transfers between devices, sum_over(): lax.ppermute(value, (major, minor), [(i, i ^ m) for i in range(count)])  16.3 us
    ppermute x7, waiting for transfers between devices, sum_over(): lax.ppermute(value, (major, minor), [(i, i ^ m) for i in range(count)])  5.81 us
    pallas_call x1, Pallas kernels, local(): call(basis_kernel, out_shape=(struct(n, slabs, 8, 128), struct(n, n)), in...  4.6 us
    pallas_call x1, Pallas kernels, local(): call(functools.partial(square_first_kernel, n=n, count=first), out_shape=...  4.03 us
    pallas_call x1, Pallas kernels, local(): call(steps_kernel, out_shape=(struct(steps, slabs, 8, 128), struct(slabs,...  3.11 us
    ppermute x2, starting transfers between devices, pair_exchange(): return (lax.ppermute(first, axis, near), distant)  3.07 us
    pallas_call x1, Pallas kernels, local(): call(halves_kernel, out_shape=jax.ShapeDtypeStruct((4 * slabs, 2 * n, 256...  2.05 us
    ppermute x2, starting transfers between devices, pair_exchange(): distant = lax.ppermute(second, axis, far)  1.33 us
  transfers between devices with their start and end apart: 11, of which 4 were waited for; matrix products, arithmetic and copies ran while one was open for 0% of the time, Pallas kernels for 16%

profile of v5, /device:TPU:0, one launch (start us, length us, event | category | flops | bytes accessed | tf_op | source)
XLA Modules:
  0.0 43.4 jit_solution(9146539960816561409)
XLA Ops:
  0.6 1.1 %pack_y.1 = (f32[3,8,8,128]{3,2,1,0:T(8,128)S(1)}, f32[8,8,128]{2,1,0:T(8,128)S(1)}, f32[4,3,8,8,128]{4,3,2,1,0:T(8,128)S(1)}, f32[34,8,128]{2,1,0:T(8,128)S(1)}, f32[34,8,128]{2,1,0:T(8,128)S(1)}) custom-call(f32[3,8,8,128]{3,2,1,0:T(8,128)} %v_in.1, f32[8,8,128]{2,1,0:T(8,128)} %nu_in.1, f32[4,3,8,8,128]{4,3,2,1,0:T(8,128)} %f_in.1), custom_call_target="tpu_custom_call" | custom-call | tf_op jit(solution)/shard_map/pack_y/pallas_call | solution.py:474
  1.7 3.0 %collective-permute-start = (f32[34,8,128]{2,1,0:T(8,128)S(1)}, f32[34,8,128]{2,1,0:T(8,128)S(1)}, u32[]{:S(2)}, u32[]{:S(2)}) collective-permute-start(f32[34,8,128]{2,1,0:T(8,128)S(1)} %get-tuple-element.23), channel_id=1, source_target_pairs={{0,1},{1,0},{2,3},{3,2},{4,5},{5,4},{6,7},{7,6},{8,9},{9,8},{10,11... | collective-permute-start | bytes 417800 | tf_op jit(solution)/shard_map/ppermute | solution.py:444
  4.7 0.7 %collective-permute-start.1 = (f32[34,8,128]{2,1,0:T(8,128)S(1)}, f32[34,8,128]{2,1,0:T(8,128)S(1)}, u32[]{:S(2)}, u32[]{:S(2)}) collective-permute-start(f32[34,8,128]{2,1,0:T(8,128)S(1)} %get-tuple-element.24), channel_id=1, source_target_pairs={{1,2},{2,1},{3,4},{4,3},{5,6},{6,5},{9,10},{10,9},{11,12},{12,11},... | collective-permute-start | bytes 417800 | tf_op jit(solution)/shard_map/ppermute | solution.py:443
  5.4 4.0 %gram_first.1 = (f32[60,24,8,128]{3,2,1,0:T(8,128)S(1)}, f32[64,128]{1,0:T(8,128)S(1)}) custom-call(f32[60,24,8,128]{3,2,1,0:T(8,128)} %bitcast.3), custom_call_target="tpu_custom_call" | custom-call | tf_op jit(solution)/shard_map/gram_first/pallas_call | solution.py:491
  9.4 0.0 collective-permute-done.1.recv_b
  9.5 0.1 pack_x.1
  9.6 0.1 collective-permute-start.2
  9.6 0.7 %collective-permute-start.3 = (f32[45,8,128]{2,1,0:T(8,128)S(1)}, f32[45,8,128]{2,1,0:T(8,128)S(1)}, u32[]{:S(2)}, u32[]{:S(2)}) collective-permute-start(f32[45,8,128]{2,1,0:T(8,128)S(1)} %get-tuple-element.30), channel_id=1, source_target_pairs={{8,16},{16,8},{9,17},{17,9},{10,18},{18,10},{11,19},{19,11},{12,20... | collective-permute-start | bytes 552968 | tf_op jit(solution)/shard_map/ppermute | solution.py:443
  10.3 1.1 %gram_rest.1.square_b = f32[64,128]{1,0:T(8,128)S(1)} custom-call(f32[60,24,8,128]{3,2,1,0:T(8,128)S(1)} %get-tuple-element.31.kept), custom_call_target="tpu_custom_call" | custom-call | tf_op jit(solution)/shard_map/gram_rest/pallas_call | solution.py:517
  11.4 0.0 collective-permute-done.2.recv_a
  11.4 3.1 %steps.1 = (f32[4,24,8,128]{3,2,1,0:T(8,128)S(1)}, f32[24,8,128]{2,1,0:T(8,128)}, f32[64,64]{1,0:T(8,128)S(1)}) custom-call(f32[3,8,8,128]{3,2,1,0:T(8,128)S(1)} %get-tuple-element.20.v, f32[8,8,128]{2,1,0:T(8,128)S(1)} %get-tuple-element.21.nu, f32[4,3,8,8,128]{4,3,2,1,0:T(8,128)S(1)} %get-tuple-element.22.f, f32[3,8,8,128]{3,2,1,0:T(8,128)S(1)} %get-tuple-element.26.rv, ...), custom_call_target="tpu_custom_call" | custom-call | tf_op jit(solution)/shard_map/steps/pallas_call | solution.py:525
  14.5 9.5 %collective-permute-start.6 = (f32[64,64]{1,0:T(8,128)S(1)}, f32[64,64]{1,0:T(8,128)S(1)}, u32[]{:S(2)}, u32[]{:S(2)}) collective-permute-start(f32[64,64]{1,0:T(8,128)S(1)} %get-tuple-element.33), channel_id=1, source_target_pairs={{0,9},{1,8},{2,11},{3,10},{4,13},{5,12},{6,15},{7,14},{8,1},{9,0},... | collective-permute-start | bytes 49160 | tf_op jit(solution)/shard_map/ppermute | solution.py:461
  24.0 0.2 collective-permute-start.4
  24.2 1.4 %collective-permute-done.6 = f32[64,64]{1,0:T(8,128)S(1)} collective-permute-done((f32[64,64]{1,0:T(8,128)S(1)}, f32[64,64]{1,0:T(8,128)S(1)}, u32[]{:S(2)}, u32[]{:S(2)}) %collective-permute-start.6) | collective-permute-done | bytes 16416 | tf_op jit(solution)/shard_map/ppermute | solution.py:461
  25.6 2.3 %collective-permute-done.5 = f32[64,64]{1,0:T(8,128)S(1)} collective-permute-done((f32[64,64]{1,0:T(8,128)S(1)}, f32[64,64]{1,0:T(8,128)S(1)}, u32[]{:S(2)}, u32[]{:S(2)}) %collective-permute-start.5) | collective-permute-done | bytes 16416 | tf_op jit(solution)/shard_map/ppermute | solution.py:461
  28.0 1.7 %collective-permute-start.9 = (f32[64,64]{1,0:T(8,128)S(1)}, f32[64,64]{1,0:T(8,128)S(1)}, u32[]{:S(2)}, u32[]{:S(2)}) collective-permute-start(f32[64,64]{1,0:T(8,128)S(1)} %add_add_fusion.1), channel_id=1, source_target_pairs={{0,18},{1,19},{2,16},{3,17},{4,22},{5,23},{6,20},{7,21},{8,26},{9,... | collective-permute-start | bytes 49160 | tf_op jit(solution)/shard_map/ppermute | solution.py:461
  29.6 0.0 collective-permute-start.8
  29.7 1.8 %collective-permute-start.7 = (f32[64,64]{1,0:T(8,128)S(1)}, f32[64,64]{1,0:T(8,128)S(1)}, u32[]{:S(2)}, u32[]{:S(2)}) collective-permute-start(f32[64,64]{1,0:T(8,128)S(1)} %add_add_fusion.1), channel_id=1, source_target_pairs={{0,16},{1,17},{2,18},{3,19},{4,20},{5,21},{6,22},{7,23},{8,24},{9,... | collective-permute-start | bytes 49160 | tf_op jit(solution)/shard_map/ppermute | solution.py:461
  31.5 1.3 %collective-permute-done.9 = f32[64,64]{1,0:T(8,128)S(1)} collective-permute-done((f32[64,64]{1,0:T(8,128)S(1)}, f32[64,64]{1,0:T(8,128)S(1)}, u32[]{:S(2)}, u32[]{:S(2)}) %collective-permute-start.9) | collective-permute-done | bytes 16416 | tf_op jit(solution)/shard_map/ppermute | solution.py:461
  32.9 0.7 %collective-permute-done.8 = f32[64,64]{1,0:T(8,128)S(1)} collective-permute-done((f32[64,64]{1,0:T(8,128)S(1)}, f32[64,64]{1,0:T(8,128)S(1)}, u32[]{:S(2)}, u32[]{:S(2)}) %collective-permute-start.8) | collective-permute-done | bytes 16416 | tf_op jit(solution)/shard_map/ppermute | solution.py:461
  33.6 0.0 collective-permute-done.7
  33.6 3.1 %collective-permute-start.10 = (f32[64,64]{1,0:T(8,128)S(1)}, f32[64,64]{1,0:T(8,128)S(1)}, u32[]{:S(2)}, u32[]{:S(2)}) collective-permute-start(f32[64,64]{1,0:T(8,128)S(1)} %add_add_fusion), channel_id=1, source_target_pairs={{0,4},{1,5},{2,6},{3,7},{4,0},{5,1},{6,2},{7,3},{8,12},{9,13},{10,... | collective-permute-start | bytes 49160 | tf_op jit(solution)/shard_map/ppermute | solution.py:461
  36.7 2.0 %halves.1.panel = bf16[96,128,256]{2,1,0:T(8,128)(2,1)S(1)} custom-call(f32[60,24,8,128]{3,2,1,0:T(8,128)S(1)} %get-tuple-element.31.kept, f32[4,24,8,128]{3,2,1,0:T(8,128)S(1)} %get-tuple-element.34.snaps), custom_call_target="tpu_custom_call" | custom-call | tf_op jit(solution)/shard_map/halves/pallas_call | solution.py:540
  38.8 4.6 %factor_basis.1 = (f32[64,24,8,128]{3,2,1,0:T(8,128)}, f32[64,64]{1,0:T(8,128)}) custom-call(f32[64,64]{1,0:T(8,128)S(1)} %add.27.part, bf16[96,128,256]{2,1,0:T(8,128)(2,1)S(1)} %halves.1.panel), custom_call_target="tpu_custom_call" | custom-call | tf_op jit(solution)/shard_map/factor_basis/pallas_call | solution.py:549
  (8 shorter events, 0.0 us)
Async XLA Ops:
  1.7 7.7 %collective-permute-start = (f32[34,8,128]{2,1,0:T(8,128)S(1)}, f32[34,8,128]{2,1,0:T(8,128)S(1)}, u32[]{:S(2)}, u32[]{:S(2)}) collective-permute-start(f32[34,8,128]{2,1,0:T(8,128)S(1)} %get-tuple-element.23), channel_id=1, source_target_pairs={{0,1},{1,0},{2,3},{3,2},{4,5},{5,4},{6,7},{7,6},{8,9},{9,8},{10,11... | collective-permute-start | bytes 417800 | tf_op jit(solution)/shard_map/ppermute | solution.py:444
  4.7 4.7 %collective-permute-start.1 = (f32[34,8,128]{2,1,0:T(8,128)S(1)}, f32[34,8,128]{2,1,0:T(8,128)S(1)}, u32[]{:S(2)}, u32[]{:S(2)}) collective-permute-start(f32[34,8,128]{2,1,0:T(8,128)S(1)} %get-tuple-element.24), channel_id=1, source_target_pairs={{1,2},{2,1},{3,4},{4,3},{5,6},{6,5},{9,10},{10,9},{11,12},{12,11},... | collective-permute-start | bytes 417800 | tf_op jit(solution)/shard_map/ppermute | solution.py:443
  9.6 1.9 %collective-permute-start.2 = (f32[45,8,128]{2,1,0:T(8,128)S(1)}, f32[45,8,128]{2,1,0:T(8,128)S(1)}, u32[]{:S(2)}, u32[]{:S(2)}) collective-permute-start(f32[45,8,128]{2,1,0:T(8,128)S(1)} %get-tuple-element.29), channel_id=1, source_target_pairs={{0,8},{8,0},{16,24},{24,16},{1,9},{9,1},{17,25},{25,17},{2,10},{10... | collective-permute-start | bytes 552968 | tf_op jit(solution)/shard_map/ppermute | solution.py:444
  9.6 1.8 %collective-permute-start.3 = (f32[45,8,128]{2,1,0:T(8,128)S(1)}, f32[45,8,128]{2,1,0:T(8,128)S(1)}, u32[]{:S(2)}, u32[]{:S(2)}) collective-permute-start(f32[45,8,128]{2,1,0:T(8,128)S(1)} %get-tuple-element.30), channel_id=1, source_target_pairs={{8,16},{16,8},{9,17},{17,9},{10,18},{18,10},{11,19},{19,11},{12,20... | collective-permute-start | bytes 552968 | tf_op jit(solution)/shard_map/ppermute | solution.py:443
  14.5 11.1 %collective-permute-start.6 = (f32[64,64]{1,0:T(8,128)S(1)}, f32[64,64]{1,0:T(8,128)S(1)}, u32[]{:S(2)}, u32[]{:S(2)}) collective-permute-start(f32[64,64]{1,0:T(8,128)S(1)} %get-tuple-element.33), channel_id=1, source_target_pairs={{0,9},{1,8},{2,11},{3,10},{4,13},{5,12},{6,15},{7,14},{8,1},{9,0},... | collective-permute-start | bytes 49160 | tf_op jit(solution)/shard_map/ppermute | solution.py:461
  24.0 3.9 %collective-permute-start.5 = (f32[64,64]{1,0:T(8,128)S(1)}, f32[64,64]{1,0:T(8,128)S(1)}, u32[]{:S(2)}, u32[]{:S(2)}) collective-permute-start(f32[64,64]{1,0:T(8,128)S(1)} %get-tuple-element.33), channel_id=1, source_target_pairs={{0,1},{1,0},{2,3},{3,2},{4,5},{5,4},{6,7},{7,6},{8,9},{9,8},{10,11... | collective-permute-start | bytes 49160 | tf_op jit(solution)/shard_map/ppermute | solution.py:461
  24.0 3.9 %collective-permute-start.4 = (f32[64,64]{1,0:T(8,128)S(1)}, f32[64,64]{1,0:T(8,128)S(1)}, u32[]{:S(2)}, u32[]{:S(2)}) collective-permute-start(f32[64,64]{1,0:T(8,128)S(1)} %get-tuple-element.33), channel_id=1, source_target_pairs={{0,8},{1,9},{2,10},{3,11},{4,12},{5,13},{6,14},{7,15},{8,0},{9,1},... | collective-permute-start | bytes 49160 | tf_op jit(solution)/shard_map/ppermute | solution.py:461
  28.0 4.9 %collective-permute-start.9 = (f32[64,64]{1,0:T(8,128)S(1)}, f32[64,64]{1,0:T(8,128)S(1)}, u32[]{:S(2)}, u32[]{:S(2)}) collective-permute-start(f32[64,64]{1,0:T(8,128)S(1)} %add_add_fusion.1), channel_id=1, source_target_pairs={{0,18},{1,19},{2,16},{3,17},{4,22},{5,23},{6,20},{7,21},{8,26},{9,... | collective-permute-start | bytes 49160 | tf_op jit(solution)/shard_map/ppermute | solution.py:461
  29.6 3.9 %collective-permute-start.8 = (f32[64,64]{1,0:T(8,128)S(1)}, f32[64,64]{1,0:T(8,128)S(1)}, u32[]{:S(2)}, u32[]{:S(2)}) collective-permute-start(f32[64,64]{1,0:T(8,128)S(1)} %add_add_fusion.1), channel_id=1, source_target_pairs={{0,2},{1,3},{2,0},{3,1},{4,6},{5,7},{6,4},{7,5},{8,10},{9,11},{10,... | collective-permute-start | bytes 49160 | tf_op jit(solution)/shard_map/ppermute | solution.py:461
  29.7 3.9 %collective-permute-start.7 = (f32[64,64]{1,0:T(8,128)S(1)}, f32[64,64]{1,0:T(8,128)S(1)}, u32[]{:S(2)}, u32[]{:S(2)}) collective-permute-start(f32[64,64]{1,0:T(8,128)S(1)} %add_add_fusion.1), channel_id=1, source_target_pairs={{0,16},{1,17},{2,18},{3,19},{4,20},{5,21},{6,22},{7,23},{8,24},{9,... | collective-permute-start | bytes 49160 | tf_op jit(solution)/shard_map/ppermute | solution.py:461
  33.6 5.1 %collective-permute-start.10 = (f32[64,64]{1,0:T(8,128)S(1)}, f32[64,64]{1,0:T(8,128)S(1)}, u32[]{:S(2)}, u32[]{:S(2)}) collective-permute-start(f32[64,64]{1,0:T(8,128)S(1)} %add_add_fusion), channel_id=1, source_target_pairs={{0,4},{1,5},{2,6},{3,7},{4,0},{5,1},{6,2},{7,3},{8,12},{9,13},{10,... | collective-permute-start | bytes 49160 | tf_op jit(solution)/shard_map/ppermute | solution.py:461

commit v6 on v5

--- a/solution.py
+++ b/solution.py
@@ -444,25 +444,27 @@
     return lax.ppermute(first, axis, near), distant
 
 
-def sum_over(value, minor, major):
+def sum_over(value, minor, major, beside):
     inner, outer = lax.axis_size(minor), lax.axis_size(major)
     count = inner * outer
     if count & (count - 1):
-        return lax.psum(value, (major, minor))
+        return lax.psum(value, (major, minor)), beside
     low = [1 << i for i in range(inner.bit_length() - 1)]
     high = [inner << i for i in range(outer.bit_length() - 1)]
     both = min(len(low), len(high))
     groups = [[high[i], low[i]] for i in range(both)]
     rest = low[both:] + high[both:]
     groups += [rest[i : i + 2] for i in range(0, len(rest), 2)]
-    for group in groups:
+    for at, group in enumerate(groups):
+        if at == len(groups) - 1:
+            value, beside = lax.optimization_barrier((value, beside))
         masks = group + ([group[0] ^ group[1]] if len(group) == 2 else [])
         others = [
             lax.ppermute(value, (major, minor), [(i, i ^ m) for i in range(count)]) for m in masks
         ]
         for other in others:
             value = value + other
-    return value
+    return value, beside
 
 
 def local(velocity, viscosity, forcing, earlier):
@@ -545,7 +547,7 @@
         compiler_params=limit(8),
         name="halves",
     )(kept, snaps)
-    part = sum_over(part, "gy", "gx")
+    part, panel = sum_over(part, "gy", "gx", panel)
     basis, factor = call(
         basis_kernel,
         out_shape=(struct(n, slabs, 8, 128), struct(n, n)),

time: 43.5 us -> 43.4 us (level)
  transfers between devices with their start and end apart: 11 -> 11, of which waited for: 4 -> 3; matrix products, arithmetic and copies ran while one was open for 0% -> 0% of each run, Pallas kernels for 16% -> 17%
where the time goes in v6:
time: 43.4 us; the launch traced here: 43.2 us
  starting transfers between devices  20.7 us (48%)
  Pallas kernels  16 us (37%)
  waiting for transfers between devices  5.64 us (13%)
  between operations  0.77 us (2%)
    ppermute x7, starting transfers between devices, sum_over(): lax.ppermute(value, (major, minor), [(i, i ^ m) for i in range(count)])  16.3 us
    ppermute x7, waiting for transfers between devices, sum_over(): lax.ppermute(value, (major, minor), [(i, i ^ m) for i in range(count)])  5.63 us
    pallas_call x1, Pallas kernels, local(): call(basis_kernel, out_shape=(struct(n, slabs, 8, 128), struct(n, n)), in...  4.59 us
    pallas_call x1, Pallas kernels, local(): call(functools.partial(square_first_kernel, n=n, count=first), out_shape=...  4.03 us
    pallas_call x1, Pallas kernels, local(): call(steps_kernel, out_shape=(struct(steps, slabs, 8, 128), struct(slabs,...  3.11 us
    ppermute x2, starting transfers between devices, pair_exchange(): return (lax.ppermute(first, axis, near), distant)  3.07 us
    pallas_call x1, Pallas kernels, local(): call(halves_kernel, out_shape=jax.ShapeDtypeStruct((4 * slabs, 2 * n, 256...  2.05 us
    ppermute x2, starting transfers between devices, pair_exchange(): distant = lax.ppermute(second, axis, far)  1.33 us
  transfers between devices with their start and end apart: 11, of which 3 were waited for; matrix products, arithmetic and copies ran while one was open for 0% of the time, Pallas kernels for 17%

profile of v6, /device:TPU:0, one launch (start us, length us, event | category | flops | bytes accessed | tf_op | source)
XLA Modules:
  0.0 43.2 jit_solution(12801769160389477463)
XLA Ops:
  0.6 1.1 %pack_y.1 = (f32[3,8,8,128]{3,2,1,0:T(8,128)S(1)}, f32[8,8,128]{2,1,0:T(8,128)S(1)}, f32[4,3,8,8,128]{4,3,2,1,0:T(8,128)S(1)}, f32[34,8,128]{2,1,0:T(8,128)S(1)}, f32[34,8,128]{2,1,0:T(8,128)S(1)}) custom-call(f32[3,8,8,128]{3,2,1,0:T(8,128)} %v_in.1, f32[8,8,128]{2,1,0:T(8,128)} %nu_in.1, f32[4,3,8,8,128]{4,3,2,1,0:T(8,128)} %f_in.1), custom_call_target="tpu_custom_call" | custom-call | tf_op jit(solution)/shard_map/pack_y/pallas_call | solution.py:476
  1.7 3.0 %collective-permute-start = (f32[34,8,128]{2,1,0:T(8,128)S(1)}, f32[34,8,128]{2,1,0:T(8,128)S(1)}, u32[]{:S(2)}, u32[]{:S(2)}) collective-permute-start(f32[34,8,128]{2,1,0:T(8,128)S(1)} %get-tuple-element.25), channel_id=1, source_target_pairs={{0,1},{1,0},{2,3},{3,2},{4,5},{5,4},{6,7},{7,6},{8,9},{9,8},{10,11... | collective-permute-start | bytes 417800 | tf_op jit(solution)/shard_map/ppermute | solution.py:444
  4.7 0.7 %collective-permute-start.1 = (f32[34,8,128]{2,1,0:T(8,128)S(1)}, f32[34,8,128]{2,1,0:T(8,128)S(1)}, u32[]{:S(2)}, u32[]{:S(2)}) collective-permute-start(f32[34,8,128]{2,1,0:T(8,128)S(1)} %get-tuple-element.26), channel_id=1, source_target_pairs={{1,2},{2,1},{3,4},{4,3},{5,6},{6,5},{9,10},{10,9},{11,12},{12,11},... | collective-permute-start | bytes 417800 | tf_op jit(solution)/shard_map/ppermute | solution.py:443
  5.4 4.0 %gram_first.1 = (f32[60,24,8,128]{3,2,1,0:T(8,128)S(1)}, f32[64,128]{1,0:T(8,128)S(1)}) custom-call(f32[60,24,8,128]{3,2,1,0:T(8,128)} %bitcast.3), custom_call_target="tpu_custom_call" | custom-call | tf_op jit(solution)/shard_map/gram_first/pallas_call | solution.py:493
  9.4 0.0 collective-permute-done.1.recv_b
  9.5 0.1 pack_x.1
  9.6 0.1 collective-permute-start.2
  9.6 0.7 %collective-permute-start.3 = (f32[45,8,128]{2,1,0:T(8,128)S(1)}, f32[45,8,128]{2,1,0:T(8,128)S(1)}, u32[]{:S(2)}, u32[]{:S(2)}) collective-permute-start(f32[45,8,128]{2,1,0:T(8,128)S(1)} %get-tuple-element.32), channel_id=1, source_target_pairs={{8,16},{16,8},{9,17},{17,9},{10,18},{18,10},{11,19},{19,11},{12,20... | collective-permute-start | bytes 552968 | tf_op jit(solution)/shard_map/ppermute | solution.py:443
  10.3 1.1 %gram_rest.1.square_b = f32[64,128]{1,0:T(8,128)S(1)} custom-call(f32[60,24,8,128]{3,2,1,0:T(8,128)S(1)} %get-tuple-element.33.kept), custom_call_target="tpu_custom_call" | custom-call | tf_op jit(solution)/shard_map/gram_rest/pallas_call | solution.py:519
  11.4 0.0 collective-permute-done.2.recv_a
  11.4 0.0 collective-permute-done.3.recv_b
  11.4 3.1 %steps.1 = (f32[4,24,8,128]{3,2,1,0:T(8,128)S(1)}, f32[24,8,128]{2,1,0:T(8,128)}, f32[64,64]{1,0:T(8,128)S(1)}) custom-call(f32[3,8,8,128]{3,2,1,0:T(8,128)S(1)} %get-tuple-element.22.v, f32[8,8,128]{2,1,0:T(8,128)S(1)} %get-tuple-element.23.nu, f32[4,3,8,8,128]{4,3,2,1,0:T(8,128)S(1)} %get-tuple-element.24.f, f32[3,8,8,128]{3,2,1,0:T(8,128)S(1)} %get-tuple-element.28.rv, ...), custom_call_target="tpu_custom_call" | custom-call | tf_op jit(solution)/shard_map/steps/pallas_call | solution.py:527
  14.5 9.5 %collective-permute-start.6 = (f32[64,64]{1,0:T(8,128)S(1)}, f32[64,64]{1,0:T(8,128)S(1)}, u32[]{:S(2)}, u32[]{:S(2)}) collective-permute-start(f32[64,64]{1,0:T(8,128)S(1)} %get-tuple-element.35), channel_id=1, source_target_pairs={{0,9},{1,8},{2,11},{3,10},{4,13},{5,12},{6,15},{7,14},{8,1},{9,0},... | collective-permute-start | bytes 49160 | tf_op jit(solution)/shard_map/ppermute | solution.py:463
  24.0 0.2 collective-permute-start.4
  24.2 1.4 %collective-permute-done.6 = f32[64,64]{1,0:T(8,128)S(1)} collective-permute-done((f32[64,64]{1,0:T(8,128)S(1)}, f32[64,64]{1,0:T(8,128)S(1)}, u32[]{:S(2)}, u32[]{:S(2)}) %collective-permute-start.6) | collective-permute-done | bytes 16416 | tf_op jit(solution)/shard_map/ppermute | solution.py:463
  25.6 2.3 %collective-permute-done.5 = f32[64,64]{1,0:T(8,128)S(1)} collective-permute-done((f32[64,64]{1,0:T(8,128)S(1)}, f32[64,64]{1,0:T(8,128)S(1)}, u32[]{:S(2)}, u32[]{:S(2)}) %collective-permute-start.5) | collective-permute-done | bytes 16416 | tf_op jit(solution)/shard_map/ppermute | solution.py:463
  28.0 1.7 %collective-permute-start.9 = (f32[64,64]{1,0:T(8,128)S(1)}, f32[64,64]{1,0:T(8,128)S(1)}, u32[]{:S(2)}, u32[]{:S(2)}) collective-permute-start(f32[64,64]{1,0:T(8,128)S(1)} %add_add_fusion.1), channel_id=1, source_target_pairs={{0,18},{1,19},{2,16},{3,17},{4,22},{5,23},{6,20},{7,21},{8,26},{9,... | collective-permute-start | bytes 49160 | tf_op jit(solution)/shard_map/ppermute | solution.py:463
  29.6 0.0 collective-permute-start.8
  29.7 1.8 %collective-permute-start.7 = (f32[64,64]{1,0:T(8,128)S(1)}, f32[64,64]{1,0:T(8,128)S(1)}, u32[]{:S(2)}, u32[]{:S(2)}) collective-permute-start(f32[64,64]{1,0:T(8,128)S(1)} %add_add_fusion.1), channel_id=1, source_target_pairs={{0,16},{1,17},{2,18},{3,19},{4,20},{5,21},{6,22},{7,23},{8,24},{9,... | collective-permute-start | bytes 49160 | tf_op jit(solution)/shard_map/ppermute | solution.py:463
  31.5 2.0 %halves.1.panel = bf16[96,128,256]{2,1,0:T(8,128)(2,1)S(1)} custom-call(f32[60,24,8,128]{3,2,1,0:T(8,128)S(1)} %get-tuple-element.33.kept, f32[4,24,8,128]{3,2,1,0:T(8,128)S(1)} %get-tuple-element.36.snaps), custom_call_target="tpu_custom_call" | custom-call | tf_op jit(solution)/shard_map/halves/pallas_call | solution.py:542
  33.6 0.0 collective-permute-done.7
  33.6 3.0 %collective-permute-start.10 = (f32[64,64]{1,0:T(8,128)S(1)}, f32[64,64]{1,0:T(8,128)S(1)}, u32[]{:S(2)}, u32[]{:S(2)}) collective-permute-start(f32[64,64]{1,0:T(8,128)S(1)} %add_add_fusion), channel_id=1, source_target_pairs={{0,4},{1,5},{2,6},{3,7},{4,0},{5,1},{6,2},{7,3},{8,12},{9,13},{10,... | collective-permute-start | bytes 49160 | tf_op jit(solution)/shard_map/ppermute | solution.py:463
  36.7 1.9 %collective-permute-done.10 = f32[64,64]{1,0:T(8,128)S(1)} collective-permute-done((f32[64,64]{1,0:T(8,128)S(1)}, f32[64,64]{1,0:T(8,128)S(1)}, u32[]{:S(2)}, u32[]{:S(2)}) %collective-permute-start.10) | collective-permute-done | bytes 16416 | tf_op jit(solution)/shard_map/ppermute | solution.py:463
  38.6 4.6 %factor_basis.1 = (f32[64,24,8,128]{3,2,1,0:T(8,128)}, f32[64,64]{1,0:T(8,128)}) custom-call(f32[64,64]{1,0:T(8,128)S(1)} %add.27.part, bf16[96,128,256]{2,1,0:T(8,128)(2,1)S(1)} %halves.1.panel), custom_call_target="tpu_custom_call" | custom-call | tf_op jit(solution)/shard_map/factor_basis/pallas_call | solution.py:551
  (8 shorter events, 0.0 us)
Async XLA Ops:
  1.7 7.7 %collective-permute-start = (f32[34,8,128]{2,1,0:T(8,128)S(1)}, f32[34,8,128]{2,1,0:T(8,128)S(1)}, u32[]{:S(2)}, u32[]{:S(2)}) collective-permute-start(f32[34,8,128]{2,1,0:T(8,128)S(1)} %get-tuple-element.25), channel_id=1, source_target_pairs={{0,1},{1,0},{2,3},{3,2},{4,5},{5,4},{6,7},{7,6},{8,9},{9,8},{10,11... | collective-permute-start | bytes 417800 | tf_op jit(solution)/shard_map/ppermute | solution.py:444
  4.7 4.7 %collective-permute-start.1 = (f32[34,8,128]{2,1,0:T(8,128)S(1)}, f32[34,8,128]{2,1,0:T(8,128)S(1)}, u32[]{:S(2)}, u32[]{:S(2)}) collective-permute-start(f32[34,8,128]{2,1,0:T(8,128)S(1)} %get-tuple-element.26), channel_id=1, source_target_pairs={{1,2},{2,1},{3,4},{4,3},{5,6},{6,5},{9,10},{10,9},{11,12},{12,11},... | collective-permute-start | bytes 417800 | tf_op jit(solution)/shard_map/ppermute | solution.py:443
  9.6 1.9 %collective-permute-start.2 = (f32[45,8,128]{2,1,0:T(8,128)S(1)}, f32[45,8,128]{2,1,0:T(8,128)S(1)}, u32[]{:S(2)}, u32[]{:S(2)}) collective-permute-start(f32[45,8,128]{2,1,0:T(8,128)S(1)} %get-tuple-element.31), channel_id=1, source_target_pairs={{0,8},{8,0},{16,24},{24,16},{1,9},{9,1},{17,25},{25,17},{2,10},{10... | collective-permute-start | bytes 552968 | tf_op jit(solution)/shard_map/ppermute | solution.py:444
  9.6 1.8 %collective-permute-start.3 = (f32[45,8,128]{2,1,0:T(8,128)S(1)}, f32[45,8,128]{2,1,0:T(8,128)S(1)}, u32[]{:S(2)}, u32[]{:S(2)}) collective-permute-start(f32[45,8,128]{2,1,0:T(8,128)S(1)} %get-tuple-element.32), channel_id=1, source_target_pairs={{8,16},{16,8},{9,17},{17,9},{10,18},{18,10},{11,19},{19,11},{12,20... | collective-permute-start | bytes 552968 | tf_op jit(solution)/shard_map/ppermute | solution.py:443
  14.5 11.1 %collective-permute-start.6 = (f32[64,64]{1,0:T(8,128)S(1)}, f32[64,64]{1,0:T(8,128)S(1)}, u32[]{:S(2)}, u32[]{:S(2)}) collective-permute-start(f32[64,64]{1,0:T(8,128)S(1)} %get-tuple-element.35), channel_id=1, source_target_pairs={{0,9},{1,8},{2,11},{3,10},{4,13},{5,12},{6,15},{7,14},{8,1},{9,0},... | collective-permute-start | bytes 49160 | tf_op jit(solution)/shard_map/ppermute | solution.py:463
  24.0 3.9 %collective-permute-start.5 = (f32[64,64]{1,0:T(8,128)S(1)}, f32[64,64]{1,0:T(8,128)S(1)}, u32[]{:S(2)}, u32[]{:S(2)}) collective-permute-start(f32[64,64]{1,0:T(8,128)S(1)} %get-tuple-element.35), channel_id=1, source_target_pairs={{0,1},{1,0},{2,3},{3,2},{4,5},{5,4},{6,7},{7,6},{8,9},{9,8},{10,11... | collective-permute-start | bytes 49160 | tf_op jit(solution)/shard_map/ppermute | solution.py:463
  24.0 3.9 %collective-permute-start.4 = (f32[64,64]{1,0:T(8,128)S(1)}, f32[64,64]{1,0:T(8,128)S(1)}, u32[]{:S(2)}, u32[]{:S(2)}) collective-permute-start(f32[64,64]{1,0:T(8,128)S(1)} %get-tuple-element.35), channel_id=1, source_target_pairs={{0,8},{1,9},{2,10},{3,11},{4,12},{5,13},{6,14},{7,15},{8,0},{9,1},... | collective-permute-start | bytes 49160 | tf_op jit(solution)/shard_map/ppermute | solution.py:463
  28.0 5.6 %collective-permute-start.9 = (f32[64,64]{1,0:T(8,128)S(1)}, f32[64,64]{1,0:T(8,128)S(1)}, u32[]{:S(2)}, u32[]{:S(2)}) collective-permute-start(f32[64,64]{1,0:T(8,128)S(1)} %add_add_fusion.1), channel_id=1, source_target_pairs={{0,18},{1,19},{2,16},{3,17},{4,22},{5,23},{6,20},{7,21},{8,26},{9,... | collective-permute-start | bytes 49160 | tf_op jit(solution)/shard_map/ppermute | solution.py:463
  29.6 3.9 %collective-permute-start.8 = (f32[64,64]{1,0:T(8,128)S(1)}, f32[64,64]{1,0:T(8,128)S(1)}, u32[]{:S(2)}, u32[]{:S(2)}) collective-permute-start(f32[64,64]{1,0:T(8,128)S(1)} %add_add_fusion.1), channel_id=1, source_target_pairs={{0,2},{1,3},{2,0},{3,1},{4,6},{5,7},{6,4},{7,5},{8,10},{9,11},{10,... | collective-permute-start | bytes 49160 | tf_op jit(solution)/shard_map/ppermute | solution.py:463
  29.7 3.9 %collective-permute-start.7 = (f32[64,64]{1,0:T(8,128)S(1)}, f32[64,64]{1,0:T(8,128)S(1)}, u32[]{:S(2)}, u32[]{:S(2)}) collective-permute-start(f32[64,64]{1,0:T(8,128)S(1)} %add_add_fusion.1), channel_id=1, source_target_pairs={{0,16},{1,17},{2,18},{3,19},{4,20},{5,21},{6,22},{7,23},{8,24},{9,... | collective-permute-start | bytes 49160 | tf_op jit(solution)/shard_map/ppermute | solution.py:463
  33.6 4.9 %collective-permute-start.10 = (f32[64,64]{1,0:T(8,128)S(1)}, f32[64,64]{1,0:T(8,128)S(1)}, u32[]{:S(2)}, u32[]{:S(2)}) collective-permute-start(f32[64,64]{1,0:T(8,128)S(1)} %add_add_fusion), channel_id=1, source_target_pairs={{0,4},{1,5},{2,6},{3,7},{4,0},{5,1},{6,2},{7,3},{8,12},{9,13},{10,... | collective-permute-start | bytes 49160 | tf_op jit(solution)/shard_map/ppermute | solution.py:463
